TPU v7x, 32 devices: a whole 2x2x4 slice. The times are simulated.
32 devices in a mesh: dp: 2 (over y), hid: 4 (over x, core), wid: 4 (over z).
Axes of the slice: x: 2, y: 2, z: 4, core: 2. Of those that a mesh axis runs over, the one named last changes fastest.
Arguments:
- tokens: bfloat16 [2, 3072, 1536], P(None, ('dp', 'wid'), 'hid'), may hold values from -6 to 6
- cotangent: bfloat16 [2, 3072, 1536], P(None, ('dp', 'wid'), 'hid'), may hold values from -6 to 6
- lengths: int32 [2, 8, 3], P(None, ('dp', 'wid')), may hold values from 1 to 256, 384 in all within a row
- keep: int32 [2, 3072], P(None, ('dp', 'wid')), may hold values 0 or 1
- norm_one: bfloat16 [1, 1536], P(None, 'hid'), may hold values from 0.5 to 1.5
- w_query: bfloat16 [1536, 1536], P(('dp', 'wid'), 'hid'), may hold values from -0.15625 to 0.15625
- w_key: bfloat16 [1536, 1536], P(('dp', 'wid'), 'hid'), may hold values from -0.15625 to 0.15625
- w_value: bfloat16 [1536, 1536], P(('dp', 'wid'), 'hid'), may hold values from -0.15625 to 0.15625
- w_house: bfloat16 [1536, 1536], P(('dp', 'wid'), 'hid'), may hold values from -0.15625 to 0.15625
- w_beta: bfloat16 [1536, 12], P(('dp', 'wid'), 'hid'), may hold values from -0.15625 to 0.15625
- w_out: bfloat16 [1536, 1536], P('hid', ('dp', 'wid')), may hold values from -0.75 to 0.75
- norm_two: bfloat16 [1, 1536], P(None, 'hid'), may hold values from 0.5 to 1.5
- w_gate: bfloat16 [1536, 4096], P(('dp', 'wid'), 'hid'), may hold values from -0.15625 to 0.15625
- w_up: bfloat16 [1536, 4096], P(('dp', 'wid'), 'hid'), may hold values from -0.15625 to 0.15625
- w_down: bfloat16 [4096, 1536], P('hid', ('dp', 'wid')), may hold values from -0.09375 to 0.09375
Outputs:
- layer_out: bfloat16 [2, 3072, 1536], P(None, ('dp', 'wid'), 'hid')
- tokens_grad: bfloat16 [2, 3072, 1536], P(None, ('dp', 'wid'), 'hid')
- norm_one_grad: float32 [1, 1536], P(None, 'hid')
- w_query_grad: float32 [1536, 1536], P(('dp', 'wid'), 'hid')
- w_key_grad: float32 [1536, 1536], P(('dp', 'wid'), 'hid')
- w_value_grad: float32 [1536, 1536], P(('dp', 'wid'), 'hid')
- w_house_grad: float32 [1536, 1536], P(('dp', 'wid'), 'hid')
- w_beta_grad: float32 [1536, 12], P(('dp', 'wid'), 'hid')
- w_out_grad: float32 [1536, 1536], P('hid', ('dp', 'wid'))
- norm_two_grad: float32 [1, 1536], P(None, 'hid')
- w_gate_grad: float32 [1536, 4096], P(('dp', 'wid'), 'hid')
- w_up_grad: float32 [1536, 4096], P(('dp', 'wid'), 'hid')
- w_down_grad: float32 [4096, 1536], P('hid', ('dp', 'wid'))
Inputs may be any that keep to these rules, and one draw needn't show every extreme that they name: Each buffer holds 3 sequences packed in order, their lengths summing to 384, the longest exactly 256 tokens.
All inputs are finite; a program needn't handle non-finite values. No bound on the sum of `keep` on one device may be relied on, other than what follows from the above.
Results may differ from a plain program's by a relative error of at most 0.025.
Values may be sent and summed in bfloat16 or wider, within the bound.
A program may use at most 128 MiB of HBM per device.

v0:
```python
import math

import jax
import jax.numpy as jnp
from jax import lax
from jax.sharding import PartitionSpec as P

HEAD = 128
BLK = 128


PRECISE = lax.Precision.HIGHEST
EPSILON = 1e-06


def segment_ids(length_row, length):
    ends = jnp.cumsum(length_row)
    places = jnp.arange(length, dtype=jnp.int32)
    return jnp.sum((places[:, None] >= ends[None, :]).astype(jnp.int32), axis=1)


def split_heads(matrix):
    return matrix.reshape(matrix.shape[0], matrix.shape[1] // HEAD, HEAD).transpose(1, 0, 2)


def merge_heads(stacked):
    return stacked.transpose(1, 0, 2).reshape(stacked.shape[1], stacked.shape[0] * stacked.shape[2])


def normalize_heads(stacked):
    return stacked * lax.rsqrt(jnp.sum(stacked * stacked, axis=2, keepdims=True) + EPSILON)


def path_head(queries, key_rows, value_rows, house_rows, beta_row, segment, keep_key, block_size):
    length, head_width = queries.shape
    block_count = length // block_size
    query_b = queries.reshape(block_count, block_size, head_width)
    key_b = key_rows.reshape(block_count, block_size, head_width)
    value_b = value_rows.reshape(block_count, block_size, head_width)
    house_b = house_rows.reshape(block_count, block_size, head_width)
    beta_b = beta_row.reshape(block_count, block_size)
    within = jnp.arange(block_size, dtype=jnp.int32)
    lower_eq = (within[:, None] >= within[None, :]).astype(jnp.float32)
    lower_st = (within[:, None] > within[None, :]).astype(jnp.float32)
    identity = jnp.eye(block_size, dtype=jnp.float32)
    inner = jnp.einsum("asd,atd->ast", house_b, house_b, precision=PRECISE)
    triangle = inner * lower_st + identity[None] / beta_b[:, :, None]
    inverse = jax.vmap(
        lambda matrix: jax.scipy.linalg.solve_triangular(matrix, identity, lower=True)
    )(triangle)
    masked_qw = jnp.einsum("aid,asd->ais", query_b, house_b, precision=PRECISE) * lower_eq
    left_part = jnp.einsum("ais,ast->ait", masked_qw, inverse, precision=PRECISE)
    masked_wk = jnp.einsum("atd,ajd->atj", house_b, key_b, precision=PRECISE) * lower_st
    right_part = jnp.einsum("ast,atj->asj", inverse, masked_wk, precision=PRECISE)
    moved_q = query_b - jnp.einsum("ait,atd->aid", left_part, house_b, precision=PRECISE)
    moved_k = key_b - jnp.einsum("asj,asd->ajd", right_part, house_b, precision=PRECISE)
    near_scores = jnp.einsum("aid,ajd->aij", query_b, key_b, precision=PRECISE) - jnp.einsum(
        "ait,atj->aij", left_part, masked_wk, precision=PRECISE
    )
    block_maps = jnp.eye(head_width, dtype=jnp.float32)[None] - jnp.einsum(
        "asd,ast,ate->ade", house_b, inverse, house_b, precision=PRECISE
    )
    seg_blocks = segment.reshape(block_count, block_size)
    keep_blocks = keep_key.reshape(block_count, block_size)
    causal = within[:, None] >= within[None, :]
    same_pos = within[:, None] == within[None, :]
    scale = 1.0 / math.sqrt(head_width)
    valid_list = []
    masked_list = []
    top_list = []
    carried = moved_q
    for offset in range(block_count):
        count = block_count - offset
        same_seg = seg_blocks[offset:][:, :, None] == seg_blocks[:count][:, None, :]
        key_ok = keep_blocks[:count][:, None, :] == 1
        if offset == 0:
            scores = near_scores
            valid = same_seg & causal[None] & (key_ok | same_pos[None])
        else:
            scores = jnp.einsum("aid,ajd->aij", carried, moved_k[:count], precision=PRECISE)
            valid = same_seg & key_ok
            if offset + 1 < block_count:
                carried = jnp.einsum(
                    "aid,ade->aie", carried[1:], block_maps[1:count], precision=PRECISE
                )
        if offset == 0:
            carried = moved_q[1:]
        masked = jnp.where(valid, scores * scale, -1e30)
        valid_list.append(valid)
        masked_list.append(masked)
        top_list.append(
            jnp.pad(jnp.max(masked, axis=2), ((offset, 0), (0, 0)), constant_values=-1e30)
        )
    top_score = jnp.max(jnp.stack(top_list, axis=0), axis=0)
    expo_list = []
    total = jnp.zeros((block_count, block_size), jnp.float32)
    for offset in range(block_count):
        expo = jnp.where(
            valid_list[offset], jnp.exp(masked_list[offset] - top_score[offset:][:, :, None]), 0.0
        )
        expo_list.append(expo)
        total = total + jnp.pad(jnp.sum(expo, axis=2), ((offset, 0), (0, 0)))
    mixed = jnp.zeros((block_count, block_size, head_width), jnp.float32)
    for offset in range(block_count):
        count = block_count - offset
        probs = expo_list[offset] / total[offset:][:, :, None]
        part = jnp.einsum("aij,ajd->aid", probs, value_b[:count], precision=PRECISE)
        mixed = mixed + jnp.pad(part, ((offset, 0), (0, 0), (0, 0)))
    return mixed.reshape(length, head_width)


def attend_heads(queries, key_rows, value_rows, house_rows, beta_rows, segment, keep_key):

    def one_head(parts):
        return path_head(parts[0], parts[1], parts[2], parts[3], parts[4], segment, keep_key, BLK)

    return lax.map(jax.checkpoint(one_head), (queries, key_rows, value_rows, house_rows, beta_rows))


def matmul_nn(left, right):
    return jnp.dot(left, right, preferred_element_type=jnp.float32)


def matmul_nt(left, right):
    return lax.dot_general(
        left, right, (((1,), (1,)), ((), ())), preferred_element_type=jnp.float32
    )


def matmul_tn(left, right):
    return lax.dot_general(
        left, right, (((0,), (0,)), ((), ())), preferred_element_type=jnp.float32
    )


def fetch_weights(w_query, w_key, w_value, w_house, w_beta, w_gate, w_up, w_out, w_down):
    row_full = (
        lax.all_gather(w_query, ("dp", "wid"), axis=0, tiled=True),
        lax.all_gather(w_key, ("dp", "wid"), axis=0, tiled=True),
        lax.all_gather(w_value, ("dp", "wid"), axis=0, tiled=True),
        lax.all_gather(w_house, ("dp", "wid"), axis=0, tiled=True),
        lax.all_gather(w_beta, ("dp", "wid"), axis=0, tiled=True),
        lax.all_gather(w_gate, ("dp", "wid"), axis=0, tiled=True),
        lax.all_gather(w_up, ("dp", "wid"), axis=0, tiled=True),
    )
    col_full = (
        lax.all_gather(w_out, ("dp", "wid"), axis=1, tiled=True),
        lax.all_gather(w_down, ("dp", "wid"), axis=1, tiled=True),
    )
    return (row_full, col_full)


def reduce_grads(row_terms, col_terms):
    row_sums = (
        lax.psum_scatter(
            row_terms[0].astype(jnp.bfloat16), ("dp", "wid"), scatter_dimension=0, tiled=True
        ).astype(jnp.float32),
        lax.psum_scatter(
            row_terms[1].astype(jnp.bfloat16), ("dp", "wid"), scatter_dimension=0, tiled=True
        ).astype(jnp.float32),
        lax.psum_scatter(
            row_terms[2].astype(jnp.bfloat16), ("dp", "wid"), scatter_dimension=0, tiled=True
        ).astype(jnp.float32),
        lax.psum_scatter(
            row_terms[3].astype(jnp.bfloat16), ("dp", "wid"), scatter_dimension=0, tiled=True
        ).astype(jnp.float32),
        lax.psum_scatter(
            row_terms[4].astype(jnp.bfloat16), ("dp", "wid"), scatter_dimension=0, tiled=True
        ).astype(jnp.float32),
        lax.psum_scatter(
            row_terms[5].astype(jnp.bfloat16), ("dp", "wid"), scatter_dimension=0, tiled=True
        ).astype(jnp.float32),
        lax.psum_scatter(
            row_terms[6].astype(jnp.bfloat16), ("dp", "wid"), scatter_dimension=0, tiled=True
        ).astype(jnp.float32),
    )
    col_sums = (
        lax.psum_scatter(
            col_terms[0].astype(jnp.bfloat16), ("dp", "wid"), scatter_dimension=1, tiled=True
        ).astype(jnp.float32),
        lax.psum_scatter(
            col_terms[1].astype(jnp.bfloat16), ("dp", "wid"), scatter_dimension=1, tiled=True
        ).astype(jnp.float32),
    )
    return (tuple(row_sums), tuple(col_sums))


def norm_forward(local_rows, gain_local):
    full_rows, full_gain = (
        lax.all_gather(local_rows, "hid", axis=1, tiled=True),
        lax.all_gather(gain_local, "hid", axis=1, tiled=True),
    )
    rows_wide = full_rows.astype(jnp.float32)
    row_scale = lax.rsqrt(jnp.mean(rows_wide * rows_wide, axis=1, keepdims=True) + EPSILON)
    normed = (rows_wide * row_scale * full_gain.astype(jnp.float32)).astype(jnp.bfloat16)
    return (normed, row_scale)


def sum_branch(partial_terms):
    return lax.psum_scatter(
        partial_terms.astype(jnp.bfloat16), "hid", scatter_dimension=1, tiled=True
    ).astype(jnp.float32)


def spread_grad(grad_local):
    return lax.all_gather(grad_local, "hid", axis=1, tiled=True)


def norm_backward(local_rows, gain_local, row_scale, grad_partial):
    grad_local = lax.psum_scatter(
        grad_partial.astype(jnp.bfloat16), "hid", scatter_dimension=1, tiled=True
    ).astype(jnp.float32)
    rows_local = local_rows.astype(jnp.float32)
    gain_vals = gain_local.astype(jnp.float32)
    row_total = lax.psum(jnp.sum(rows_local * gain_vals * grad_local, axis=1, keepdims=True), "hid")
    width_all = grad_partial.shape[1]
    back_rows = (
        row_scale * gain_vals * grad_local
        - rows_local * (row_scale * row_scale * row_scale) * row_total / width_all
    )
    gain_grad = jnp.sum(rows_local * row_scale * grad_local, axis=0, keepdims=True)
    return (back_rows, gain_grad)


def shards(
    tokens,
    cotangent,
    lengths,
    keep,
    norm_one,
    w_query,
    w_key,
    w_value,
    w_house,
    w_beta,
    w_out,
    norm_two,
    w_gate,
    w_up,
    w_down,
):
    row_locals = (w_query, w_key, w_value, w_house, w_beta, w_gate, w_up)
    col_locals = (w_out, w_down)
    start_rows = tuple((jnp.zeros(weight.shape, jnp.float32) for weight in row_locals))
    start_cols = tuple((jnp.zeros(weight.shape, jnp.float32) for weight in col_locals))
    start_gain = jnp.zeros(norm_one.shape, jnp.float32)

    def one_micro(running, micro_batch):
        tokens_mb, cotangent_mb, length_row, keep_row = micro_batch
        row_full, col_full = fetch_weights(
            w_query, w_key, w_value, w_house, w_beta, w_gate, w_up, w_out, w_down
        )
        query_w, key_w, value_w, house_w, beta_w, gate_w, up_w = row_full
        out_w, down_w = col_full
        segment = segment_ids(length_row[0], tokens_mb.shape[0])
        normed_one, scale_one = norm_forward(tokens_mb, norm_one)
        queries = matmul_nn(normed_one, query_w).astype(jnp.bfloat16)
        keys_all = matmul_nn(normed_one, key_w).astype(jnp.bfloat16)
        values_all = matmul_nn(normed_one, value_w).astype(jnp.bfloat16)
        house_raw = matmul_nn(normed_one, house_w)
        beta_all = 2.0 * jax.nn.sigmoid(matmul_nn(normed_one, beta_w))
        house_hat, house_pull = jax.vjp(normalize_heads, split_heads(house_raw))
        house_low = house_hat.astype(jnp.bfloat16)

        def attend_local(query_heads, key_heads, value_heads, house_heads, beta_heads):
            return attend_heads(
                query_heads, key_heads, value_heads, house_heads, beta_heads, segment, keep_row
            )

        mixed_heads, attend_pull = jax.vjp(
            attend_local,
            split_heads(queries).astype(jnp.float32),
            split_heads(keys_all).astype(jnp.float32),
            split_heads(values_all).astype(jnp.float32),
            house_low.astype(jnp.float32),
            beta_all.T,
        )
        mixed = merge_heads(mixed_heads).astype(jnp.bfloat16)
        branch = sum_branch(matmul_nn(mixed, out_w))
        hidden_res = tokens_mb.astype(jnp.float32) + branch
        hidden_low = hidden_res.astype(jnp.bfloat16)
        normed_two, scale_two = norm_forward(hidden_low, norm_two)
        gate_proj = matmul_nn(normed_two, gate_w)
        up_proj = matmul_nn(normed_two, up_w)
        activated = (jax.nn.silu(gate_proj) * up_proj).astype(jnp.bfloat16)
        ffn_out = sum_branch(matmul_nn(activated, down_w))
        layer_result = (hidden_res + ffn_out).astype(jnp.bfloat16)
        ffn_grad = spread_grad(cotangent_mb)
        act_grad = matmul_nt(ffn_grad, down_w)
        grad_down = matmul_tn(activated, ffn_grad)
        sigmoid_gate = jax.nn.sigmoid(gate_proj)
        gate_grad = (
            act_grad * up_proj * sigmoid_gate * (1.0 + gate_proj * (1.0 - sigmoid_gate))
        ).astype(jnp.bfloat16)
        up_grad = (act_grad * jax.nn.silu(gate_proj)).astype(jnp.bfloat16)
        grad_gate = matmul_tn(normed_two, gate_grad)
        grad_up = matmul_tn(normed_two, up_grad)
        back_two, gain_two = norm_backward(
            hidden_low, norm_two, scale_two, matmul_nt(gate_grad, gate_w) + matmul_nt(up_grad, up_w)
        )
        hidden_grad = cotangent_mb.astype(jnp.float32) + back_two
        branch_grad = spread_grad(hidden_grad.astype(jnp.bfloat16))
        mixed_grad = matmul_nt(branch_grad, out_w)
        grad_out = matmul_tn(mixed, branch_grad)
        query_heads_grad, key_heads_grad, value_heads_grad, house_hat_grad, beta_heads_grad = (
            attend_pull(split_heads(mixed_grad))
        )
        house_raw_grad = house_pull(house_hat_grad)[0]
        query_grad = merge_heads(query_heads_grad).astype(jnp.bfloat16)
        key_grad = merge_heads(key_heads_grad).astype(jnp.bfloat16)
        value_grad = merge_heads(value_heads_grad).astype(jnp.bfloat16)
        house_grad = merge_heads(house_raw_grad).astype(jnp.bfloat16)
        beta_grad = (beta_heads_grad.T * beta_all * (1.0 - 0.5 * beta_all)).astype(jnp.bfloat16)
        grad_query = matmul_tn(normed_one, query_grad)
        grad_key = matmul_tn(normed_one, key_grad)
        grad_value = matmul_tn(normed_one, value_grad)
        grad_house = matmul_tn(normed_one, house_grad)
        grad_beta = matmul_tn(normed_one, beta_grad)
        input_part = (
            matmul_nt(query_grad, query_w)
            + matmul_nt(key_grad, key_w)
            + matmul_nt(value_grad, value_w)
        )
        input_part = input_part + matmul_nt(house_grad, house_w) + matmul_nt(beta_grad, beta_w)
        back_one, gain_one = norm_backward(tokens_mb, norm_one, scale_one, input_part)
        input_grad = (hidden_grad + back_one).astype(jnp.bfloat16)
        row_terms = (grad_query, grad_key, grad_value, grad_house, grad_beta, grad_gate, grad_up)
        col_terms = (grad_out, grad_down)
        row_terms, col_terms = reduce_grads(row_terms, col_terms)
        sums_rows, sums_cols, sums_one, sums_two = running
        running = (
            jax.tree.map(jnp.add, sums_rows, row_terms),
            jax.tree.map(jnp.add, sums_cols, col_terms),
            sums_one + gain_one,
            sums_two + gain_two,
        )
        return (running, (layer_result, input_grad))

    running, (layer_out, tokens_grad) = lax.scan(
        one_micro,
        (start_rows, start_cols, start_gain, start_gain),
        (tokens, cotangent, lengths, keep),
    )
    final_rows, final_cols, gain_one_sum, gain_two_sum = running
    norm_one_grad, norm_two_grad = lax.psum((gain_one_sum, gain_two_sum), ("dp", "wid"))
    return (
        layer_out,
        tokens_grad,
        norm_one_grad,
        final_rows[0],
        final_rows[1],
        final_rows[2],
        final_rows[3],
        final_rows[4],
        final_cols[0],
        norm_two_grad,
        final_rows[5],
        final_rows[6],
        final_cols[1],
    )


def solution(mesh):
    placed = (
        P(None, ("dp", "wid"), "hid"),
        P(None, ("dp", "wid"), "hid"),
        P(None, ("dp", "wid"), None),
        P(None, ("dp", "wid")),
        P(None, "hid"),
        P(("dp", "wid"), "hid"),
        P(("dp", "wid"), "hid"),
        P(("dp", "wid"), "hid"),
        P(("dp", "wid"), "hid"),
        P(("dp", "wid"), "hid"),
        P("hid", ("dp", "wid")),
        P(None, "hid"),
        P(("dp", "wid"), "hid"),
        P(("dp", "wid"), "hid"),
        P("hid", ("dp", "wid")),
    )
    return jax.shard_map(
        shards,
        mesh=mesh,
        in_specs=placed,
        out_specs=(
            P(None, ("dp", "wid"), "hid"),
            P(None, ("dp", "wid"), "hid"),
            P(None, "hid"),
            P(("dp", "wid"), "hid"),
            P(("dp", "wid"), "hid"),
            P(("dp", "wid"), "hid"),
            P(("dp", "wid"), "hid"),
            P(("dp", "wid"), "hid"),
            P("hid", ("dp", "wid")),
            P(None, "hid"),
            P(("dp", "wid"), "hid"),
            P(("dp", "wid"), "hid"),
            P("hid", ("dp", "wid")),
        ),
        check_vma=False,
    )
```

profile of v0, /device:TPU:0, one launch (start us, length us, event | category | flops | bytes accessed | tf_op | source)
XLA Modules:
  0.0 2997.7 jit_solution(441268274830005823)
XLA Ops:
  7.3 2963.4 %while.135 = (s32[]{:T(128)}, f32[192,384]{1,0:T(8,128)}, f32[192,384]{1,0:T(8,128)}, f32[192,384]{1,0:T(8,128)}, f32[192,384]{1,0:T(8,128)}, /*index=5*/f32[192...) while((s32[]{:T(128)}, f32[192,384]{1,0:T(8,128)}, ...), condition=%wide.region_53.55_spmd.clone, body=%wide.region_0.54_spmd.clone.sunk | while | flops 22235643904 | bytes 488829632 | solution.py:339
  201.4 118.8 %while.136 = (s32[]{:T(128)}, bf16[3,384,128]{1,2,0:T(8,128)(2,1)S(1)}, f32[3,384,128]{2,1,0:T(8,128)}, f32[3,384,128]{2,1,0:T(8,128)}, f32[3,384,128]{2,1,0:T(8...) while((s32[]{:T(128)}, ...), condition=%wide.region_12.13_spmd.clone.clone, body=%wide.region_5.12_spmd.clone.clone.sunk | while | flops 1160118272 | bytes 12799429 | solution.py:117
  367.6 62.8 %all-gather.41.cloned.1.call-done = bf16[1024,1536]{0,1:T(8,128)(2,1)} async-done(((bf16[1024,192]{0,1:T(8,128)(2,1)}), bf16[1024,1536]{0,1:T(8,128)(2,1)}) %all-gather.41.cloned.1.call-update) | async-done | bytes 3145744 | tf_op jit(solution)/shard_map/while/body/eval_jaxpr/all_gather | solution.py:148
  449.6 61.0 %all-gather.35.cloned.1.call-done = bf16[1536,1024]{1,0:T(8,128)(2,1)} async-done(((bf16[192,1024]{1,0:T(8,128)(2,1)}), bf16[1536,1024]{1,0:T(8,128)(2,1)}) %all-gather.35.cloned.1.call-update) | async-done | bytes 3145744 | tf_op jit(solution)/shard_map/while/body/eval_jaxpr/all_gather | solution.py:143
  640.0 192.7 %while.137 = (s32[]{:T(128)}, bf16[3,384,128]{1,2,0:T(8,128)(2,1)}, bf16[3,384,128]{1,2,0:T(8,128)(2,1)}, bf16[3,384,128]{1,2,0:T(8,128)(2,1)}, f32[3,384,128]{1...) while((s32[]{:T(128)}, bf16[3,384,128]{1,2,0:T(8,128)(2,1)}, ...), condition=%wide.region_36.37_spmd, body=%wide.region_18.36_spmd.sunk | while | flops 3329469952 | bytes 42413528 | solution.py:117
  898.8 75.8 %reduce-scatter.50.cloned.1.call-done = bf16[192,1024]{1,0:T(8,128)(2,1)} async-done(((bf16[1536,1024]{1,0:T(8,128)(2,1)}), bf16[192,1024]{1,0:T(8,128)(2,1)}) %reduce-scatter.50.cloned.1.call-update) | async-done | bytes 393232 | tf_op jit(solution)/shard_map/while/body/eval_jaxpr/reduce_scatter | solution.py:173
  976.0 75.7 %reduce-scatter.48.cloned.1.call-done = bf16[192,1024]{1,0:T(8,128)(2,1)} async-done(((bf16[1536,1024]{1,0:T(8,128)(2,1)}), bf16[192,1024]{1,0:T(8,128)(2,1)}) %reduce-scatter.48.cloned.1.call-update) | async-done | bytes 393232 | tf_op jit(solution)/shard_map/while/body/eval_jaxpr/reduce_scatter | solution.py:170
  1053.0 75.9 %reduce-scatter.54.cloned.1.call-done = bf16[1024,192]{0,1:T(8,128)(2,1)} async-done(((bf16[1024,1536]{0,1:T(8,128)(2,1)}), bf16[1024,192]{0,1:T(8,128)(2,1)}) %reduce-scatter.54.cloned.1.call-update) | async-done | bytes 393232 | tf_op jit(solution)/shard_map/while/body/eval_jaxpr/reduce_scatter | solution.py:181
  1163.7 59.9 %reduce-scatter.44.cloned.1.call-done = bf16[192,384]{1,0:T(8,128)(2,1)} async-done(((bf16[1536,384]{1,0:T(8,128)(2,1)}), bf16[192,384]{1,0:T(8,128)(2,1)}) %reduce-scatter.44.cloned.1.call-update) | async-done | bytes 147472 | tf_op jit(solution)/shard_map/while/body/eval_jaxpr/reduce_scatter | solution.py:164
  1225.2 64.7 %reduce-scatter.52.cloned.1.call-done = bf16[384,192]{0,1:T(8,128)(2,1)} async-done(((bf16[384,1536]{0,1:T(8,128)(2,1)}), bf16[384,192]{0,1:T(8,128)(2,1)}) %reduce-scatter.52.cloned.1.call-update) | async-done | bytes 147472 | tf_op jit(solution)/shard_map/while/body/eval_jaxpr/reduce_scatter | solution.py:178
  1291.6 64.7 %reduce-scatter.40.cloned.1.call-done = bf16[192,384]{1,0:T(8,128)(2,1)} async-done(((bf16[1536,384]{1,0:T(8,128)(2,1)}), bf16[192,384]{1,0:T(8,128)(2,1)}) %reduce-scatter.40.cloned.1.call-update) | async-done | bytes 147472 | tf_op jit(solution)/shard_map/while/body/eval_jaxpr/reduce_scatter | solution.py:158
  1358.0 64.6 %reduce-scatter.42.cloned.1.call-done = bf16[192,384]{1,0:T(8,128)(2,1)} async-done(((bf16[1536,384]{1,0:T(8,128)(2,1)}), bf16[192,384]{1,0:T(8,128)(2,1)}) %reduce-scatter.42.cloned.1.call-update) | async-done | bytes 147472 | tf_op jit(solution)/shard_map/while/body/eval_jaxpr/reduce_scatter | solution.py:161
  1425.7 63.3 %reduce-scatter.38.cloned.1.call-done = bf16[192,384]{1,0:T(8,128)(2,1)} async-done(((bf16[1536,384]{1,0:T(8,128)(2,1)}), bf16[192,384]{1,0:T(8,128)(2,1)}) %reduce-scatter.38.cloned.1.call-update) | async-done | bytes 147472 | tf_op jit(solution)/shard_map/while/body/eval_jaxpr/reduce_scatter | solution.py:155
  1680.6 118.7 %while.136 = (s32[]{:T(128)}, bf16[3,384,128]{1,2,0:T(8,128)(2,1)S(1)}, f32[3,384,128]{2,1,0:T(8,128)}, f32[3,384,128]{2,1,0:T(8,128)}, f32[3,384,128]{2,1,0:T(8...) while((s32[]{:T(128)}, ...), condition=%wide.region_12.13_spmd.clone.clone, body=%wide.region_5.12_spmd.clone.clone.sunk | while | flops 1160118272 | bytes 12799429 | solution.py:117
  1846.5 62.8 %all-gather.41.cloned.1.call-done = bf16[1024,1536]{0,1:T(8,128)(2,1)} async-done(((bf16[1024,192]{0,1:T(8,128)(2,1)}), bf16[1024,1536]{0,1:T(8,128)(2,1)}) %all-gather.41.cloned.1.call-update) | async-done | bytes 3145744 | tf_op jit(solution)/shard_map/while/body/eval_jaxpr/all_gather | solution.py:148
  1928.6 60.8 %all-gather.35.cloned.1.call-done = bf16[1536,1024]{1,0:T(8,128)(2,1)} async-done(((bf16[192,1024]{1,0:T(8,128)(2,1)}), bf16[1536,1024]{1,0:T(8,128)(2,1)}) %all-gather.35.cloned.1.call-update) | async-done | bytes 3145744 | tf_op jit(solution)/shard_map/while/body/eval_jaxpr/all_gather | solution.py:143
  2118.9 192.8 %while.137 = (s32[]{:T(128)}, bf16[3,384,128]{1,2,0:T(8,128)(2,1)}, bf16[3,384,128]{1,2,0:T(8,128)(2,1)}, bf16[3,384,128]{1,2,0:T(8,128)(2,1)}, f32[3,384,128]{1...) while((s32[]{:T(128)}, bf16[3,384,128]{1,2,0:T(8,128)(2,1)}, ...), condition=%wide.region_36.37_spmd, body=%wide.region_18.36_spmd.sunk | while | flops 3329469952 | bytes 42413528 | solution.py:117
  2377.7 76.0 %reduce-scatter.50.cloned.1.call-done = bf16[192,1024]{1,0:T(8,128)(2,1)} async-done(((bf16[1536,1024]{1,0:T(8,128)(2,1)}), bf16[192,1024]{1,0:T(8,128)(2,1)}) %reduce-scatter.50.cloned.1.call-update) | async-done | bytes 393232 | tf_op jit(solution)/shard_map/while/body/eval_jaxpr/reduce_scatter | solution.py:173
  2455.0 75.6 %reduce-scatter.48.cloned.1.call-done = bf16[192,1024]{1,0:T(8,128)(2,1)} async-done(((bf16[1536,1024]{1,0:T(8,128)(2,1)}), bf16[192,1024]{1,0:T(8,128)(2,1)}) %reduce-scatter.48.cloned.1.call-update) | async-done | bytes 393232 | tf_op jit(solution)/shard_map/while/body/eval_jaxpr/reduce_scatter | solution.py:170
  2532.0 75.8 %reduce-scatter.54.cloned.1.call-done = bf16[1024,192]{0,1:T(8,128)(2,1)} async-done(((bf16[1024,1536]{0,1:T(8,128)(2,1)}), bf16[1024,192]{0,1:T(8,128)(2,1)}) %reduce-scatter.54.cloned.1.call-update) | async-done | bytes 393232 | tf_op jit(solution)/shard_map/while/body/eval_jaxpr/reduce_scatter | solution.py:181
  2703.9 64.7 %reduce-scatter.52.cloned.1.call-done = bf16[384,192]{0,1:T(8,128)(2,1)} async-done(((bf16[384,1536]{0,1:T(8,128)(2,1)}), bf16[384,192]{0,1:T(8,128)(2,1)}) %reduce-scatter.52.cloned.1.call-update) | async-done | bytes 147472 | tf_op jit(solution)/shard_map/while/body/eval_jaxpr/reduce_scatter | solution.py:178
  2770.3 64.6 %reduce-scatter.40.cloned.1.call-done = bf16[192,384]{1,0:T(8,128)(2,1)} async-done(((bf16[1536,384]{1,0:T(8,128)(2,1)}), bf16[192,384]{1,0:T(8,128)(2,1)}) %reduce-scatter.40.cloned.1.call-update) | async-done | bytes 147472 | tf_op jit(solution)/shard_map/while/body/eval_jaxpr/reduce_scatter | solution.py:158
  2836.7 64.6 %reduce-scatter.42.cloned.1.call-done = bf16[192,384]{1,0:T(8,128)(2,1)} async-done(((bf16[1536,384]{1,0:T(8,128)(2,1)}), bf16[192,384]{1,0:T(8,128)(2,1)}) %reduce-scatter.42.cloned.1.call-update) | async-done | bytes 147472 | tf_op jit(solution)/shard_map/while/body/eval_jaxpr/reduce_scatter | solution.py:161
  2904.5 63.4 %reduce-scatter.38.cloned.1.call-done = bf16[192,384]{1,0:T(8,128)(2,1)} async-done(((bf16[1536,384]{1,0:T(8,128)(2,1)}), bf16[192,384]{1,0:T(8,128)(2,1)}) %reduce-scatter.38.cloned.1.call-update) | async-done | bytes 147472 | tf_op jit(solution)/shard_map/while/body/eval_jaxpr/reduce_scatter | solution.py:155
  (1553 shorter events, 1696.5 us)
Async XLA Ops:
  12.1 308.1 %all-gather.37.cloned.1.call-start = ((), (), s32[]{:S(2)}) async-start(), calls=%async_computation.19 | async-start | bytes 1327104 | tf_op jit(solution)/shard_map/while/body/eval_jaxpr/all_gather | solution.py:147
  12.6 335.9 %reduce-scatter.34.cloned.1.call-start = ((), (), s32[]{:S(2)}) async-start(), calls=%async_computation.20 | async-start | bytes 1474560 | tf_op jit(solution)/shard_map/while
  351.8 255.7 %reduce-scatter.36.cloned.1.call-start = ((), (), s32[]{:S(2)}) async-start(), calls=%async_computation.25 | async-start | bytes 1474560 | tf_op jit(solution)/shard_map/while
  616.3 254.1 %reduce-scatter.58.cloned.1.call-start = ((), (), s32[]{:S(2)}) async-start(), calls=%async_computation.37 | async-start | bytes 1474560 | tf_op jit(solution)/shard_map/while
  624.8 273.1 %reduce-scatter.46.cloned.1.call-start = ((), (), s32[]{:S(2)}) async-start(), calls=%async_computation.31 | async-start | bytes 442368 | tf_op jit(solution)/shard_map/while
  844.8 284.1 %reduce-scatter.54.cloned.1.call-start = ((), (), s32[]{:S(2)}) async-start(), calls=%async_computation.35 | async-start | bytes 3538944 | tf_op jit(solution)/shard_map/while/body/eval_jaxpr/reduce_scatter | solution.py:181
  849.9 306.4 %reduce-scatter.56.cloned.1.call-start = ((), (), s32[]{:S(2)}) async-start(), calls=%async_computation.36 | async-start | bytes 1474560 | tf_op jit(solution)/shard_map/while
  858.9 364.6 %reduce-scatter.44.cloned.1.call-start = ((), (), s32[]{:S(2)}) async-start(), calls=%async_computation.30 | async-start | bytes 1327104 | tf_op jit(solution)/shard_map/while/body/eval_jaxpr/reduce_scatter | solution.py:164
  862.4 427.5 %reduce-scatter.52.cloned.1.call-start = ((), (), s32[]{:S(2)}) async-start(), calls=%async_computation.34 | async-start | bytes 1327104 | tf_op jit(solution)/shard_map/while/body/eval_jaxpr/reduce_scatter | solution.py:178
  865.8 490.5 %reduce-scatter.40.cloned.1.call-start = ((), (), s32[]{:S(2)}) async-start(), calls=%async_computation.28 | async-start | bytes 1327104 | tf_op jit(solution)/shard_map/while/body/eval_jaxpr/reduce_scatter | solution.py:158
  868.1 554.4 %reduce-scatter.42.cloned.1.call-start = ((), (), s32[]{:S(2)}) async-start(), calls=%async_computation.29 | async-start | bytes 1327104 | tf_op jit(solution)/shard_map/while/body/eval_jaxpr/reduce_scatter | solution.py:161
  870.3 618.6 %reduce-scatter.38.cloned.1.call-start = ((), (), s32[]{:S(2)}) async-start(), calls=%async_computation.27 | async-start | bytes 1327104 | tf_op jit(solution)/shard_map/while/body/eval_jaxpr/reduce_scatter | solution.py:155
  1495.3 304.0 %all-gather.37.cloned.1.call-start = ((), (), s32[]{:S(2)}) async-start(), calls=%async_computation.19 | async-start | bytes 1327104 | tf_op jit(solution)/shard_map/while/body/eval_jaxpr/all_gather | solution.py:147
  1496.1 331.5 %reduce-scatter.34.cloned.1.call-start = ((), (), s32[]{:S(2)}) async-start(), calls=%async_computation.20 | async-start | bytes 1474560 | tf_op jit(solution)/shard_map/while
  1830.7 255.7 %reduce-scatter.36.cloned.1.call-start = ((), (), s32[]{:S(2)}) async-start(), calls=%async_computation.25 | async-start | bytes 1474560 | tf_op jit(solution)/shard_map/while
  2095.2 254.2 %reduce-scatter.58.cloned.1.call-start = ((), (), s32[]{:S(2)}) async-start(), calls=%async_computation.37 | async-start | bytes 1474560 | tf_op jit(solution)/shard_map/while
  2103.7 273.1 %reduce-scatter.46.cloned.1.call-start = ((), (), s32[]{:S(2)}) async-start(), calls=%async_computation.31 | async-start | bytes 442368 | tf_op jit(solution)/shard_map/while
  2323.8 283.9 %reduce-scatter.54.cloned.1.call-start = ((), (), s32[]{:S(2)}) async-start(), calls=%async_computation.35 | async-start | bytes 3538944 | tf_op jit(solution)/shard_map/while/body/eval_jaxpr/reduce_scatter | solution.py:181
  2328.8 306.1 %reduce-scatter.56.cloned.1.call-start = ((), (), s32[]{:S(2)}) async-start(), calls=%async_computation.36 | async-start | bytes 1474560 | tf_op jit(solution)/shard_map/while
  2337.9 364.2 %reduce-scatter.44.cloned.1.call-start = ((), (), s32[]{:S(2)}) async-start(), calls=%async_computation.30 | async-start | bytes 1327104 | tf_op jit(solution)/shard_map/while/body/eval_jaxpr/reduce_scatter | solution.py:164
  2341.4 427.2 %reduce-scatter.52.cloned.1.call-start = ((), (), s32[]{:S(2)}) async-start(), calls=%async_computation.34 | async-start | bytes 1327104 | tf_op jit(solution)/shard_map/while/body/eval_jaxpr/reduce_scatter | solution.py:178
  2344.8 490.1 %reduce-scatter.40.cloned.1.call-start = ((), (), s32[]{:S(2)}) async-start(), calls=%async_computation.28 | async-start | bytes 1327104 | tf_op jit(solution)/shard_map/while/body/eval_jaxpr/reduce_scatter | solution.py:158
  2347.1 554.2 %reduce-scatter.42.cloned.1.call-start = ((), (), s32[]{:S(2)}) async-start(), calls=%async_computation.29 | async-start | bytes 1327104 | tf_op jit(solution)/shard_map/while/body/eval_jaxpr/reduce_scatter | solution.py:161
  2349.3 618.6 %reduce-scatter.38.cloned.1.call-start = ((), (), s32[]{:S(2)}) async-start(), calls=%async_computation.27 | async-start | bytes 1327104 | tf_op jit(solution)/shard_map/while/body/eval_jaxpr/reduce_scatter | solution.py:155
  (200 other events, 12212.6 us)
Sparse Core Ops, SparseCore 0:
  369.9 60.4 all-gather.40
  450.1 60.4 all-gather.34
  512.8 59.0 all-gather.44
  836.5 61.3 reduce-scatter.45
  901.3 73.2 reduce-scatter.49
  978.1 73.5 reduce-scatter.47
  1055.3 73.5 reduce-scatter.53
  1159.6 63.9 reduce-scatter.43
  1226.9 62.9 reduce-scatter.51
  1293.3 62.9 reduce-scatter.39
  1359.5 62.9 reduce-scatter.41
  1426.0 62.9 reduce-scatter.37
  1848.8 60.4 all-gather.40
  1929.0 60.4 all-gather.34
  1991.6 59.0 all-gather.44
  2315.4 61.3 reduce-scatter.45
  2380.4 73.2 reduce-scatter.49
  2457.1 73.5 reduce-scatter.47
  2534.2 73.4 reduce-scatter.53
  2638.2 63.9 reduce-scatter.43
  2705.4 63.1 reduce-scatter.51
  2771.8 63.0 reduce-scatter.39
  2838.2 63.1 reduce-scatter.41
  2904.7 63.1 reduce-scatter.37
  (26 shorter events, 739.6 us)
where the time goes:
time: 3000 us
  waiting for transfers between devices  1990 us (66%)
  other arithmetic  412 us (14%)
  matrix products  330 us (11%)
  local copies, waits for them, and re-layouts  122 us (4%)
  blocking collectives  121 us (4%)
    another operation x18, other arithmetic, path_head(): jax.scipy.linalg.solve_triangular(matrix, identity, lower=True)  354 us
    while x60, waiting for transfers between devices  201 us
    reduce_scatter x2, waiting for transfers between devices, reduce_grads(): lax.psum_scatter(row_terms[6].astype(jnp.bfloat16), ('dp', 'wid'), scatte...  152 us
    reduce_scatter x2, waiting for transfers between devices, reduce_grads(): lax.psum_scatter(col_terms[1].astype(jnp.bfloat16), ('dp', 'wid'), scatte...  152 us
    reduce_scatter x2, waiting for transfers between devices, reduce_grads(): lax.psum_scatter(row_terms[5].astype(jnp.bfloat16), ('dp', 'wid'), scatte...  151 us
    reduce_scatter x2, waiting for transfers between devices, reduce_grads(): lax.psum_scatter(col_terms[0].astype(jnp.bfloat16), ('dp', 'wid'), scatte...  129 us
    reduce_scatter x2, waiting for transfers between devices, reduce_grads(): lax.psum_scatter(row_terms[1].astype(jnp.bfloat16), ('dp', 'wid'), scatte...  129 us
    reduce_scatter x2, waiting for transfers between devices, reduce_grads(): lax.psum_scatter(row_terms[2].astype(jnp.bfloat16), ('dp', 'wid'), scatte...  129 us
  transfers between devices with their start and end apart: 50, of which 44 were waited for; matrix products, arithmetic and copies ran while one was open for 27% of the time, Pallas kernels for 0%

commit v1 on v0

v1 whole, which is shorter than its diff:
```python
import functools
import math

import jax
import jax.numpy as jnp
from jax import lax
from jax.experimental import pallas as pl
from jax.experimental.pallas import tpu as pltpu
from jax.sharding import PartitionSpec as P

BLK = 128
BUF = 384
EPSILON = 1e-06
F32 = jnp.float32
BF = jnp.bfloat16
MESH = pl.DeviceIdType.MESH
ANY = pl.BlockSpec(memory_space=pl.ANY)
VM = pl.BlockSpec(memory_space=pltpu.VMEM)
SM = pl.BlockSpec(memory_space=pltpu.SMEM)
DMA = pltpu.SemaphoreType.DMA
NRES = 30


def _dot(a,b,ca,cb): return lax.dot_general(a,b,(((ca,),(cb,)),((),())),preferred_element_type=F32)
def nn(a,b): return _dot(a.astype(BF),b.astype(BF),1,0)
def nt(a,b): return _dot(a.astype(BF),b.astype(BF),1,1)
def tn(a,b): return _dot(a.astype(BF),b.astype(BF),0,0)
def split(a):
    hi=a.astype(BF); return hi,(a-hi.astype(F32)).astype(BF)
def nn3(a,b):
    ah,al=split(a); bh,bl=split(b)
    return _dot(ah,bh,1,0)+(_dot(ah,bl,1,0)+_dot(al,bh,1,0))
INV=nn3
def iotas():
    return lax.broadcasted_iota(jnp.int32,(BLK,BLK),0), lax.broadcasted_iota(jnp.int32,(BLK,BLK),1)
def tri_inverse(inner, beta_col, row, col):
    diag=jnp.where(row==col, beta_col, 0.0)
    beta_lane=jnp.sum(diag,axis=0,keepdims=True)
    first=((row>>1)==(col>>1))&(row>col)
    x=diag-jnp.where(first, inner*beta_col*beta_lane, 0.0)
    lb=1
    while (1<<lb)<BLK:
        m=((row>>(lb+1))==(col>>(lb+1)))&((row>>lb)>(col>>lb))
        low=jnp.where(m,inner,0.0)
        x=x-INV(INV(x,low),x)
        lb+=1
    return x
def masks(a,c,e0,e1,keep_row,row,col):
    qp=row+BLK*a; kp=col+BLK*c
    segq=(qp>=e0).astype(jnp.int32)+(qp>=e1).astype(jnp.int32)
    segk=(kp>=e0).astype(jnp.int32)+(kp>=e1).astype(jnp.int32)
    ok=(segq==segk)
    if a==c: return ok&(row>=col)&((keep_row==1)|(row==col))
    return ok&(keep_row==1)
def fwd_unit(q,k,v,h,beta,keep,e0,e1):
    nb=len(q); row,col=iotas(); le=row>=col; st=row>col
    X,A1,L,W,R,Qm,Km=[],[],[],[],[],[],[]
    for a in range(nb):
        x=tri_inverse(nt(h[a],h[a]),beta[a],row,col).astype(BF)
        a1=jnp.where(le,nt(q[a],h[a]),0.0).astype(BF)
        w=jnp.where(st,nt(h[a],k[a]),0.0).astype(BF)
        l=nn(a1,x).astype(BF); r=nn(x,w).astype(BF)
        X.append(x);A1.append(a1);W.append(w);L.append(l);R.append(r)
        Qm.append((q[a].astype(F32)-nn(l,h[a])).astype(BF))
        Km.append((k[a].astype(F32)-tn(r,h[a])).astype(BF))
    scale=1.0/math.sqrt(BLK)
    S={}
    for a in range(nb):
        S[a,a]=nt(q[a],k[a])-nn(L[a],W[a])
    S[1,0]=nt(Qm[1],Km[0]); S[2,1]=nt(Qm[2],Km[1])
    u=nt(Qm[2],h[1]).astype(BF); ux=nn(u,X[1]).astype(BF)
    cq=(Qm[2].astype(F32)-nn(ux,h[1])).astype(BF)
    S[2,0]=nt(cq,Km[0])
    P={}; out=[]
    for a in range(nb):
        sc={c:jnp.where(masks(a,c,e0,e1,keep[c],row,col),S[a,c]*scale,-1e30) for c in range(a+1)}
        top=jnp.max(sc[0],axis=1,keepdims=True)
        for c in range(1,a+1): top=jnp.maximum(top,jnp.max(sc[c],axis=1,keepdims=True))
        ex={c:jnp.exp(sc[c]-top) for c in sc}
        tot=sum(jnp.sum(e,axis=1,keepdims=True) for e in ex.values())
        inv=1.0/tot
        o=0.0
        for c in sc:
            P[a,c]=(ex[c]*inv).astype(BF); o=o+nn(P[a,c],v[c])
        out.append(o)
    res=X+A1+L+W+R+Qm+Km+[u,ux,cq]+[P[0,0],P[1,0],P[1,1],P[2,0],P[2,1],P[2,2]]
    return out,res
def bwd_unit(q,k,v,h,do,res):
    nb=3; row,col=iotas(); le=row>=col; st=row>col
    X,A1,L,W,R,Qm,Km=[res[3*i:3*i+3] for i in range(7)]
    u,ux,cq=res[21:24]; pl_=res[24:30]
    P={(0,0):pl_[0],(1,0):pl_[1],(1,1):pl_[2],(2,0):pl_[3],(2,1):pl_[4],(2,2):pl_[5]}
    scale=1.0/math.sqrt(BLK)
    G={}; dv=[0.0]*nb
    for a in range(nb):
        dp={c:nt(do[a],v[c]) for c in range(a+1)}
        delta=sum(jnp.sum(P[a,c].astype(F32)*dp[c],axis=1,keepdims=True) for c in range(a+1))
        for c in range(a+1):
            G[a,c]=(P[a,c].astype(F32)*(dp[c]-delta)*scale).astype(BF)
            dv[c]=dv[c]+tn(P[a,c],do[a])
    dq=[nn(G[a,a],k[a]) for a in range(nb)]
    dk=[tn(G[a,a],q[a]) for a in range(nb)]
    dL=[-nt(G[a,a],W[a]) for a in range(nb)]
    dW=[-tn(L[a],G[a,a]) for a in range(nb)]
    dh=[0.0]*nb; dX=[0.0]*nb
    dcq=nn(G[2,0],Km[0]).astype(BF)
    dQm=[None, nn(G[1,0],Km[0]), nn(G[2,1],Km[1])+dcq.astype(F32)]
    dKm=[tn(G[1,0],Qm[1])+tn(G[2,0],cq), tn(G[2,1],Qm[2]), None]
    dux=(-nt(dcq,h[1])).astype(BF)
    dh[1]=dh[1]-tn(ux,dcq)
    du=nt(dux,X[1]).astype(BF)
    dX[1]=dX[1]+tn(u,dux)
    dQm[2]=dQm[2]+nn(du,h[1])
    dh[1]=dh[1]+tn(du,Qm[2])
    dbeta=[]
    for a in range(nb):
        if dQm[a] is not None:
            d_=dQm[a].astype(BF)
            dq[a]=dq[a]+d_.astype(F32); dL[a]=dL[a]-nt(d_,h[a]); dh[a]=dh[a]-tn(L[a],d_)
        if dKm[a] is not None:
            d_=dKm[a].astype(BF)
            dk[a]=dk[a]+d_.astype(F32); dR=(-nt(h[a],d_)).astype(BF); dh[a]=dh[a]-nn(R[a],d_)
            dX[a]=dX[a]+nt(dR,W[a]); dW[a]=dW[a]+tn(X[a],dR)
        dl=dL[a].astype(BF)
        dA=jnp.where(le,nt(dl,X[a]),0.0).astype(BF)
        dX[a]=dX[a]+tn(A1[a],dl)
        dw=jnp.where(st,dW[a],0.0).astype(BF)
        dh[a]=dh[a]+nn(dw,k[a]); dk[a]=dk[a]+tn(dw,h[a])
        dq[a]=dq[a]+nn(dA,h[a]); dh[a]=dh[a]+tn(dA,q[a])
        dM=nt(tn(X[a],dX[a]),X[a])
        dn=jnp.where(st,-dM,0.0).astype(BF)
        dh[a]=dh[a]+nn(dn,h[a])+tn(dn,h[a])
        dbeta.append(jnp.sum(jnp.where(row==col,dM,0.0),axis=1,keepdims=True))
    return dq,dk,dv,dh,dbeta


def spans(rows, step):
    return pl.ds(pl.multiple_of(rows, step), step)


class Place:
    def __init__(self, names, sizes):
        self.names, self.sizes = names, sizes
        self.d, self.h, self.w = (lax.axis_index(n) for n in ("dp", "hid", "wid"))
        self.dp, self.wid = sizes["dp"], sizes["wid"]
        self.c = lax.rem(self.h, 2)
        self.x = lax.div(self.h, 2)
        self.sib = self.at(h=self.h + 1 - 2 * self.c)
        self.xpeer = self.at(h=lax.rem(self.h + 2, 4))

    def at(self, d=None, h=None, w=None):
        where = {"dp": self.d if d is None else d, "hid": self.h if h is None else h, "wid": self.w if w is None else w}
        return tuple(where[n] for n in self.names)

    def greet(self, peers):
        barrier = pltpu.get_barrier_semaphore()
        for peer in peers:
            pl.semaphore_signal(barrier, inc=1, device_id=peer, device_id_type=MESH)
        pl.semaphore_wait(barrier, len(peers))

    def dp_peer(self, j):
        return self.at(d=lax.rem(self.d + j, self.dp))

    def wid_peer(self, k):
        return self.at(w=lax.rem(self.w + k, self.wid))

    def hid_peer(self, k):
        return self.at(h=lax.rem(self.h + k, 4))

    def group(self):
        return [
            self.at(d=lax.rem(self.d + i, self.dp), w=lax.rem(self.w + k, self.wid))
            for i in range(self.dp)
            for k in range(self.wid)
            if i + k > 0
        ]


def send(src, dst, sent, got, peer):
    return pltpu.make_async_remote_copy(
        src_ref=src, dst_ref=dst, send_sem=sent, recv_sem=got, device_id=peer, device_id_type=MESH
    )


class Gather:
    def __init__(self, me, rows, pack, full, col, source_col, width, ch, sz, rz, sy, ry):
        self.me, self.rows, self.full, self.ch = me, rows, full, ch
        self.col, self.width = col, width
        self.own = pack.at[:, pl.ds(source_col, width)]
        self.sz, self.rz, self.sy, self.ry = sz, rz, sy, ry

    def piece(self, d, o):
        return self.full.at[
            pl.ds(pl.multiple_of((d * self.me.wid + o) * self.rows, 16), self.rows), pl.ds(self.col, self.width)
        ]

    def zcopy(self, way, step):
        me, side = self.me, (way + 1) // 2
        origin = lax.clamp(0, me.w - way * step, me.wid - 1)
        src = self.own if step == 0 else self.piece(me.d, origin)
        return send(
            src,
            self.piece(me.d, origin),
            self.sz.at[self.ch, side, step],
            self.rz.at[self.ch, side, step],
            me.at(w=lax.clamp(0, me.w + way, me.wid - 1)),
        )

    def zrecv(self, way, step):
        me, side = self.me, (way + 1) // 2
        origin = lax.clamp(0, me.w - way * step, me.wid - 1)
        send(
            self.own,
            self.piece(me.d, origin),
            self.sz.at[self.ch, side, step - 1],
            self.rz.at[self.ch, side, step - 1],
            me.at(w=lax.clamp(0, me.w + way, me.wid - 1)),
        ).wait_recv()

    def ycopy(self, origin, j, src):
        me = self.me
        return send(
            src,
            self.piece(me.d, origin),
            self.sy.at[self.ch, origin, j - 1],
            self.ry.at[self.ch, origin, j - 1],
            me.dp_peer(j),
        )

    def has_next(self, way):
        return self.me.w < self.me.wid - 1 if way == 1 else self.me.w > 0

    def has_piece(self, way, step):
        return self.me.w - step >= 0 if way == 1 else self.me.w + step < self.me.wid

    def start_z(self):
        for way in (1, -1):

            @pl.when(self.has_next(way))
            def _():
                self.zcopy(way, 0).start()

    def start_y(self):
        for j in range(1, self.me.dp):
            self.ycopy(self.me.w, j, self.own).start()

    def step(self):
        me = self.me
        for step in range(1, me.wid):
            for way in (1, -1):

                @pl.when(self.has_piece(way, step))
                def _():
                    self.zrecv(way, step)

                    @pl.when(self.has_next(way))
                    def _():
                        self.zcopy(way, step).start()

                    origin = lax.clamp(0, me.w - way * step, me.wid - 1)
                    for j in range(1, me.dp):
                        self.ycopy(origin, j, self.piece(me.d, origin)).start()

    def finish(self):
        me = self.me
        for j in range(1, me.dp):
            for o in range(me.wid):
                send(
                    self.own,
                    self.piece(lax.rem(me.d + me.dp - j, me.dp), o),
                    self.sy.at[self.ch, o, j - 1],
                    self.ry.at[self.ch, o, j - 1],
                    me.dp_peer(j),
                ).wait_recv()

    def drain(self):
        me = self.me
        for way in (1, -1):

            @pl.when(self.has_next(way))
            def _():
                self.zcopy(way, 0).wait_send()

            for step in range(1, me.wid):

                @pl.when(self.has_piece(way, step) & self.has_next(way))
                def _():
                    self.zcopy(way, step).wait_send()

        for j in range(1, me.dp):
            for o in range(me.wid):
                self.ycopy(o, j, self.own).wait_send()


def column(values, lane_index):
    lanes = lax.broadcasted_iota(jnp.int32, values.shape, 1)
    return jnp.sum(jnp.where(lanes == lane_index, values, 0.0), axis=1, keepdims=True)


def forward_kernel(
    cfg, lens, keep, tok, cot, gains, pack,
    layer_out, hgrad, gain2, mgrad, qs, ks, vs, hs, hraw, beta, gf, res_o, n1_o, tok_o, wa_o, g_o,
    WA, WB, tokf, cotf, n1, n2, hlow, ng, mix, act, gg, ug, resb, s1, r1, s2, r2, acc, t2, q2, stage, hidown,
    local, hx_s, hx_r, sz, rz, sy, ry, s1s, s1r, s2s, s2r, s3s, s3r, outs, ress, stages,
):
    me = Place(cfg["names"], cfg["sizes"])
    T, D, CB, HL, HD, FL, RS = (cfg[k] for k in ("T", "D", "CB", "HL", "HD", "FL", "RS"))
    NCH = (HD + 3 * FL) // HD
    WAC = 4 * HD + BLK
    NB = T // BUF
    own_cols = pl.ds(pl.multiple_of(me.h * CB, BLK), CB)
    own_rows = pl.ds(pl.multiple_of((me.d * me.wid + me.w) * RS, 16), RS)
    c = me.c
    me.greet(
        [me.dp_peer(j) for j in range(1, me.dp)]
        + [me.wid_peer(k) for k in range(1, me.wid)]
        + [me.hid_peer(k) for k in range(1, 4)]
    )
    hid = []
    for i, (src, dst) in enumerate(((tok, tokf), (gains, gf), (cot, cotf))):
        here = pltpu.make_async_copy(src, dst.at[:, own_cols], local.at[i])
        away = [
            send(src, dst.at[:, own_cols], hx_s.at[i, k - 1], hx_r.at[i, k - 1], me.hid_peer(k)) for k in range(1, 4)
        ]
        hid.append([here] + away)
    for i in range(2):
        for copy in hid[i]:
            copy.start()
    sems = (sz, rz, sy, ry)
    first = [
        Gather(me, RS, pack, WA, a * HD, a * HD, HD + (BLK if a == 3 else 0), a, *sems) for a in range(4)
    ]

    def late(i):
        col = i * HD if isinstance(i, int) else pl.multiple_of(i * HD, BLK)
        source = WAC + i * HD if isinstance(i, int) else pl.multiple_of(WAC + i * HD, BLK)
        return Gather(me, RS, pack, WB, col, source, HD, 4 + i, *sems)

    for g in first:
        g.start_z()
        g.start_y()
    own_a = pltpu.make_async_copy(pack.at[:, pl.ds(0, WAC)], WA.at[own_rows, :], local.at[3])
    own_b = pltpu.make_async_copy(pack.at[:, pl.ds(WAC, HD + 3 * FL)], WB.at[own_rows, :], local.at[4])
    own_a.start()
    own_b.start()

    def start_late(i, carry):
        late(i).start_z()
        late(i).start_y()
        return carry

    lax.fori_loop(0, NCH, start_late, 0)
    for copy in hid[2]:
        copy.start()
    for i in range(2):
        for copy in hid[i]:
            copy.wait()
    outputs = []

    def save(src, dst, i):
        copy = pltpu.make_async_copy(src, dst, outs.at[i])
        copy.start()
        outputs.append(copy)

    save(tokf, tok_o, 0)
    RB = 32

    def norm(src, dst, gain, base):
        def body(i, carry):
            rows = spans(base + i * RB, RB)
            wide = src[rows, :].astype(F32)
            scale = lax.rsqrt(jnp.mean(wide * wide, axis=1, keepdims=True) + EPSILON)
            dst[rows, :] = (wide * scale * gf[gain : gain + 1, :]).astype(BF)
            return carry

        lax.fori_loop(0, BUF // RB, body, 0)

    for m in range(NB):
        norm(tokf, n1, 0, m * BUF)
    save(n1, n1_o, 1)

    def project(a):
        g = first[a]
        for m in range(NB):
            rows = n1[m * BUF : (m + 1) * BUF, :]
            made = nn(rows, WA[:, a * HD : (a + 1) * HD])
            for hd in range(HL):
                part = made[:, hd * BLK : (hd + 1) * BLK]
                u = m * HL + hd
                if a < 3:
                    (qs, ks, vs)[a][u] = part.astype(BF)
                else:
                    hraw[u] = part
                    hs[u] = (part * lax.rsqrt(jnp.sum(part * part, axis=1, keepdims=True) + EPSILON)).astype(BF)
            if a == 3:
                beta[m * BUF : (m + 1) * BUF, :] = 2.0 * jax.nn.sigmoid(nn(rows, WA[:, 4 * HD :]))

    own_a.wait()
    first[0].step()
    first[1].step()
    first[0].finish()
    project(0)
    first[2].step()
    first[1].finish()
    project(1)
    first[3].step()
    first[2].finish()
    project(2)
    first[3].finish()
    project(3)
    save(WA, wa_o, 2)
    own_b.wait()

    def attend(u, carry):
        m, hd = lax.div(u, HL), lax.rem(u, HL)
        slot = lax.rem(u, 2)
        e0 = lens[m, 0]
        e1 = e0 + lens[m, 1]
        parts = [slice(a * BLK, (a + 1) * BLK) for a in range(3)]
        strength = [column(beta[spans(m * BUF + a * BLK, BLK), :], hd) for a in range(3)]
        keys = [keep[m, :, p] for p in parts]
        out, res = fwd_unit(
            [qs[u, p, :] for p in parts], [ks[u, p, :] for p in parts], [vs[u, p, :] for p in parts],
            [hs[u, p, :] for p in parts], strength, keys, e0, e1,
        )
        for a in range(3):
            mix[spans(m * BUF + a * BLK, BLK), pl.ds(pl.multiple_of(hd * BLK, BLK), BLK)] = out[a].astype(BF)

        @pl.when(u >= 2)
        def _():
            pltpu.make_async_copy(resb.at[slot], res_o.at[u], ress.at[slot]).wait()

        for i, value in enumerate(res):
            resb[slot, i] = value
        pltpu.make_async_copy(resb.at[slot], res_o.at[u], ress.at[slot]).start()

        @pl.when(u < NCH)
        def _():
            late(u).step()

        return carry

    U = NB * HL
    lax.fori_loop(0, U, attend, 0)
    for slot in range(2):
        pltpu.make_async_copy(resb.at[slot], res_o.at[0], ress.at[slot]).wait()

    def hop1(tag, m, j):
        return send(s1.at[m, j], r1.at[tag // 2, m, j], s1s.at[tag, m, j], s1r.at[tag, m, j], me.sib)

    def hop2(tag, m, j):
        return send(s2.at[m, j], r2.at[tag, m, j], s2s.at[tag, m, j], s2r.at[tag, m, j], me.xpeer)

    def block(b):
        return pl.ds(pl.multiple_of(b * CB, BLK), CB)

    def first_hop(tag, m, partial):
        for j in range(2):
            s1[m, j] = partial((1 - c) + 2 * j).astype(BF)
            hop1(tag, m, j).start()
        for j in range(2):
            acc[m, j] = partial(c + 2 * j)

    def second_hop(tag, m):
        for j in range(2):
            hop1(tag, m, j).wait()
            s2[m, j] = (acc[m, j] + r1[tag // 2, m, j].astype(F32)).astype(BF)
            hop2(tag, m, j).start()

    def total(tag, m, j):
        return s2[m, j].astype(F32) + r2[tag, m, j].astype(F32)

    def third(tag, full, m, b):
        part = full.at[m * BUF : (m + 1) * BUF, block(b)]
        return send(part, part, s3s.at[tag, m, lax.div(b, 2)], s3r.at[tag, m, lax.div(b, 2)], me.sib)

    def wait_third(tag, full, m):
        for j in range(2):
            third(tag, full, m, (1 - c) + 2 * j).wait_recv()
            third(tag, full, m, c + 2 * j).wait_send()

    def rows_of(m):
        return slice(m * BUF, (m + 1) * BUF)

    def branch(m):
        return lambda b: nt(mix[rows_of(m), :], WB[block(b), 0:HD])

    GC, UC, DC = HD, HD + FL, HD + 2 * FL
    late(0).finish()
    for m in range(NB):
        first_hop(0, m, branch(m))
    rest = list(range(min(U, NCH), NCH))
    half = (len(rest) + 1) // 2
    for i in rest[:half]:
        late(i).step()
    for m in range(NB):
        second_hop(0, m)
    for i in rest[half:]:
        late(i).step()

    def residual(m):
        for j in range(2):
            hop2(0, m, j).wait()
            b = c + 2 * j
            hidden = tokf[rows_of(m), block(b)].astype(F32) + total(0, m, j)
            hlow[rows_of(m), block(b)] = hidden.astype(BF)
            third(0, hlow, m, b).start()
        hidown[rows_of(m), :] = tokf[rows_of(m), own_cols].astype(F32) + (
            s2[m, me.x].astype(F32) + r2[0, m, me.x].astype(F32)
        )

    for m in range(NB):
        residual(m)
    for m in range(NB):
        wait_third(0, hlow, m)
        norm(hlow, n2, 8, m * BUF)
    for copy in hid[2]:
        copy.wait()

    def finish_late(i, carry):
        late(i).finish()
        return carry

    lax.fori_loop(1, NCH, finish_late, 0)
    NT = 256

    def ffn(m):
        def body(n, carry):
            at = pl.multiple_of(n * NT, NT)
            gate = nn(n2[rows_of(m), :], WB[:, pl.ds(pl.multiple_of(GC + at, BLK), NT)])
            up = nn(n2[rows_of(m), :], WB[:, pl.ds(pl.multiple_of(UC + at, BLK), NT)])
            back = nn(cotf[rows_of(m), :], WB[:, pl.ds(pl.multiple_of(DC + at, BLK), NT)])
            sig = jax.nn.sigmoid(gate)
            silu = gate * sig
            cols = pl.ds(at, NT)
            act[rows_of(m), cols] = (silu * up).astype(BF)
            gg[rows_of(m), cols] = (back * up * sig * (1.0 + gate * (1.0 - sig))).astype(BF)
            ug[rows_of(m), cols] = (back * silu).astype(BF)
            return carry

        lax.fori_loop(0, FL // NT, body, 0)

    def normed_back(m):
        return lambda b: nt(gg[rows_of(m), :], WB[block(b), GC : GC + FL]) + nt(
            ug[rows_of(m), :], WB[block(b), UC : UC + FL]
        )

    def down(m):
        return lambda b: nt(act[rows_of(m), :], WB[block(b), DC : DC + FL])

    for m in range(NB):
        ffn(m)
        first_hop(1, m, normed_back(m))
    for m in range(NB):
        second_hop(1, m)

    def staged(i, col, width):
        return pltpu.make_async_copy(
            stage.at[i, :, pl.ds(0, width)],
            g_o.at[pl.ds(pl.multiple_of(i * CB, BLK), CB), pl.ds(col, width)],
            stages.at[i],
        )

    busy = []

    def weight_term(left, right, col, width):
        before = busy[-1] if busy else None

        def body(i, carry):
            if before is not None:
                staged(i, *before).wait()
            stage[i, :, pl.ds(0, width)] = tn(left[:, pl.ds(pl.multiple_of(i * CB, BLK), CB)], right[...]).astype(BF)
            staged(i, col, width).start()
            return carry

        lax.fori_loop(0, D // CB, body, 0)
        busy.append((col, width))

    weight_term(cotf, act, DC, FL)

    def spread_back(m):
        for j in range(2):
            hop2(1, m, j).wait()
            b = c + 2 * j
            ng[rows_of(m), block(b)] = total(1, m, j).astype(BF)
            third(1, ng, m, b).start()

    def hop2_out(m):
        return send(t2.at[m], q2.at[m], s2s.at[2, m, 0], s2r.at[2, m, 0], me.xpeer)

    for m in range(NB):
        first_hop(2, m, down(m))
    for m in range(NB):
        spread_back(m)
    for m in range(NB):
        for j in range(2):
            hop1(2, m, j).wait()
        other = 1 - me.x
        t2[m] = (acc[m, other] + r1[1, m, other].astype(F32)).astype(BF)
        hop2_out(m).start()
    weight_term(n2, gg, GC, FL)
    gain2[...] = jnp.zeros_like(gain2)

    def branch_back(m):
        def body(i, carry):
            rows = spans(m * BUF + i * RB, RB)
            low = hlow[rows, :].astype(F32)
            scale = lax.rsqrt(jnp.mean(low * low, axis=1, keepdims=True) + EPSILON)
            scaled = ng[rows, :].astype(F32) * gf[8:9, :]
            row_total = jnp.sum(low * scaled, axis=1, keepdims=True)
            cube = scale * scale * scale * row_total / D
            low_own = hlow[rows, own_cols].astype(F32)
            ng_own = ng[rows, own_cols].astype(F32)
            hgrad[rows, :] = (
                cotf[rows, own_cols].astype(F32) + scale * gf[8:9, own_cols] * ng_own - low_own * cube
            )
            gain2[...] += jnp.broadcast_to(jnp.sum(low_own * scale * ng_own, axis=0, keepdims=True), gain2.shape)
            ng[rows, :] = (cotf[rows, :].astype(F32) + scale * scaled - low * cube).astype(BF)
            return carry

        lax.fori_loop(0, BUF // RB, body, 0)
        made = nn(ng[rows_of(m), :], WB[:, 0:HD])
        for hd in range(HL):
            mgrad[m * HL + hd] = made[:, hd * BLK : (hd + 1) * BLK].astype(BF)

    for m in range(NB):
        wait_third(1, ng, m)
        branch_back(m)
    weight_term(n2, ug, UC, FL)
    weight_term(ng, mix, 0, HD)
    for m in range(NB):
        hop2_out(m).wait()
        layer_out[rows_of(m), :] = (
            hidown[rows_of(m), :] + (acc[m, me.x] + r1[1, m, me.x].astype(F32) + q2[m].astype(F32))
        ).astype(BF)

    def last_stage(i, carry):
        staged(i, *busy[-1]).wait()
        return carry

    lax.fori_loop(0, D // CB, last_stage, 0)
    for copy in outputs:
        copy.wait()
    for g in first:
        g.drain()

    def drain_late(i, carry):
        late(i).drain()
        return carry

    lax.fori_loop(0, NCH, drain_late, 0)


def backward_kernel(
    cfg, tok_i, n1_i, gf, wa_i, q_i, k_i, v_i, h_i, hraw_i, beta, mgrad_i, res_i, g_i, hgrad, gain2,
    oA, oF, tgrad, one, two,
    tokf, n1, WA, qs, ks, vs, hs, hraw, mgrad, resb, dA, dbeta, ga, ry, gm, zr, rya, zra,
    s1, r1, acc, t2, q2, rts, rtr, rt, gbuf,
    local, ress, gms, sys, syr, szs, szr, ays, ayr, azs, azr, s1s, s1r, s2s, s2r, rs_s, rs_r, gs_s, gs_r,
):
    me = Place(cfg["names"], cfg["sizes"])
    T, D, CB, HL, HD, FL, RS = (cfg[k] for k in ("T", "D", "CB", "HL", "HD", "FL", "RS"))
    NCH = (HD + 3 * FL) // HD
    NB, U = T // BUF, T // BUF * HL
    DR = RS * me.wid
    c = me.c
    own_cols = pl.ds(pl.multiple_of(me.h * CB, BLK), CB)
    me.greet(me.group() + [me.hid_peer(k) for k in range(1, 4)])

    def dp_rows(j):
        return pl.ds(pl.multiple_of(lax.rem(me.d + j, me.dp) * DR, 16), DR)

    def late_cols(i):
        return pl.ds(pl.multiple_of(i * HD, BLK), HD)

    def late_y(i, j):
        return send(
            g_i.at[dp_rows(j), late_cols(i)], ry.at[i, j - 1], sys.at[i, j - 1], syr.at[i, j - 1], me.dp_peer(j)
        )

    def send_late(i, carry):
        for j in range(1, me.dp):
            late_y(i, j).start()
        return carry

    lax.fori_loop(0, NCH, send_late, 0)
    loads = [
        pltpu.make_async_copy(src, dst, local.at[i])
        for i, (src, dst) in enumerate(
            ((q_i, qs), (k_i, ks), (v_i, vs), (h_i, hs), (hraw_i, hraw), (mgrad_i, mgrad), (n1_i, n1), (tok_i, tokf))
        )
    ]
    loads.append(pltpu.make_async_copy(wa_i, WA, local.at[8]))

    def fetch_res(u):
        slot = lax.rem(u, 2)
        return pltpu.make_async_copy(res_i.at[u], resb.at[slot], ress.at[slot])

    def fetch_mine(i):
        slot = lax.rem(i, 2)
        return pltpu.make_async_copy(g_i.at[dp_rows(0), late_cols(i)], gm.at[slot], gms.at[slot])

    fetch_res(0).start()
    for copy in loads:
        copy.start()
    fetch_mine(0).start()
    for copy in loads[:6]:
        copy.wait()
    dbeta[...] = jnp.zeros_like(dbeta)

    def mine_of(o):
        return pl.ds(pl.multiple_of(o * RS, 16), RS)

    def late_z(i, k):
        o = lax.rem(me.w + k, me.wid)
        return send(ry.at[i, 0, mine_of(o), :], zr.at[i, k - 1], szs.at[i, k - 1], szr.at[i, k - 1], me.wid_peer(k))

    def late_stage(i):
        slot = lax.rem(i, 2)
        fetch_mine(i).wait()

        @pl.when(i + 1 < NCH)
        def _():
            fetch_mine(i + 1).start()

        for j in range(1, me.dp):
            late_y(i, j).wait_recv()
        for k in list(range(1, me.wid)) + [0]:
            rows = mine_of(lax.rem(me.w + k, me.wid))
            total = gm[slot, rows, :].astype(F32)
            for j in range(1, me.dp):
                total = total + ry[i, j - 1, rows, :].astype(F32)
            ry[i, 0, rows, :] = total.astype(BF)
            if k > 0:
                late_z(i, k).start()

    def attend_back(u, carry):
        m, hd = lax.div(u, HL), lax.rem(u, HL)
        slot = lax.rem(u, 2)
        parts = [slice(a * BLK, (a + 1) * BLK) for a in range(3)]
        fetch_res(u).wait()

        @pl.when(u + 1 < U)
        def _():
            fetch_res(u + 1).start()

        dq, dk, dv, dh, db = bwd_unit(
            [qs[u, p, :] for p in parts], [ks[u, p, :] for p in parts], [vs[u, p, :] for p in parts],
            [hs[u, p, :] for p in parts], [mgrad[u, p, :] for p in parts], [resb[slot, i] for i in range(NRES)],
        )
        for a in range(3):
            rows = spans(m * BUF + a * BLK, BLK)
            for n, value in enumerate((dq[a], dk[a], dv[a])):
                dA[rows, pl.ds(pl.multiple_of(n * HD + hd * BLK, BLK), BLK)] = value.astype(BF)
            raw = hraw[u, parts[a], :]
            scale = lax.rsqrt(jnp.sum(raw * raw, axis=1, keepdims=True) + EPSILON)
            along = jnp.sum(raw * dh[a], axis=1, keepdims=True)
            dA[rows, pl.ds(pl.multiple_of(3 * HD + hd * BLK, BLK), BLK)] = (
                scale * dh[a] - raw * (scale * scale * scale * along)
            ).astype(BF)
            strength = column(beta[rows, :], hd)
            pull = db[a] * (1.0 / jnp.maximum(strength, 1e-30) - 0.5)
            lanes = lax.broadcasted_iota(jnp.int32, (BLK, BLK), 1)
            dbeta[rows, :] += jnp.where(lanes == hd, pull, 0.0)

        @pl.when(u < NCH)
        def _():
            late_stage(u)

        return carry

    lax.fori_loop(0, U, attend_back, 0)
    dA[:, 4 * HD :] = dbeta[...].astype(BF)
    for copy in loads[6:]:
        copy.wait()

    bounds = [(a * HD, HD + (BLK if a == 3 else 0)) for a in range(4)]

    def first_y(a, j):
        col, width = bounds[a]
        return send(
            ga.at[dp_rows(j), pl.ds(col, width)], rya.at[j - 1, :, pl.ds(col, width)],
            ays.at[a, j - 1], ayr.at[a, j - 1], me.dp_peer(j),
        )

    whole = DR % CB == 0
    for a, (col, width) in enumerate(bounds):
        for j in list(range(1, me.dp)) + [0]:
            if whole:
                for i in range(DR // CB):
                    at = pl.multiple_of(lax.rem(me.d + j, me.dp) * DR + i * CB, BLK)
                    ga[pl.ds(at, CB), col : col + width] = tn(n1[:, pl.ds(at, CB)], dA[:, col : col + width]).astype(BF)
            elif j == min(1, me.dp - 1):
                for i in range(D // CB):
                    at = slice(i * CB, (i + 1) * CB)
                    ga[at, col : col + width] = tn(n1[:, at], dA[:, col : col + width]).astype(BF)
            if j > 0:
                first_y(a, j).start()

    def block(b):
        return pl.ds(pl.multiple_of(b * CB, BLK), CB)

    def hop1(j):
        return send(s1.at[j], r1.at[j], s1s.at[j], s1r.at[j], me.sib)

    hop2 = send(t2, q2, s2s, s2r, me.xpeer)
    rt[...] = jnp.zeros_like(rt)

    def partial(b, m):
        rows = slice(m * BUF, (m + 1) * BUF)
        made = nt(dA[rows, :], WA[block(b), :])
        along = jnp.sum(made * tokf[rows, block(b)].astype(F32) * gf[0:1, block(b)], axis=1, keepdims=True)
        rt[rows, :] += jnp.broadcast_to(along, (BUF, BLK))
        return made

    for j in range(2):
        for m in range(NB):
            s1[j, m * BUF : (m + 1) * BUF, :] = partial((1 - c) + 2 * j, m).astype(BF)
        hop1(j).start()
    for j in range(2):
        for m in range(NB):
            acc[j, m * BUF : (m + 1) * BUF, :] = partial(c + 2 * j, m)
    for i in range(T // BLK):
        rts[:, i * BLK : (i + 1) * BLK] = rt[i * BLK : (i + 1) * BLK, :].T[0:8, :]
    rt_copies = [send(rts, rtr.at[k - 1], rs_s.at[k - 1], rs_r.at[k - 1], me.hid_peer(k)) for k in range(1, 4)]
    for copy in rt_copies:
        copy.start()
    for j in range(2):
        hop1(j).wait()
    other = 1 - me.x
    t2[...] = (acc[other] + r1[other].astype(F32)).astype(BF)
    hop2.start()
    for i in range(min(U, NCH), NCH):
        late_stage(jnp.int32(i))
    hop2.wait()
    for copy in rt_copies:
        copy.wait()
    slot = me.d * me.wid + me.w
    gbuf[slot] = jnp.concatenate([jnp.zeros_like(gain2), gain2[...]], axis=0)

    def token_rows(i, carry):
        rows = spans(i * BLK, BLK)
        lane = rts[0:1, rows] + rtr[0, 0:1, rows] + rtr[1, 0:1, rows] + rtr[2, 0:1, rows]
        row_total = jnp.broadcast_to(lane, (BLK, BLK)).T[:, 0:1]
        wide = tokf[rows, :].astype(F32)
        scale = lax.rsqrt(jnp.mean(wide * wide, axis=1, keepdims=True) + EPSILON)
        made = acc[me.x, rows, :] + r1[me.x, rows, :].astype(F32) + q2[rows, :].astype(F32)
        own = tokf[rows, own_cols].astype(F32)
        back = scale * gf[0:1, own_cols] * made - own * (scale * scale * scale * row_total / D)
        tgrad[rows, :] = (hgrad[rows, :] + back).astype(BF)
        gbuf[slot, 0:8, :] += jnp.broadcast_to(jnp.sum(own * scale * made, axis=0, keepdims=True), (8, CB))
        return carry

    lax.fori_loop(0, T // BLK, token_rows, 0)
    gain_copies = []
    for n, peer in enumerate(me.group()):
        copy = send(gbuf.at[slot], gbuf.at[slot], gs_s.at[n], gs_r.at[n], peer)
        copy.start()
        gain_copies.append(copy)

    def first_z(a, k):
        col, width = bounds[a]
        o = lax.rem(me.w + k, me.wid)
        return send(
            rya.at[0, mine_of(o), pl.ds(col, width)], zra.at[k - 1, :, pl.ds(col, width)],
            azs.at[a, k - 1], azr.at[a, k - 1], me.wid_peer(k),
        )

    for a, (col, width) in enumerate(bounds):
        for j in range(1, me.dp):
            first_y(a, j).wait_recv()
        cols = slice(col, col + width)
        for k in list(range(1, me.wid)) + [0]:
            o = lax.rem(me.w + k, me.wid)
            rows = mine_of(o)
            total = ga[pl.ds(pl.multiple_of(me.d * DR + o * RS, 16), RS), cols].astype(F32)
            for j in range(1, me.dp):
                total = total + rya[j - 1, rows, cols].astype(F32)
            rya[0, rows, cols] = total.astype(BF)
            if k > 0:
                first_z(a, k).start()

    def late_sum(i, carry):
        total = ry[i, 0, mine_of(me.w), :].astype(F32)
        for k in range(1, me.wid):
            late_z(i, k).wait()
            total = total + zr[i, k - 1].astype(F32)
        oF[:, late_cols(i)] = total
        for j in range(1, me.dp):
            late_y(i, j).wait_send()
        return carry

    lax.fori_loop(0, NCH, late_sum, 0)
    for copy in gain_copies:
        copy.wait()
    both = gbuf[0]
    for n in range(1, me.dp * me.wid):
        both = both + gbuf[n]
    one[...] = both[0:1, :]
    two[...] = both[8:9, :]
    for a, (col, width) in enumerate(bounds):
        cols = slice(col, col + width)
        total = rya[0, mine_of(me.w), cols].astype(F32)
        for k in range(1, me.wid):
            first_z(a, k).wait()
            total = total + zra[k - 1, :, cols].astype(F32)
        oA[:, cols] = total
        for j in range(1, me.dp):
            first_y(a, j).wait_send()


def solution(mesh):
    names = tuple(mesh.axis_names)
    sizes = {n: mesh.shape[n] for n in names}
    dp, wid = sizes["dp"], sizes["wid"]
    assert sizes["hid"] == 4

    def shards(
        tokens, cotangent, lengths, keep, norm_one, w_query, w_key, w_value, w_house, w_beta, w_out, norm_two,
        w_gate, w_up, w_down,
    ):
        micro, rows, CB = tokens.shape
        T, D, HD, FL, RS = micro * rows, CB * 4, w_query.shape[1], w_gate.shape[1], w_query.shape[0]
        HL, NB = HD // BLK, T // BUF
        U, WAC, WBC = NB * HL, 4 * HD + BLK, HD + 3 * FL
        NCH, DR = WBC // HD, D // dp
        heads = w_beta.shape[1]
        cfg = dict(names=names, sizes=sizes, T=T, D=D, CB=CB, HL=HL, HD=HD, FL=FL, RS=RS)
        pack = jnp.concatenate(
            [w_query, w_key, w_value, w_house, jnp.pad(w_beta, ((0, 0), (0, BLK - heads))), w_out.T, w_gate, w_up,
             w_down.T], axis=1)
        gains = jnp.concatenate([jnp.broadcast_to(g, (8, CB)) for g in (norm_one, norm_two)], axis=0).astype(F32)
        sd = jax.ShapeDtypeStruct
        nch = 4 + NCH
        params = dict(has_side_effects=True, vmem_limit_bytes=62 << 20)
        unit = lambda t: sd((U, BUF, BLK), t)
        fwd = pl.pallas_call(
            functools.partial(forward_kernel, cfg),
            out_shape=(
                sd((T, CB), BF), sd((T, CB), F32), sd((8, CB), F32), unit(BF), unit(BF), unit(BF), unit(BF), unit(BF),
                unit(F32), sd((T, BLK), F32), sd((16, D), F32), sd((U, NRES, BLK, BLK), BF), sd((T, D), BF),
                sd((T, D), BF), sd((D, WAC), BF), sd((D, WBC), BF),
            ),
            in_specs=[SM, VM, ANY, ANY, ANY, ANY],
            out_specs=(VM,) * 11 + (ANY,) * 5,
            scratch_shapes=[
                pltpu.VMEM((D, WAC), BF), pltpu.VMEM((D, WBC), BF), pltpu.VMEM((T, D), BF), pltpu.VMEM((T, D), BF),
                pltpu.VMEM((T, D), BF), pltpu.VMEM((T, D), BF), pltpu.VMEM((T, D), BF), pltpu.VMEM((T, D), BF),
                pltpu.VMEM((T, HD), BF), pltpu.VMEM((T, FL), BF), pltpu.VMEM((T, FL), BF), pltpu.VMEM((T, FL), BF),
                pltpu.VMEM((2, NRES, BLK, BLK), BF),
                pltpu.VMEM((NB, 2, BUF, CB), BF), pltpu.VMEM((2, NB, 2, BUF, CB), BF),
                pltpu.VMEM((NB, 2, BUF, CB), BF), pltpu.VMEM((2, NB, 2, BUF, CB), BF),
                pltpu.VMEM((NB, 2, BUF, CB), F32),
                pltpu.VMEM((NB, BUF, CB), BF), pltpu.VMEM((NB, BUF, CB), BF),
                pltpu.VMEM((4, CB, max(FL, HD)), BF), pltpu.VMEM((T, CB), F32),
                DMA((5,)), DMA((3, 3)), DMA((3, 3)), DMA((nch, 2, wid)), DMA((nch, 2, wid)),
                DMA((nch, wid, max(dp - 1, 1))), DMA((nch, wid, max(dp - 1, 1))),
                DMA((3, NB, 2)), DMA((3, NB, 2)), DMA((3, NB, 2)), DMA((3, NB, 2)), DMA((2, NB, 2)), DMA((2, NB, 2)),
                DMA((3,)), DMA((2,)), DMA((4,)),
            ],
            compiler_params=pltpu.CompilerParams(collective_id=0, **params),
            name="forward",
        )
        (layer_out, hgrad, gain2, mgrad, qs, ks, vs, hs, hraw, beta, gf, res, n1, tokf, wa, g) = fwd(
            lengths.reshape(NB, lengths.shape[2]), keep.reshape(NB, 1, BUF), tokens.reshape(T, CB),
            cotangent.reshape(T, CB), gains, pack,
        )
        bwd = pl.pallas_call(
            functools.partial(backward_kernel, cfg),
            out_shape=(
                sd((RS, WAC), F32), sd((RS, WBC), F32), sd((T, CB), BF), sd((1, CB), F32), sd((1, CB), F32),
            ),
            in_specs=[ANY, ANY, VM, ANY] + [ANY] * 5 + [VM, ANY, ANY, ANY, VM, VM],
            out_specs=(VM,) * 5,
            scratch_shapes=[
                pltpu.VMEM((T, D), BF), pltpu.VMEM((T, D), BF), pltpu.VMEM((D, WAC), BF),
                *[pltpu.VMEM((U, BUF, BLK), BF)] * 4, pltpu.VMEM((U, BUF, BLK), F32), pltpu.VMEM((U, BUF, BLK), BF),
                pltpu.VMEM((2, NRES, BLK, BLK), BF), pltpu.VMEM((T, WAC), BF), pltpu.VMEM((T, BLK), F32),
                pltpu.VMEM((D, WAC), BF), pltpu.VMEM((NCH, dp - 1, DR, HD), BF), pltpu.VMEM((2, DR, HD), BF),
                pltpu.VMEM((NCH, wid - 1, RS, HD), BF), pltpu.VMEM((dp - 1, DR, WAC), BF),
                pltpu.VMEM((wid - 1, RS, WAC), BF),
                pltpu.VMEM((2, T, CB), BF), pltpu.VMEM((2, T, CB), BF), pltpu.VMEM((2, T, CB), F32),
                pltpu.VMEM((T, CB), BF), pltpu.VMEM((T, CB), BF),
                pltpu.VMEM((8, T), F32), pltpu.VMEM((3, 8, T), F32), pltpu.VMEM((T, BLK), F32),
                pltpu.VMEM((dp * wid, 16, CB), F32),
                DMA((9,)), DMA((2,)), DMA((2,)), DMA((NCH, dp - 1)), DMA((NCH, dp - 1)), DMA((NCH, wid - 1)),
                DMA((NCH, wid - 1)), DMA((4, dp - 1)), DMA((4, dp - 1)), DMA((4, wid - 1)), DMA((4, wid - 1)),
                DMA((2,)), DMA((2,)), DMA, DMA, DMA((3,)), DMA((3,)), DMA((dp * wid - 1,)), DMA((dp * wid - 1,)),
            ],
            compiler_params=pltpu.CompilerParams(collective_id=1, **params),
            name="backward",
        )
        oA, oF, tgrad, one, two = bwd(tokf, n1, gf, wa, qs, ks, vs, hs, hraw, beta, mgrad, res, g, hgrad, gain2)
        cut = lambda i: oA[:, i * HD : (i + 1) * HD]
        return (
            layer_out.reshape(tokens.shape), tgrad.reshape(tokens.shape), one, cut(0), cut(1), cut(2), cut(3),
            oA[:, 4 * HD : 4 * HD + heads], oF[:, :HD].T, two, oF[:, HD : HD + FL], oF[:, HD + FL : HD + 2 * FL],
            oF[:, HD + 2 * FL :].T,
        )

    rows = P(("dp", "wid"), "hid")
    cols = P("hid", ("dp", "wid"))
    wide = P(None, ("dp", "wid"), "hid")
    gain = P(None, "hid")
    return jax.shard_map(
        shards,
        mesh=mesh,
        in_specs=(
            wide, wide, P(None, ("dp", "wid"), None), P(None, ("dp", "wid")), gain, rows, rows, rows, rows, rows,
            cols, gain, rows, rows, cols,
        ),
        out_specs=(wide, wide, gain, rows, rows, rows, rows, rows, cols, gain, rows, rows, cols),
        check_vma=False,
    )
```

time: 3000 us -> 500 us (0.17)
  waiting for transfers between devices: 1990 us -> 0 us
  Pallas kernels: 0 us -> 476 us
  other arithmetic: 412 us -> 2.09 us
  matrix products: 330 us -> 0 us
  blocking collectives: 121 us -> 0 us
  local copies, waits for them, and re-layouts: 122 us -> 17.6 us
    reduce_scatter x16 -> x0, waiting for transfers between devices: 1090 us -> none  [the longest x2 152 us: reduce_grads(): lax.psum_scatter(row_terms[6].astype(jnp.bfloat16), ('dp', 'wid'), scatte...]
    all_gather x24 -> x0, waiting for transfers between devices: 696 us -> none  [the longest x2 126 us: fetch_weights(): lax.all_gather(w_down, ('dp', 'wid'), axis=1, tiled=True)]
    pallas_call x0 -> x2, Pallas kernels: none -> 476 us  [the longest x1 282 us: shards(): fwd(lengths.reshape(NB, lengths.shape[2]), keep.reshape(NB, 1, BUF), toke...]
    another operation x28 -> x0, other arithmetic: 354 us -> none  [the longest x18 354 us: path_head(): jax.scipy.linalg.solve_triangular(matrix, identity, lower=True)]
    dot_general x450 -> x0, matrix products: 320 us -> none  [the longest x18 54 us: matmul_nn(): return jnp.dot(left, right, preferred_element_type=jnp.float32)]
    while x60 -> x0, waiting for transfers between devices: 201 us -> none
    all_gather x6 -> x0, blocking collectives: 77.4 us -> none  [the longest x2 54.7 us: fetch_weights(): lax.all_gather(w_beta, ('dp', 'wid'), axis=0, tiled=True)]
    while x386 -> x0, local copies, waits for them, and re-layouts: 51.7 us -> none
  transfers between devices with their start and end apart: 50 -> 0, of which waited for: 44 -> 0; matrix products, arithmetic and copies ran while one was open for 27% -> 0% of each run, Pallas kernels for 0% -> 0%
where the time goes in v1:
time: 500 us; the launch traced here: 497 us
  Pallas kernels  476 us (95%)
  local copies, waits for them, and re-layouts  17.6 us (4%)
    pallas_call x1, Pallas kernels, shards(): fwd(lengths.reshape(NB, lengths.shape[2]), keep.reshape(NB, 1, BUF), toke...  282 us
    pallas_call x1, Pallas kernels, shards(): bwd(tokf, n1, gf, wa, qs, ks, vs, hs, hraw, beta, mgrad, res, g, hgrad, g...  194 us
    unnamed x30, local copies, waits for them, and re-layouts  11.4 us

profile of v1, /device:TPU:0, one launch (start us, length us, event | category | flops | bytes accessed | tf_op | source)
XLA Modules:
  0.0 496.7 jit_solution(12235422546157105897)
XLA Ops:
  0.7 0.8 reduce
  1.4 0.7 reduce.1
  2.1 1.3 reshape.45.keep
  3.4 0.6 maximum_convert_fusion.gains
  4.0 0.8 copy.28
  4.8 0.9 constant_dynamic-update-slice_fusion.5
  5.8 0.9 constant_dynamic-update-slice_fusion.4
  6.7 0.9 constant_dynamic-update-slice_fusion.3
  7.7 0.9 constant_dynamic-update-slice_fusion.2
  8.7 0.9 bitcast_dynamic-update-slice_fusion.1
  9.6 1.0 constant_dynamic-update-slice_fusion.1
  10.6 0.0 copy-done.4
  10.7 0.0 copy-start.1
  10.7 1.3 copy-done.1
  12.1 281.8 %forward.1 = (bf16[768,384]{1,0:T(8,128)(2,1)}, f32[768,384]{1,0:T(8,128)}, f32[8,384]{1,0:T(8,128)}, bf16[6,384,128]{2,1,0:T(8,128)(2,1)}, bf16[6,384,128]{2,1,...) custom-call(s32[2,3]{1,0:T(2,128)} %bitcast.17, ...), custom_call_target="tpu_custom_call" | custom-call | tf_op jit(solution)/shard_map/forward/pallas_call | solution.py:964
  293.8 194.3 %backward.1 = (f32[192,1664]{1,0:T(8,128)}, f32[192,3456]{1,0:T(8,128)}, bf16[768,384]{1,0:T(8,128)(2,1)}, f32[1,384]{1,0:T(1,128)}, f32[1,384]{1,0:T(1,128)}) custom-call(bf16[768,1536]{1,0:T(8,128)(2,1)} %get-tuple-element.35.tok_i, bf16[768,1536]{1,0:T(8,128)(2,1)} %get-tuple-element.36.n1_i, f32[16,1536]{1,0:T(8,128)} %get-tuple-element.37.gf, ...), custom_call_target="tpu_custom_call" | custom-call | tf_op jit(solution)/shard_map/backward/pallas_call | solution.py:993
  488.1 1.1 slice.31
  489.2 0.7 copy.29
  489.8 2.4 fusion
  492.3 1.5 slice_bitcast_fusion
  493.8 0.8 copy.42
  494.6 0.8 copy.43
  495.4 0.6 copy.44
  496.0 0.6 copy.45
  (18 shorter events, 0.1 us)
Async XLA Ops:
  0.6 10.0 %copy-start.5 = (bf16[1024,192]{0,1:T(8,128)(2,1)S(1)}, bf16[1024,192]{0,1:T(8,128)(2,1)}, u32[]{:S(2)}) copy-start(bf16[1024,192]{0,1:T(8,128)(2,1)} %param.29) | copy-start | bytes 1179652
  0.7 10.0 %copy-start.4 = (bf16[192,1024]{1,0:T(8,128)(2,1)S(1)}, bf16[192,1024]{1,0:T(8,128)(2,1)}, u32[]{:S(2)}) copy-start(bf16[192,1024]{1,0:T(8,128)(2,1)} %param.28) | copy-start | bytes 1179652
  10.7 1.3 copy-start.1
  488.1 4.2 copy-start
  492.3 1.5 copy-start.2
  492.3 2.3 copy-start.3
  493.8 1.6 copy-start.7
  493.8 2.2 copy-start.6

commit v2 on v1

v2 whole, which is shorter than its diff:
```python
import functools
import math

import jax
import jax.numpy as jnp
from jax import lax
from jax.experimental import pallas as pl
from jax.experimental.pallas import tpu as pltpu
from jax.sharding import PartitionSpec as P

BLK = 128
BUF = 384
EPSILON = 1e-06
F32 = jnp.float32
BF = jnp.bfloat16
MESH = pl.DeviceIdType.MESH
ANY = pl.BlockSpec(memory_space=pl.ANY)
VM = pl.BlockSpec(memory_space=pltpu.VMEM)
SM = pl.BlockSpec(memory_space=pltpu.SMEM)
DMA = pltpu.SemaphoreType.DMA
NRES = 30


def _dot(a,b,ca,cb): return lax.dot_general(a,b,(((ca,),(cb,)),((),())),preferred_element_type=F32)
def nn(a,b): return _dot(a.astype(BF),b.astype(BF),1,0)
def nt(a,b): return _dot(a.astype(BF),b.astype(BF),1,1)
def tn(a,b): return _dot(a.astype(BF),b.astype(BF),0,0)
def split(a):
    hi=a.astype(BF); return hi,(a-hi.astype(F32)).astype(BF)
def nn3(a,b):
    ah,al=split(a); bh,bl=split(b)
    return _dot(ah,bh,1,0)+(_dot(ah,bl,1,0)+_dot(al,bh,1,0))
INV=nn3
def iotas():
    return lax.broadcasted_iota(jnp.int32,(BLK,BLK),0), lax.broadcasted_iota(jnp.int32,(BLK,BLK),1)
def tri_inverse(inner, beta_col, row, col):
    diag=jnp.where(row==col, beta_col, 0.0)
    beta_lane=jnp.sum(diag,axis=0,keepdims=True)
    first=((row>>1)==(col>>1))&(row>col)
    x=diag-jnp.where(first, inner*beta_col*beta_lane, 0.0)
    lb=1
    while (1<<lb)<BLK:
        m=((row>>(lb+1))==(col>>(lb+1)))&((row>>lb)>(col>>lb))
        low=jnp.where(m,inner,0.0)
        x=x-INV(INV(x,low),x)
        lb+=1
    return x
def masks(a,c,e0,e1,keep_row,row,col):
    qp=row+BLK*a; kp=col+BLK*c
    segq=(qp>=e0).astype(jnp.int32)+(qp>=e1).astype(jnp.int32)
    segk=(kp>=e0).astype(jnp.int32)+(kp>=e1).astype(jnp.int32)
    ok=(segq==segk)
    if a==c: return ok&(row>=col)&((keep_row==1)|(row==col))
    return ok&(keep_row==1)
def fwd_unit(q,k,v,h,beta,keep,e0,e1):
    nb=len(q); row,col=iotas(); le=row>=col; st=row>col
    X,A1,L,W,R,Qm,Km=[],[],[],[],[],[],[]
    for a in range(nb):
        x=tri_inverse(nt(h[a],h[a]),beta[a],row,col).astype(BF)
        a1=jnp.where(le,nt(q[a],h[a]),0.0).astype(BF)
        w=jnp.where(st,nt(h[a],k[a]),0.0).astype(BF)
        l=nn(a1,x).astype(BF); r=nn(x,w).astype(BF)
        X.append(x);A1.append(a1);W.append(w);L.append(l);R.append(r)
        Qm.append((q[a].astype(F32)-nn(l,h[a])).astype(BF))
        Km.append((k[a].astype(F32)-tn(r,h[a])).astype(BF))
    scale=1.0/math.sqrt(BLK)
    S={}
    for a in range(nb):
        S[a,a]=nt(q[a],k[a])-nn(L[a],W[a])
    S[1,0]=nt(Qm[1],Km[0]); S[2,1]=nt(Qm[2],Km[1])
    u=nt(Qm[2],h[1]).astype(BF); ux=nn(u,X[1]).astype(BF)
    cq=(Qm[2].astype(F32)-nn(ux,h[1])).astype(BF)
    S[2,0]=nt(cq,Km[0])
    P={}; out=[]
    for a in range(nb):
        sc={c:jnp.where(masks(a,c,e0,e1,keep[c],row,col),S[a,c]*scale,-1e30) for c in range(a+1)}
        top=jnp.max(sc[0],axis=1,keepdims=True)
        for c in range(1,a+1): top=jnp.maximum(top,jnp.max(sc[c],axis=1,keepdims=True))
        ex={c:jnp.exp(sc[c]-top) for c in sc}
        tot=sum(jnp.sum(e,axis=1,keepdims=True) for e in ex.values())
        inv=1.0/tot
        o=0.0
        for c in sc:
            P[a,c]=(ex[c]*inv).astype(BF); o=o+nn(P[a,c],v[c])
        out.append(o)
    res=X+A1+L+W+R+Qm+Km+[u,ux,cq]+[P[0,0],P[1,0],P[1,1],P[2,0],P[2,1],P[2,2]]
    return out,res
def bwd_unit(q,k,v,h,do,res):
    nb=3; row,col=iotas(); le=row>=col; st=row>col
    X,A1,L,W,R,Qm,Km=[res[3*i:3*i+3] for i in range(7)]
    u,ux,cq=res[21:24]; pl_=res[24:30]
    P={(0,0):pl_[0],(1,0):pl_[1],(1,1):pl_[2],(2,0):pl_[3],(2,1):pl_[4],(2,2):pl_[5]}
    scale=1.0/math.sqrt(BLK)
    G={}; dv=[0.0]*nb
    for a in range(nb):
        dp={c:nt(do[a],v[c]) for c in range(a+1)}
        delta=sum(jnp.sum(P[a,c].astype(F32)*dp[c],axis=1,keepdims=True) for c in range(a+1))
        for c in range(a+1):
            G[a,c]=(P[a,c].astype(F32)*(dp[c]-delta)*scale).astype(BF)
            dv[c]=dv[c]+tn(P[a,c],do[a])
    dq=[nn(G[a,a],k[a]) for a in range(nb)]
    dk=[tn(G[a,a],q[a]) for a in range(nb)]
    dL=[-nt(G[a,a],W[a]) for a in range(nb)]
    dW=[-tn(L[a],G[a,a]) for a in range(nb)]
    dh=[0.0]*nb; dX=[0.0]*nb
    dcq=nn(G[2,0],Km[0]).astype(BF)
    dQm=[None, nn(G[1,0],Km[0]), nn(G[2,1],Km[1])+dcq.astype(F32)]
    dKm=[tn(G[1,0],Qm[1])+tn(G[2,0],cq), tn(G[2,1],Qm[2]), None]
    dux=(-nt(dcq,h[1])).astype(BF)
    dh[1]=dh[1]-tn(ux,dcq)
    du=nt(dux,X[1]).astype(BF)
    dX[1]=dX[1]+tn(u,dux)
    dQm[2]=dQm[2]+nn(du,h[1])
    dh[1]=dh[1]+tn(du,Qm[2])
    dbeta=[]
    for a in range(nb):
        if dQm[a] is not None:
            d_=dQm[a].astype(BF)
            dq[a]=dq[a]+d_.astype(F32); dL[a]=dL[a]-nt(d_,h[a]); dh[a]=dh[a]-tn(L[a],d_)
        if dKm[a] is not None:
            d_=dKm[a].astype(BF)
            dk[a]=dk[a]+d_.astype(F32); dR=(-nt(h[a],d_)).astype(BF); dh[a]=dh[a]-nn(R[a],d_)
            dX[a]=dX[a]+nt(dR,W[a]); dW[a]=dW[a]+tn(X[a],dR)
        dl=dL[a].astype(BF)
        dA=jnp.where(le,nt(dl,X[a]),0.0).astype(BF)
        dX[a]=dX[a]+tn(A1[a],dl)
        dw=jnp.where(st,dW[a],0.0).astype(BF)
        dh[a]=dh[a]+nn(dw,k[a]); dk[a]=dk[a]+tn(dw,h[a])
        dq[a]=dq[a]+nn(dA,h[a]); dh[a]=dh[a]+tn(dA,q[a])
        dM=nt(tn(X[a],dX[a]),X[a])
        dn=jnp.where(st,-dM,0.0).astype(BF)
        dh[a]=dh[a]+nn(dn,h[a])+tn(dn,h[a])
        dbeta.append(jnp.sum(jnp.where(row==col,dM,0.0),axis=1,keepdims=True))
    return dq,dk,dv,dh,dbeta


def spans(rows, step):
    return pl.ds(pl.multiple_of(rows, step), step)


class Place:
    def __init__(self, names, sizes):
        self.names, self.sizes = names, sizes
        self.d, self.h, self.w = (lax.axis_index(n) for n in ("dp", "hid", "wid"))
        self.dp, self.wid = sizes["dp"], sizes["wid"]
        self.c = lax.rem(self.h, 2)
        self.x = lax.div(self.h, 2)
        self.sib = self.at(h=self.h + 1 - 2 * self.c)
        self.xpeer = self.at(h=lax.rem(self.h + 2, 4))

    def at(self, d=None, h=None, w=None):
        where = {"dp": self.d if d is None else d, "hid": self.h if h is None else h, "wid": self.w if w is None else w}
        return tuple(where[n] for n in self.names)

    def greet(self, peers):
        barrier = pltpu.get_barrier_semaphore()
        for peer in peers:
            pl.semaphore_signal(barrier, inc=1, device_id=peer, device_id_type=MESH)
        pl.semaphore_wait(barrier, len(peers))

    def dp_peer(self, j):
        return self.at(d=lax.rem(self.d + j, self.dp))

    def wid_peer(self, k):
        return self.at(w=lax.rem(self.w + k, self.wid))

    def hid_peer(self, k):
        return self.at(h=lax.rem(self.h + k, 4))

    def group(self):
        return [
            self.at(d=lax.rem(self.d + i, self.dp), w=lax.rem(self.w + k, self.wid))
            for i in range(self.dp)
            for k in range(self.wid)
            if i + k > 0
        ]


def send(src, dst, sent, got, peer):
    return pltpu.make_async_remote_copy(
        src_ref=src, dst_ref=dst, send_sem=sent, recv_sem=got, device_id=peer, device_id_type=MESH
    )


class Gather:
    def __init__(self, me, rows, full, col, width, ch, sz, rz, sy, ry):
        self.me, self.rows, self.full, self.ch = me, rows, full, ch
        self.col, self.width = col, width
        self.sz, self.rz, self.sy, self.ry = sz, rz, sy, ry

    def piece(self, d, o):
        return self.full.at[
            pl.ds(pl.multiple_of((d * self.me.wid + o) * self.rows, 16), self.rows), pl.ds(self.col, self.width)
        ]

    def origin(self, way, hop):
        return lax.clamp(0, self.me.w - way * hop, self.me.wid - 1)

    def zcopy(self, way, hop, sem):
        me, side = self.me, (way + 1) // 2
        part = self.piece(me.d, self.origin(way, hop))
        return send(
            part, part, self.sz.at[self.ch, side, sem], self.rz.at[self.ch, side, sem],
            me.at(w=lax.clamp(0, me.w + way, me.wid - 1)),
        )

    def ycopy(self, d, o, j):
        part = self.piece(d, o)
        return send(part, part, self.sy.at[self.ch, o, j - 1], self.ry.at[self.ch, o, j - 1], self.me.dp_peer(j))

    def has_next(self, way):
        return self.me.w < self.me.wid - 1 if way == 1 else self.me.w > 0

    def has_piece(self, way, hop):
        return self.me.w - hop >= 0 if way == 1 else self.me.w + hop < self.me.wid

    def start_z(self):
        for way in (1, -1):

            @pl.when(self.has_next(way))
            def _():
                self.zcopy(way, 0, 0).start()

    def start_y(self):
        for j in range(1, self.me.dp):
            self.ycopy(self.me.d, self.me.w, j).start()

    def hop(self, hop):
        me = self.me
        for way in (1, -1):

            @pl.when(self.has_piece(way, hop))
            def _():
                self.zcopy(way, hop, hop - 1).wait_recv()

                @pl.when(self.has_next(way))
                def _():
                    self.zcopy(way, hop, hop).start()

                for j in range(1, me.dp):
                    self.ycopy(me.d, self.origin(way, hop), j).start()

    def finish(self):
        me = self.me
        for j in range(1, me.dp):
            for o in range(me.wid):
                self.ycopy(lax.rem(me.d + me.dp - j, me.dp), o, j).wait_recv()

    def drain(self):
        me = self.me
        for way in (1, -1):
            for hop in range(me.wid):

                @pl.when(self.has_piece(way, hop) & self.has_next(way))
                def _():
                    self.zcopy(way, hop, hop).wait_send()

        for j in range(1, me.dp):
            for o in range(me.wid):
                self.ycopy(me.d, o, j).wait_send()


def column(values, lane_index):
    lanes = lax.broadcasted_iota(jnp.int32, values.shape, 1)
    return jnp.sum(jnp.where(lanes == lane_index, values, 0.0), axis=1, keepdims=True)


def layer_kernel(
    cfg, lens, keep, tok, cot, gains, w_q, w_k, w_v, w_h, w_b, w_o, w_g, w_u, w_d,
    layer_out, tgrad, one, two, o_q, o_k, o_v, o_h, o_b, o_o, o_g, o_u, o_d, g_h, ry_h, z_h, res_h,
    W, tokf, cotf, n1, n2, hlow, ng, mix, act, gg, ug, qs, ks, vs, hs, hraw, mgrad, beta, dbeta, dB, gf, resb,
    s1, r1, s2, r2, acc, t2, q2, hidown, hgrad, stage, outv, rts, rtr, rt, gbuf,
    local, own, hx_s, hx_r, sz, rz, sy, ry, s1s, s1r, s2s, s2r, s3s, s3r, ress, stages,
    ys, yr, zs, zr, zo, ld, outs, rs_s, rs_r, gs_s, gs_r,
):
    me = Place(cfg["names"], cfg["sizes"])
    T, D, CB, HL, HD, FL, RS = (cfg[k] for k in ("T", "D", "CB", "HL", "HD", "FL", "RS"))
    FW = cfg["FW"]
    NF = 3 * FL // FW
    FB = 5 * HD
    BC = FB + 3 * FL
    GC, UC, DC, OC = FB, FB + FL, FB + 2 * FL, 4 * HD
    NB, U, DR = T // BUF, T // BUF * HL, RS * me.wid
    c = me.c
    own_cols = pl.ds(pl.multiple_of(me.h * CB, BLK), CB)
    own_rows = pl.ds(pl.multiple_of((me.d * me.wid + me.w) * RS, 16), RS)
    me.greet(me.group() + [me.hid_peer(k) for k in range(1, 4)])

    places = [(w_q, 0), (w_k, HD), (w_v, 2 * HD), (w_h, 3 * HD), (w_b, BC), (w_o, OC), (w_g, GC), (w_u, UC), (w_d, DC)]
    mine = [
        pltpu.make_async_copy(ref, W.at[own_rows, pl.ds(col, ref.shape[1])], own.at[i])
        for i, (ref, col) in enumerate(places)
    ]
    hid = []
    for i, (src, dst) in enumerate(((tok, tokf), (gains, gf), (cot, cotf))):
        here = pltpu.make_async_copy(src, dst.at[:, own_cols], local.at[i])
        away = [
            send(src, dst.at[:, own_cols], hx_s.at[i, k - 1], hx_r.at[i, k - 1], me.hid_peer(k)) for k in range(1, 4)
        ]
        hid.append([here] + away)
    for copy in mine[:6]:
        copy.start()
    for i in range(2):
        for copy in hid[i]:
            copy.start()
    for copy in mine[6:]:
        copy.start()
    sems = (sz, rz, sy, ry)
    first = [
        Gather(me, RS, W, col, ref.shape[1], i, *sems) for i, (ref, col) in enumerate(places[:6])
    ]

    def late(i):
        return Gather(me, RS, W, pl.multiple_of(FB + i * FW, BLK), FW, 6 + i, *sems)

    for i, g in enumerate(first):
        mine[i].wait()
        g.start_z()
        g.start_y()
    for copy in mine[6:]:
        copy.wait()

    def start_late(i, carry):
        late(i).start_z()
        late(i).start_y()
        return carry

    lax.fori_loop(0, NF, start_late, 0)
    for copy in hid[2]:
        copy.start()
    for i in range(2):
        for copy in hid[i]:
            copy.wait()
    RB = 32

    def rows_of(m):
        return pl.ds(pl.multiple_of(m * BUF, BLK), BUF)

    def norm(src, dst, gain, base):
        def body(i, carry):
            rows = spans(base + i * RB, RB)
            wide = src[rows, :].astype(F32)
            scale = lax.rsqrt(jnp.mean(wide * wide, axis=1, keepdims=True) + EPSILON)
            dst[rows, :] = (wide * scale * gf[gain : gain + 1, :]).astype(BF)
            return carry

        lax.fori_loop(0, BUF // RB, body, 0)

    for m in range(NB):
        norm(tokf, n1, 0, m * BUF)

    def project(a):
        for m in range(NB):
            rows = n1[m * BUF : (m + 1) * BUF, :]
            made = nn(rows, W[:, a * HD : (a + 1) * HD])
            for hd in range(HL):
                part = made[:, hd * BLK : (hd + 1) * BLK]
                u = m * HL + hd
                if a < 3:
                    (qs, ks, vs)[a][u] = part.astype(BF)
                else:
                    hraw[u] = part
                    hs[u] = (part * lax.rsqrt(jnp.sum(part * part, axis=1, keepdims=True) + EPSILON)).astype(BF)
            if a == 3:
                beta[m * BUF : (m + 1) * BUF, :] = 2.0 * jax.nn.sigmoid(nn(rows, W[:, BC:]))

    def tick(k):
        for hop in range(1, me.wid):
            if 0 <= k - hop + 1 < len(first):
                first[k - hop + 1].hop(hop)

    for k in range(len(first) + me.wid - 2):
        tick(k)
        if 2 <= k < 5:
            first[k - 2].finish()
            project(k - 2)
    first[3].finish()
    first[4].finish()
    project(3)

    def late_tick(k):
        for hop in range(1, me.wid):

            @pl.when((k >= hop - 1) & (k - hop + 1 < NF))
            def _():
                late(k - hop + 1).hop(hop)

    def attend(u, carry):
        m, hd = lax.div(u, HL), lax.rem(u, HL)
        slot = lax.rem(u, 2)
        e0 = lens[m, 0]
        e1 = e0 + lens[m, 1]
        parts = [slice(a * BLK, (a + 1) * BLK) for a in range(3)]
        strength = [column(beta[spans(m * BUF + a * BLK, BLK), :], hd) for a in range(3)]
        keys = [keep[m, :, p] for p in parts]
        late_tick(u)
        out, res = fwd_unit(
            [qs[u, p, :] for p in parts], [ks[u, p, :] for p in parts], [vs[u, p, :] for p in parts],
            [hs[u, p, :] for p in parts], strength, keys, e0, e1,
        )
        for a in range(3):
            mix[spans(m * BUF + a * BLK, BLK), pl.ds(pl.multiple_of(hd * BLK, BLK), BLK)] = out[a].astype(BF)

        @pl.when(u >= 2)
        def _():
            pltpu.make_async_copy(resb.at[slot], res_h.at[u], ress.at[slot]).wait()

        for i, value in enumerate(res):
            resb[slot, i] = value
        pltpu.make_async_copy(resb.at[slot], res_h.at[u], ress.at[slot]).start()
        return carry

    lax.fori_loop(0, U, attend, 0)
    for slot in range(2):
        pltpu.make_async_copy(resb.at[slot], res_h.at[0], ress.at[slot]).wait()

    def block(b):
        return pl.ds(pl.multiple_of(b * CB, BLK), CB)

    def hop1(tag, m, j):
        return send(s1.at[m, j], r1.at[tag % 3 // 2, m, j], s1s.at[tag, m, j], s1r.at[tag, m, j], me.sib)

    def hop2(tag, m, j):
        return send(s2.at[m, j], r2.at[tag, m, j], s2s.at[tag, m, j], s2r.at[tag, m, j], me.xpeer)

    def first_hop(tag, m, partial):
        for j in range(2):
            s1[m, j] = partial((1 - c) + 2 * j).astype(BF)
            hop1(tag, m, j).start()
        for j in range(2):
            acc[m, j] = partial(c + 2 * j)

    def second_hop(tag, m):
        for j in range(2):
            hop1(tag, m, j).wait()
            s2[m, j] = (acc[m, j] + r1[tag // 2, m, j].astype(F32)).astype(BF)
            hop2(tag, m, j).start()

    def total(tag, m, j):
        return s2[m, j].astype(F32) + r2[tag, m, j].astype(F32)

    def third(tag, full, m, j, core):
        part = full.at[rows_of(m), block(core + 2 * j)]
        return send(part, part, s3s.at[tag, m, j], s3r.at[tag, m, j], me.sib)

    def wait_third(tag, full, m):
        for j in range(2):
            third(tag, full, m, j, 1 - c).wait_recv()
            third(tag, full, m, j, c).wait_send()

    def branch(m):
        return lambda b: nt(mix[rows_of(m), :], W[block(b), OC : OC + HD])

    first[5].finish()
    for m in range(NB):
        first_hop(0, m, branch(m))

    def more(k, carry):
        late_tick(k)
        return carry

    lax.fori_loop(U, NF + me.wid - 2, more, 0)
    for m in range(NB):
        second_hop(0, m)

    def residual(m):
        for j in range(2):
            hop2(0, m, j).wait()
            b = c + 2 * j
            hidden = tokf[rows_of(m), block(b)].astype(F32) + total(0, m, j)
            hlow[rows_of(m), block(b)] = hidden.astype(BF)
            third(0, hlow, m, j, c).start()
        hidown[rows_of(m), :] = tokf[rows_of(m), own_cols].astype(F32) + (
            s2[m, me.x].astype(F32) + r2[0, m, me.x].astype(F32)
        )

    for m in range(NB):
        residual(m)
    for m in range(NB):
        wait_third(0, hlow, m)
        norm(hlow, n2, 8, m * BUF)
    for copy in hid[2]:
        copy.wait()

    def finish_late(i, carry):
        late(i).finish()
        return carry

    NT = 256
    ND = 2 * FL // FW
    lax.fori_loop(0, ND, finish_late, 0)

    def ffn(m):
        def body(n, carry):
            at = pl.multiple_of(n * NT, NT)
            gate = nn(n2[rows_of(m), :], W[:, pl.ds(pl.multiple_of(GC + at, BLK), NT)])
            up = nn(n2[rows_of(m), :], W[:, pl.ds(pl.multiple_of(UC + at, BLK), NT)])
            sig = jax.nn.sigmoid(gate)
            silu = gate * sig
            cols = pl.ds(at, NT)
            act[rows_of(m), cols] = (silu * up).astype(BF)
            gg[rows_of(m), cols] = (up * sig * (1.0 + gate * (1.0 - sig))).astype(BF)
            ug[rows_of(m), cols] = silu.astype(BF)
            return carry

        lax.fori_loop(0, FL // NT, body, 0)

    def ffn_back(m):
        def body(n, carry):
            at = pl.multiple_of(n * NT, NT)
            cols = pl.ds(at, NT)
            back = nn(cotf[rows_of(m), :], W[:, pl.ds(pl.multiple_of(DC + at, BLK), NT)])
            gg[rows_of(m), cols] = (back * gg[rows_of(m), cols].astype(F32)).astype(BF)
            ug[rows_of(m), cols] = (back * ug[rows_of(m), cols].astype(F32)).astype(BF)
            return carry

        lax.fori_loop(0, FL // NT, body, 0)

    def dp_rows(j):
        return pl.ds(pl.multiple_of(lax.rem(me.d + j, me.dp) * DR, 16), DR)

    def staged(side, i, col, width):
        return pltpu.make_async_copy(
            stage.at[side, i, :, pl.ds(0, width)],
            g_h.at[pl.ds(pl.multiple_of(i * CB, BLK), CB), pl.ds(col, width)],
            stages.at[side, i],
        )

    def rs_y(ch, col, width, j):
        return send(
            g_h.at[dp_rows(j), pl.ds(col, width)], ry_h.at[j - 1, :, pl.ds(col, width)],
            ys.at[ch, j - 1], yr.at[ch, j - 1], me.dp_peer(j),
        )

    pending = []
    made_terms = [0]

    def flush():
        side, ch, col, width = pending.pop()
        for i in range(D // CB):
            staged(side, i, col, width).wait()
        for j in range(1, me.dp):
            rs_y(ch, col, width, j).start()

    def weight_term(ch, left, right, at, col, width):
        side = made_terms[0] % 2
        made_terms[0] += 1

        def body(i, carry):
            stage[side, i, :, pl.ds(0, width)] = tn(
                left[:, pl.ds(pl.multiple_of(i * CB, BLK), CB)], right[:, at : at + width]
            ).astype(BF)
            staged(side, i, col, width).start()
            return carry

        lax.fori_loop(0, D // CB, body, 0)
        if pending:
            flush()
        pending.append((side, ch, col, width))

    def ffn_terms(left, right, col):
        for n in range(FL // FW):
            weight_term(6 + (col - FB) // FW + n, left, right, n * FW, col + n * FW, FW)

    for m in range(NB):
        ffn(m)
    ffn_terms(cotf, act, DC)
    flush()
    lax.fori_loop(ND, NF, finish_late, 0)

    def normed_back(m):
        return lambda b: nt(gg[rows_of(m), :], W[block(b), GC : GC + FL]) + nt(
            ug[rows_of(m), :], W[block(b), UC : UC + FL]
        )

    def down(m):
        return lambda b: nt(act[rows_of(m), :], W[block(b), DC : DC + FL])

    ffn_back(0)
    first_hop(1, 0, normed_back(0))
    ffn_back(1)
    second_hop(1, 0)
    for m in range(1, NB):
        first_hop(1, m, normed_back(m))
        if m + 1 < NB:
            ffn_back(m + 1)
        second_hop(1, m)
    for g in first:
        g.drain()

    def drain_late(i, carry):
        late(i).drain()
        return carry

    lax.fori_loop(0, NF, drain_late, 0)
    ffn_terms(n2, gg, GC)
    ffn_terms(n2, ug, UC)
    flush()

    def hop2_out(m):
        return send(t2.at[m], q2.at[m], s2s.at[2, m, 0], s2r.at[2, m, 0], me.xpeer)

    for m in range(NB):
        first_hop(2, m, down(m))
    other = 1 - me.x
    for m in range(NB):
        for j in range(2):
            hop1(2, m, j).wait()
        t2[m] = (acc[m, other] + r1[1, m, other].astype(F32)).astype(BF)
        hop2_out(m).start()

    gm = W.at[0:DR, FB : FB + FW]
    peer_term = W.at[DR : 2 * DR, FB : FB + FW]
    loaded = W.at[DR : 2 * DR, FB + FW : FB + 2 * FW]

    def to_wid(slot):
        return W.at[0:DR, pl.ds(pl.multiple_of(FB + FW + slot * FW, BLK), FW)]

    def wid_rows(k):
        return pl.ds(pl.multiple_of(lax.rem(me.w + k, me.wid) * RS, 16), RS)

    def rs_z(ch, col, width, slot, k):
        return send(
            to_wid(slot).at[wid_rows(k), pl.ds(0, width)], z_h.at[k, :, pl.ds(col, width)],
            zs.at[ch, k - 1], zr.at[ch, k - 1], me.wid_peer(k),
        )

    def rs_own(ch, col, width, slot):
        return pltpu.make_async_copy(
            to_wid(slot).at[wid_rows(0), pl.ds(0, width)], z_h.at[0, :, pl.ds(col, width)], zo.at[ch]
        )

    def rs_free(ch, col, width, slot):
        for k in range(1, me.wid):
            rs_z(ch, col, width, slot, k).wait_send()

    def rs_stage(ch, col, width, slot):
        here = pltpu.make_async_copy(g_h.at[dp_rows(0), pl.ds(col, width)], gm.at[:, pl.ds(0, width)], ld.at[0])
        here.start()
        for j in range(1, me.dp):
            rs_y(ch, col, width, j).wait_recv()
            there = pltpu.make_async_copy(
                ry_h.at[j - 1, :, pl.ds(col, width)], peer_term.at[:, pl.ds(0, width)], ld.at[1]
            )
            there.start()
            if j == 1:
                here.wait()
            there.wait()
            for k in range(me.wid):
                rows = wid_rows(k)
                so_far = gm if j == 1 else to_wid(slot)
                to_wid(slot)[rows, 0:width] = (
                    so_far[rows, 0:width].astype(F32) + peer_term[rows, 0:width].astype(F32)
                ).astype(BF)
                if j == me.dp - 1:
                    if k > 0:
                        rs_z(ch, col, width, slot, k).start()
                    else:
                        rs_own(ch, col, width, slot).start()
        rs_own(ch, col, width, slot).wait()

    def rs_late(i):
        f = lax.rem(i + ND, NF)
        return 6 + f, pl.multiple_of(FB + f * FW, BLK), FW

    def rs_sum(ch, col, width, out, at, side, busy):
        for k in range(1, me.wid):
            rs_z(ch, col, width, 0, k).wait_recv()
        loads = [
            pltpu.make_async_copy(
                z_h.at[k, :, pl.ds(col, width)], loaded.at[pl.ds(k * RS, RS), pl.ds(0, width)], ld.at[2 + k]
            )
            for k in range(me.wid)
        ]
        for copy in loads:
            copy.start()
        if busy is not None:
            busy.wait()
        for copy in loads:
            copy.wait()
        done = loaded[0:RS, 0:width].astype(F32)
        for k in range(1, me.wid):
            done = done + loaded[k * RS : (k + 1) * RS, 0:width].astype(F32)
        outv[side, :, 0:width] = done
        copy = pltpu.make_async_copy(outv.at[side, :, pl.ds(0, width)], out.at[:, pl.ds(at, width)], outs.at[side])
        copy.start()
        return copy

    def spread_back(m):
        for j in range(2):
            hop2(1, m, j).wait()
            ng[rows_of(m), block(c + 2 * j)] = total(1, m, j).astype(BF)
            third(1, ng, m, j, c).start()

    def branch_back(m):
        def body(i, carry):
            rows = spans(m * BUF + i * RB, RB)
            low = hlow[rows, :].astype(F32)
            scale = lax.rsqrt(jnp.mean(low * low, axis=1, keepdims=True) + EPSILON)
            scaled = ng[rows, :].astype(F32) * gf[8:9, :]
            row_total = jnp.sum(low * scaled, axis=1, keepdims=True)
            cube = scale * scale * scale * row_total / D
            low_own = hlow[rows, own_cols].astype(F32)
            ng_own = ng[rows, own_cols].astype(F32)
            hgrad[rows, :] = (
                cotf[rows, own_cols].astype(F32) + scale * gf[8:9, own_cols] * ng_own - low_own * cube
            )
            gbuf[slot_here, 8:16, :] += jnp.broadcast_to(
                jnp.sum(low_own * scale * ng_own, axis=0, keepdims=True), (8, CB)
            )
            ng[rows, :] = (cotf[rows, :].astype(F32) + scale * scaled - low * cube).astype(BF)
            return carry

        lax.fori_loop(0, BUF // RB, body, 0)
        made = nn(ng[rows_of(m), :], W[:, OC : OC + HD])
        for hd in range(HL):
            mgrad[m * HL + hd] = made[:, hd * BLK : (hd + 1) * BLK].astype(BF)

    slot_here = me.d * me.wid + me.w
    gbuf[slot_here] = jnp.zeros((16, CB), F32)
    dbeta[...] = jnp.zeros_like(dbeta)
    dA = n2

    def fetch_res(u):
        slot = lax.rem(u, 2)
        return pltpu.make_async_copy(res_h.at[u], resb.at[slot], ress.at[slot])

    fetch_res(0).start()

    def attend_back(u, carry):
        m, hd = lax.div(u, HL), lax.rem(u, HL)
        slot = lax.rem(u, 2)
        parts = [slice(a * BLK, (a + 1) * BLK) for a in range(3)]

        @pl.when(hd == 0)
        def _():
            spread_back(m)
            wait_third(1, ng, m)
            branch_back(m)

        fetch_res(u).wait()

        @pl.when(u + 1 < U)
        def _():
            fetch_res(u + 1).start()

        dq, dk, dv, dh, db = bwd_unit(
            [qs[u, p, :] for p in parts], [ks[u, p, :] for p in parts], [vs[u, p, :] for p in parts],
            [hs[u, p, :] for p in parts], [mgrad[u, p, :] for p in parts], [resb[slot, i] for i in range(NRES)],
        )
        for a in range(3):
            rows = spans(m * BUF + a * BLK, BLK)
            for n, value in enumerate((dq[a], dk[a], dv[a])):
                dA[rows, pl.ds(pl.multiple_of(n * HD + hd * BLK, BLK), BLK)] = value.astype(BF)
            raw = hraw[u, parts[a], :]
            scale = lax.rsqrt(jnp.sum(raw * raw, axis=1, keepdims=True) + EPSILON)
            along = jnp.sum(raw * dh[a], axis=1, keepdims=True)
            dA[rows, pl.ds(pl.multiple_of(3 * HD + hd * BLK, BLK), BLK)] = (
                scale * dh[a] - raw * (scale * scale * scale * along)
            ).astype(BF)
            strength = column(beta[rows, :], hd)
            pull = db[a] * (1.0 / jnp.maximum(strength, 1e-30) - 0.5)
            lanes = lax.broadcasted_iota(jnp.int32, (BLK, BLK), 1)
            dbeta[rows, :] += jnp.where(lanes == hd, pull, 0.0)

        @pl.when((u >= 1) & (u <= NF))
        def _():
            i = u - 1
            slot = lax.rem(i, 4)

            @pl.when(i >= 4)
            def _():
                rs_free(*rs_late(i - 4), slot)

            rs_stage(*rs_late(i), slot)

        return carry

    lax.fori_loop(0, U, attend_back, 0)
    dB[...] = dbeta[...].astype(BF)
    statics = {5: (5, OC, HD), 0: (0, 0, HD), 1: (1, HD, HD), 2: (2, 2 * HD, HD), 3: (3, 3 * HD, HD), 4: (4, BC, BLK)}
    weight_term(5, ng, mix, 0, OC, HD)
    for a in range(4):
        weight_term(a, n1, dA, a * HD, a * HD, HD)
    weight_term(4, n1, dB, 0, BC, BLK)
    flush()

    rt[...] = jnp.zeros_like(rt)

    def first_back(m):
        def partial(b):
            made = nt(dA[rows_of(m), :], W[block(b), 0 : 4 * HD]) + nt(dB[rows_of(m), :], W[block(b), BC:])
            along = jnp.sum(made * tokf[rows_of(m), block(b)].astype(F32) * gf[0:1, block(b)], axis=1, keepdims=True)
            rt[rows_of(m), :] += jnp.broadcast_to(along, (BUF, BLK))
            return made

        return partial

    for m in range(NB):
        hop2_out(m).wait()
        layer_out[rows_of(m), :] = (
            hidown[rows_of(m), :] + (acc[m, me.x] + r1[1, m, me.x].astype(F32) + q2[m].astype(F32))
        ).astype(BF)
    for m in range(NB):
        first_hop(3, m, first_back(m))
    for i in range(T // BLK):
        rts[:, i * BLK : (i + 1) * BLK] = rt[i * BLK : (i + 1) * BLK, :].T[0:8, :]
    rt_copies = [send(rts, rtr.at[k - 1], rs_s.at[k - 1], rs_r.at[k - 1], me.hid_peer(k)) for k in range(1, 4)]
    for copy in rt_copies:
        copy.start()

    def hop2_in(m):
        return send(t2.at[m], r2.at[0, m, 0], s2s.at[3, m, 0], s2r.at[3, m, 0], me.xpeer)

    for m in range(NB):
        for j in range(2):
            hop1(3, m, j).wait()
        t2[m] = (acc[m, other] + r1[0, m, other].astype(F32)).astype(BF)
        hop2_in(m).start()

    done = min(max(U - 1, 0), NF)
    order = [(6 + (i + ND) % NF, FB + (i + ND) % NF * FW, FW) for i in range(NF)]
    order += [statics[k] for k in (5, 0, 1, 2, 3, 4)]

    def target(ch, col):
        if ch < 6:
            return (o_q, o_k, o_v, o_h, o_b, o_o)[ch], 0
        return (o_g, o_u, o_d)[(col - FB) // FL], (col - FB) % FL

    writing = [None, None]
    summed = [0]
    freed = [max(done - 4, 0)]

    def take(n):
        if n >= 4 and freed[0] == n - 4:
            rs_free(*order[n - 4], (n - 4) % 4)
            freed[0] += 1
        rs_stage(*order[n], n % 4)

    def give():
        n = summed[0]
        side = n % 2
        ch, col, width = order[n]
        out, at = target(ch, col)
        writing[side] = rs_sum(ch, col, width, out, at, side, writing[side])
        summed[0] += 1

    for n in range(done, NF + 1):
        take(n)
    give()
    give()
    for m in range(NB):
        hop2_in(m).wait()
    for copy in rt_copies:
        copy.wait()

    def token_rows(i, carry):
        rows = spans(i * BLK, BLK)
        m = lax.div(i, BUF // BLK)
        part = spans(lax.rem(i, BUF // BLK) * BLK, BLK)
        lane = rts[0:1, rows] + rtr[0, 0:1, rows] + rtr[1, 0:1, rows] + rtr[2, 0:1, rows]
        row_total = jnp.broadcast_to(lane, (BLK, BLK)).T[:, 0:1]
        wide = tokf[rows, :].astype(F32)
        scale = lax.rsqrt(jnp.mean(wide * wide, axis=1, keepdims=True) + EPSILON)
        made = acc[m, me.x, part, :] + r1[0, m, me.x, part, :].astype(F32) + r2[0, m, 0, part, :].astype(F32)
        own_tok = tokf[rows, own_cols].astype(F32)
        back = scale * gf[0:1, own_cols] * made - own_tok * (scale * scale * scale * row_total / D)
        tgrad[rows, :] = (hgrad[rows, :] + back).astype(BF)
        gbuf[slot_here, 0:8, :] += jnp.broadcast_to(jnp.sum(own_tok * scale * made, axis=0, keepdims=True), (8, CB))
        return carry

    lax.fori_loop(0, T // BLK, token_rows, 0)
    gain_copies = []
    for n, peer in enumerate(me.group()):
        copy = send(gbuf.at[slot_here], gbuf.at[slot_here], gs_s.at[n], gs_r.at[n], peer)
        copy.start()
        gain_copies.append(copy)
    for n in range(NF + 1, len(order)):
        take(n)
        give()
    for copy in gain_copies:
        copy.wait()
    both = gbuf[0]
    for n in range(1, me.dp * me.wid):
        both = both + gbuf[n]
    one[...] = both[0:1, :]
    two[...] = both[8:9, :]
    while summed[0] < len(order):
        give()
    for n in range(freed[0], len(order)):
        rs_free(*order[n], n % 4)
    for ch, col, width in order:
        for j in range(1, me.dp):
            rs_y(ch, col, width, j).wait_send()
    for copy in writing:
        copy.wait()


def solution(mesh):
    names = tuple(mesh.axis_names)
    sizes = {n: mesh.shape[n] for n in names}
    dp, wid = sizes["dp"], sizes["wid"]
    assert sizes["hid"] == 4

    def shards(
        tokens, cotangent, lengths, keep, norm_one, w_query, w_key, w_value, w_house, w_beta, w_out, norm_two,
        w_gate, w_up, w_down,
    ):
        micro, rows, CB = tokens.shape
        T, D, HD, FL, RS = micro * rows, CB * 4, w_query.shape[1], w_gate.shape[1], w_query.shape[0]
        HL, NB, FW = HD // BLK, T // BUF, 512
        U, NF, DR = NB * HL, 3 * FL // FW, D // dp
        CT = 5 * HD + 3 * FL + BLK
        heads = w_beta.shape[1]
        cfg = dict(names=names, sizes=sizes, T=T, D=D, CB=CB, HL=HL, HD=HD, FL=FL, RS=RS, FW=FW)
        gains = jnp.concatenate([jnp.broadcast_to(g, (8, CB)) for g in (norm_one, norm_two)], axis=0).astype(F32)
        sd = jax.ShapeDtypeStruct
        nch = 6 + NF
        vm = pltpu.VMEM
        unit = lambda t: vm((U, BUF, BLK), t)
        pair = vm((NB, 2, BUF, CB), BF)
        outs = pl.pallas_call(
            functools.partial(layer_kernel, cfg),
            out_shape=(
                sd((T, CB), BF), sd((T, CB), BF), sd((1, CB), F32), sd((1, CB), F32),
                *[sd((RS, HD), F32)] * 4, sd((RS, BLK), F32), sd((RS, HD), F32), *[sd((RS, FL), F32)] * 3,
                sd((D, CT), BF), sd((dp - 1, DR, CT), BF), sd((wid, RS, CT), BF), sd((U, NRES, BLK, BLK), BF),
            ),
            in_specs=[SM, VM] + [ANY] * 12,
            out_specs=(VM,) * 4 + (ANY,) * 13,
            scratch_shapes=[
                vm((D, CT), BF), *[vm((T, D), BF)] * 6, vm((T, HD), BF), *[vm((T, FL), BF)] * 3,
                *[unit(BF)] * 4, unit(F32), unit(BF), vm((T, BLK), F32), vm((T, BLK), F32), vm((T, BLK), BF),
                vm((16, D), F32), vm((2, NRES, BLK, BLK), BF),
                pair, vm((2, NB, 2, BUF, CB), BF), pair, vm((2, NB, 2, BUF, CB), BF), vm((NB, 2, BUF, CB), F32),
                vm((NB, BUF, CB), BF), vm((NB, BUF, CB), BF), vm((T, CB), F32), vm((T, CB), F32),
                vm((2, 4, CB, FW), BF), vm((2, RS, FW), F32),
                vm((8, T), F32), vm((3, 8, T), F32), vm((T, BLK), F32), vm((dp * wid, 16, CB), F32),
                DMA((3,)), DMA((9,)), DMA((3, 3)), DMA((3, 3)), DMA((nch, 2, wid)), DMA((nch, 2, wid)),
                DMA((nch, wid, dp - 1)), DMA((nch, wid, dp - 1)),
                *[DMA((4, NB, 2))] * 4, *[DMA((2, NB, 2))] * 2, DMA((2,)), DMA((2, 4)),
                DMA((nch, dp - 1)), DMA((nch, dp - 1)), DMA((nch, wid - 1)), DMA((nch, wid - 1)), DMA((nch,)),
                DMA((2 + wid,)), DMA((2,)), DMA((3,)), DMA((3,)), DMA((dp * wid - 1,)), DMA((dp * wid - 1,)),
            ],
            compiler_params=pltpu.CompilerParams(
                collective_id=0, has_side_effects=True, vmem_limit_bytes=cfg.get("limit", 63 << 20)
            ),
            name="layer",
        )(
            lengths.reshape(NB, lengths.shape[2]), keep.reshape(NB, 1, BUF), tokens.reshape(T, CB),
            cotangent.reshape(T, CB), gains, w_query, w_key, w_value, w_house,
            jnp.pad(w_beta, ((0, 0), (0, BLK - heads))), w_out.T, w_gate, w_up, w_down.T,
        )
        layer_out, tgrad, one, two, gq, gk, gv, gh, gb, go, g_gate, g_up, g_down = outs[:13]
        return (
            layer_out.reshape(tokens.shape), tgrad.reshape(tokens.shape), one, gq, gk, gv, gh, gb[:, :heads],
            go.T, two, g_gate, g_up, g_down.T,
        )

    rows = P(("dp", "wid"), "hid")
    cols = P("hid", ("dp", "wid"))
    wide = P(None, ("dp", "wid"), "hid")
    gain = P(None, "hid")
    return jax.shard_map(
        shards,
        mesh=mesh,
        in_specs=(
            wide, wide, P(None, ("dp", "wid"), None), P(None, ("dp", "wid")), gain, rows, rows, rows, rows, rows,
            cols, gain, rows, rows, cols,
        ),
        out_specs=(wide, wide, gain, rows, rows, rows, rows, rows, cols, gain, rows, rows, cols),
        check_vma=False,
    )
```

time: 500 us -> 448 us (0.90)
  Pallas kernels: 476 us -> 415 us
  local copies, waits for them, and re-layouts: 17.6 us -> 24.2 us
    pallas_call x2 -> x1, Pallas kernels: 476 us -> 415 us  [shards(): pl.pallas_call(functools.partial(layer_kernel, cfg), out_shape=(sd((T, CB...]
    unnamed x30 -> x16, local copies, waits for them, and re-layouts: 11.4 us -> 22.3 us
where the time goes in v2:
time: 448 us; the launch traced here: 442 us
  Pallas kernels  415 us (93%)
  local copies, waits for them, and re-layouts  24.2 us (5%)
    pallas_call x1, Pallas kernels, shards(): pl.pallas_call(functools.partial(layer_kernel, cfg), out_shape=(sd((T, CB...  415 us
    unnamed x16, local copies, waits for them, and re-layouts  22.3 us

profile of v2, /device:TPU:0, one launch (start us, length us, event | category | flops | bytes accessed | tf_op | source)
XLA Modules:
  0.0 442.4 jit_solution(5476300896846186746)
XLA Ops:
  0.6 0.7 reduce
  1.3 0.7 reduce.1
  2.0 1.3 reshape.45.keep
  3.3 0.6 maximum_convert_fusion.gains
  3.9 0.8 copy.28
  4.8 0.6 pad.4.w_b
  5.4 415.0 %layer.1 = (bf16[768,384]{1,0:T(8,128)(2,1)}, bf16[768,384]{1,0:T(8,128)(2,1)}, f32[1,384]{1,0:T(1,128)}, f32[1,384]{1,0:T(1,128)}, f32[192,384]{1,0:T(8,128)}, ...) custom-call(s32[2,3]{1,0:T(2,128)} %bitcast.19, ...), custom_call_target="tpu_custom_call" | custom-call | tf_op jit(solution)/shard_map/layer/pallas_call | solution.py:922
  420.5 0.0 copy-start
  420.5 1.6 copy.29
  422.1 1.9 copy.42
  424.0 1.9 copy.43
  426.0 1.2 copy.44
  427.2 1.7 copy.45
  428.9 1.7 copy.46
  430.6 1.7 copy.47
  432.3 1.7 copy.48
  434.0 1.7 copy.49
  435.7 1.2 copy.50
  436.9 2.1 copy.51
  439.0 2.1 copy.52
  441.1 0.0 copy-done
  441.1 0.9 copy.53
  (2 shorter events, 0.0 us)
Async XLA Ops:
  420.5 20.6 %copy-start = (f32[192,1024]{1,0:T(8,128)S(1)}, f32[192,1024]{1,0:T(8,128)}, u32[]{:S(2)}) copy-start(f32[192,1024]{1,0:T(8,128)} %get-tuple-element.38) | copy-start | bytes 2359300

commit v3 on v2

--- a/solution.py
+++ b/solution.py
@@ -18,7 +18,7 @@
 VM = pl.BlockSpec(memory_space=pltpu.VMEM)
 SM = pl.BlockSpec(memory_space=pltpu.SMEM)
 DMA = pltpu.SemaphoreType.DMA
-NRES = 30
+NRES = 27
 
 
 def _dot(a,b,ca,cb): return lax.dot_general(a,b,(((ca,),(cb,)),((),())),preferred_element_type=F32)
@@ -33,18 +33,21 @@
 INV=nn3
 def iotas():
     return lax.broadcasted_iota(jnp.int32,(BLK,BLK),0), lax.broadcasted_iota(jnp.int32,(BLK,BLK),1)
-def tri_inverse(inner, beta_col, row, col):
-    diag=jnp.where(row==col, beta_col, 0.0)
-    beta_lane=jnp.sum(diag,axis=0,keepdims=True)
+def tri_inverse(inners, betas, row, col, between):
     first=((row>>1)==(col>>1))&(row>col)
-    x=diag-jnp.where(first, inner*beta_col*beta_lane, 0.0)
+    xs=[]
+    for inner,beta_col in zip(inners,betas):
+        diag=jnp.where(row==col, beta_col, 0.0)
+        beta_lane=jnp.sum(diag,axis=0,keepdims=True)
+        xs.append(diag-jnp.where(first, inner*beta_col*beta_lane, 0.0))
     lb=1
     while (1<<lb)<BLK:
         m=((row>>(lb+1))==(col>>(lb+1)))&((row>>lb)>(col>>lb))
-        low=jnp.where(m,inner,0.0)
-        x=x-INV(INV(x,low),x)
+        half=[INV(x,jnp.where(m,inner,0.0)) for x,inner in zip(xs,inners)]
+        xs=[x-INV(y,x) for x,y in zip(xs,half)]
+        between(lb)
         lb+=1
-    return x
+    return xs
 def masks(a,c,e0,e1,keep_row,row,col):
     qp=row+BLK*a; kp=col+BLK*c
     segq=(qp>=e0).astype(jnp.int32)+(qp>=e1).astype(jnp.int32)
@@ -52,15 +55,15 @@
     ok=(segq==segk)
     if a==c: return ok&(row>=col)&((keep_row==1)|(row==col))
     return ok&(keep_row==1)
-def fwd_unit(q,k,v,h,beta,keep,e0,e1):
+def fwd_unit(q,k,v,h,X,keep,e0,e1):
     nb=len(q); row,col=iotas(); le=row>=col; st=row>col
-    X,A1,L,W,R,Qm,Km=[],[],[],[],[],[],[]
+    A1,L,W,R,Qm,Km=[],[],[],[],[],[]
     for a in range(nb):
-        x=tri_inverse(nt(h[a],h[a]),beta[a],row,col).astype(BF)
+        x=X[a]
         a1=jnp.where(le,nt(q[a],h[a]),0.0).astype(BF)
         w=jnp.where(st,nt(h[a],k[a]),0.0).astype(BF)
         l=nn(a1,x).astype(BF); r=nn(x,w).astype(BF)
-        X.append(x);A1.append(a1);W.append(w);L.append(l);R.append(r)
+        A1.append(a1);W.append(w);L.append(l);R.append(r)
         Qm.append((q[a].astype(F32)-nn(l,h[a])).astype(BF))
         Km.append((k[a].astype(F32)-tn(r,h[a])).astype(BF))
     scale=1.0/math.sqrt(BLK)
@@ -83,12 +86,12 @@
         for c in sc:
             P[a,c]=(ex[c]*inv).astype(BF); o=o+nn(P[a,c],v[c])
         out.append(o)
-    res=X+A1+L+W+R+Qm+Km+[u,ux,cq]+[P[0,0],P[1,0],P[1,1],P[2,0],P[2,1],P[2,2]]
+    res=A1+L+W+R+Qm+Km+[u,ux,cq]+[P[0,0],P[1,0],P[1,1],P[2,0],P[2,1],P[2,2]]
     return out,res
-def bwd_unit(q,k,v,h,do,res):
+def bwd_unit(q,k,v,h,do,X,res):
     nb=3; row,col=iotas(); le=row>=col; st=row>col
-    X,A1,L,W,R,Qm,Km=[res[3*i:3*i+3] for i in range(7)]
-    u,ux,cq=res[21:24]; pl_=res[24:30]
+    A1,L,W,R,Qm,Km=[res[3*i:3*i+3] for i in range(6)]
+    u,ux,cq=res[18:21]; pl_=res[21:27]
     P={(0,0):pl_[0],(1,0):pl_[1],(1,1):pl_[2],(2,0):pl_[3],(2,1):pl_[4],(2,2):pl_[5]}
     scale=1.0/math.sqrt(BLK)
     G={}; dv=[0.0]*nb
@@ -267,11 +270,11 @@
 
 def layer_kernel(
     cfg, lens, keep, tok, cot, gains, w_q, w_k, w_v, w_h, w_b, w_o, w_g, w_u, w_d,
-    layer_out, tgrad, one, two, o_q, o_k, o_v, o_h, o_b, o_o, o_g, o_u, o_d, g_h, ry_h, z_h, res_h,
-    W, tokf, cotf, n1, n2, hlow, ng, mix, act, gg, ug, qs, ks, vs, hs, hraw, mgrad, beta, dbeta, dB, gf, resb,
-    s1, r1, s2, r2, acc, t2, q2, hidown, hgrad, stage, outv, rts, rtr, rt, gbuf,
+    layer_out, tgrad, gsum, g_h, ry_h, z_h, res_h,
+    W, tokf, cotf, n1, n2, hlow, ng, mix, act, gg, ug, qs, ks, vs, hs, hraw, mgrad, xs, beta, dbeta, dB, gf, resb,
+    s1, r1, s2, r2, acc, t2, q2, hidown, hgrad, stage, rts, rtr, rt, gbuf,
     local, own, hx_s, hx_r, sz, rz, sy, ry, s1s, s1r, s2s, s2r, s3s, s3r, ress, stages,
-    ys, yr, zs, zr, zo, ld, outs, rs_s, rs_r, gs_s, gs_r,
+    ys, yr, zs, zr, zo, ld, rs_s, rs_r, gs_s, gs_r,
 ):
     me = Place(cfg["names"], cfg["sizes"])
     T, D, CB, HL, HD, FL, RS = (cfg[k] for k in ("T", "D", "CB", "HL", "HD", "FL", "RS"))
@@ -286,7 +289,7 @@
     own_rows = pl.ds(pl.multiple_of((me.d * me.wid + me.w) * RS, 16), RS)
     me.greet(me.group() + [me.hid_peer(k) for k in range(1, 4)])
 
-    places = [(w_q, 0), (w_k, HD), (w_v, 2 * HD), (w_h, 3 * HD), (w_b, BC), (w_o, OC), (w_g, GC), (w_u, UC), (w_d, DC)]
+    places = [(w_h, 3 * HD), (w_b, BC), (w_q, 0), (w_k, HD), (w_v, 2 * HD), (w_o, OC), (w_g, GC), (w_u, UC), (w_d, DC)]
     mine = [
         pltpu.make_async_copy(ref, W.at[own_rows, pl.ds(col, ref.shape[1])], own.at[i])
         for i, (ref, col) in enumerate(places)
@@ -313,19 +316,32 @@
     def late(i):
         return Gather(me, RS, W, pl.multiple_of(FB + i * FW, BLK), FW, 6 + i, *sems)
 
-    for i, g in enumerate(first):
-        mine[i].wait()
-        g.start_z()
-        g.start_y()
-    for copy in mine[6:]:
-        copy.wait()
-
-    def start_late(i, carry):
-        late(i).start_z()
-        late(i).start_y()
-        return carry
-
-    lax.fori_loop(0, NF, start_late, 0)
+    NG = len(first) + NF
+
+    def chunk(n):
+        return first[n] if n < len(first) else late(n - len(first))
+
+    def begin(n):
+        if n < NG:
+            if n < len(first):
+                mine[n].wait()
+            elif n == len(first):
+                for copy in mine[6:]:
+                    copy.wait()
+            chunk(n).start_z()
+            chunk(n).start_y()
+
+    events = [
+        (k - hop + 1, hop) for k in range(NG + me.wid - 2) for hop in range(1, me.wid) if 0 <= k - hop + 1 < NG
+    ]
+
+    def advance(count):
+        for _ in range(min(count, len(events))):
+            n, hop = events.pop(0)
+            chunk(n).hop(hop)
+
+    for n in range(NG):
+        begin(n)
     for copy in hid[2]:
         copy.start()
     for i in range(2):
@@ -364,26 +380,39 @@
             if a == 3:
                 beta[m * BUF : (m + 1) * BUF, :] = 2.0 * jax.nn.sigmoid(nn(rows, W[:, BC:]))
 
-    def tick(k):
-        for hop in range(1, me.wid):
-            if 0 <= k - hop + 1 < len(first):
-                first[k - hop + 1].hop(hop)
-
-    for k in range(len(first) + me.wid - 2):
-        tick(k)
-        if 2 <= k < 5:
-            first[k - 2].finish()
-            project(k - 2)
-    first[3].finish()
-    first[4].finish()
+    advance(9)
+    first[0].finish()
+    first[1].finish()
     project(3)
 
-    def late_tick(k):
-        for hop in range(1, me.wid):
-
-            @pl.when((k >= hop - 1) & (k - hop + 1 < NF))
-            def _():
-                late(k - hop + 1).hop(hop)
+    def invert(hd, carry):
+        row, col = iotas()
+        blocks = [(m, a) for m in range(NB) for a in range(3)]
+        parts = [hs[m * HL + hd, a * BLK : (a + 1) * BLK, :] for m, a in blocks]
+        strengths = [column(beta[m * BUF + a * BLK : m * BUF + (a + 1) * BLK, :], hd) for m, a in blocks]
+
+        def between(level):
+            for i in range(HL):
+                later = slots[i].get(level, [])
+                if later:
+
+                    @pl.when(hd == i)
+                    def _():
+                        for n, hop in later:
+                            chunk(n).hop(hop)
+
+        made = tri_inverse([nt(part, part) for part in parts], strengths, row, col, between)
+        for (m, a), x in zip(blocks, made):
+            xs[m * HL + hd, a] = x.astype(BF)
+        return carry
+
+    advance(2)
+    slots = [{level: [events.pop(0)] for level in (2, 4, 6) if events} for _ in range(HL)]
+    lax.fori_loop(0, HL, invert, 0)
+    for a in range(3):
+        first[2 + a].finish()
+        project(a)
+        advance(2)
 
     def attend(u, carry):
         m, hd = lax.div(u, HL), lax.rem(u, HL)
@@ -391,12 +420,10 @@
         e0 = lens[m, 0]
         e1 = e0 + lens[m, 1]
         parts = [slice(a * BLK, (a + 1) * BLK) for a in range(3)]
-        strength = [column(beta[spans(m * BUF + a * BLK, BLK), :], hd) for a in range(3)]
         keys = [keep[m, :, p] for p in parts]
-        late_tick(u)
         out, res = fwd_unit(
             [qs[u, p, :] for p in parts], [ks[u, p, :] for p in parts], [vs[u, p, :] for p in parts],
-            [hs[u, p, :] for p in parts], strength, keys, e0, e1,
+            [hs[u, p, :] for p in parts], [xs[u, a] for a in range(3)], keys, e0, e1,
         )
         for a in range(3):
             mix[spans(m * BUF + a * BLK, BLK), pl.ds(pl.multiple_of(hd * BLK, BLK), BLK)] = out[a].astype(BF)
@@ -408,11 +435,25 @@
         for i, value in enumerate(res):
             resb[slot, i] = value
         pltpu.make_async_copy(resb.at[slot], res_h.at[u], ress.at[slot]).start()
+        for m in range(NB):
+
+            @pl.when(u == (m + 1) * HL - 1)
+            def _():
+                if m == 0:
+                    first[5].finish()
+                first_hop(0, m, branch(m))
+
+            @pl.when(u == (m + 1) * HL)
+            def _():
+                second_hop(0, m)
+
+        for i, (n, hop) in enumerate(during):
+
+            @pl.when(u == i)
+            def _():
+                chunk(n).hop(hop)
+
         return carry
-
-    lax.fori_loop(0, U, attend, 0)
-    for slot in range(2):
-        pltpu.make_async_copy(resb.at[slot], res_h.at[0], ress.at[slot]).wait()
 
     def block(b):
         return pl.ds(pl.multiple_of(b * CB, BLK), CB)
@@ -451,17 +492,11 @@
     def branch(m):
         return lambda b: nt(mix[rows_of(m), :], W[block(b), OC : OC + HD])
 
-    first[5].finish()
-    for m in range(NB):
-        first_hop(0, m, branch(m))
-
-    def more(k, carry):
-        late_tick(k)
-        return carry
-
-    lax.fori_loop(U, NF + me.wid - 2, more, 0)
-    for m in range(NB):
-        second_hop(0, m)
+    during = [events.pop(0) for _ in range(min(U, len(events)))]
+    lax.fori_loop(0, U, attend, 0)
+    for slot in range(2):
+        pltpu.make_async_copy(resb.at[slot], res_h.at[0], ress.at[slot]).wait()
+    second_hop(0, NB - 1)
 
     def residual(m):
         for j in range(2):
@@ -476,9 +511,10 @@
 
     for m in range(NB):
         residual(m)
-    for m in range(NB):
+        advance(2)
         wait_third(0, hlow, m)
         norm(hlow, n2, 8, m * BUF)
+    advance(len(events))
     for copy in hid[2]:
         copy.wait()
 
@@ -659,32 +695,17 @@
                         rs_own(ch, col, width, slot).start()
         rs_own(ch, col, width, slot).wait()
 
-    def rs_late(i):
-        f = lax.rem(i + ND, NF)
-        return 6 + f, pl.multiple_of(FB + f * FW, BLK), FW
-
-    def rs_sum(ch, col, width, out, at, side, busy):
-        for k in range(1, me.wid):
-            rs_z(ch, col, width, 0, k).wait_recv()
-        loads = [
-            pltpu.make_async_copy(
-                z_h.at[k, :, pl.ds(col, width)], loaded.at[pl.ds(k * RS, RS), pl.ds(0, width)], ld.at[2 + k]
-            )
-            for k in range(me.wid)
-        ]
-        for copy in loads:
-            copy.start()
-        if busy is not None:
-            busy.wait()
-        for copy in loads:
-            copy.wait()
-        done = loaded[0:RS, 0:width].astype(F32)
-        for k in range(1, me.wid):
-            done = done + loaded[k * RS : (k + 1) * RS, 0:width].astype(F32)
-        outv[side, :, 0:width] = done
-        copy = pltpu.make_async_copy(outv.at[side, :, pl.ds(0, width)], out.at[:, pl.ds(at, width)], outs.at[side])
-        copy.start()
-        return copy
+    places_of = [(3 * HD, HD), (BC, BLK), (0, HD), (HD, HD), (2 * HD, HD), (OC, HD)]
+    order = [(6 + (i + ND) % NF, FB + (i + ND) % NF * FW, FW) for i in range(NF)]
+    order += [(k, *places_of[k]) for k in (5, 2, 3, 4, 0, 1)]
+    taken = [0]
+
+    def take():
+        n = taken[0]
+        taken[0] += 1
+        if n >= 4:
+            rs_free(*order[n - 4], n % 4)
+        rs_stage(*order[n], n % 4)
 
     def spread_back(m):
         for j in range(2):
@@ -732,12 +753,6 @@
         slot = lax.rem(u, 2)
         parts = [slice(a * BLK, (a + 1) * BLK) for a in range(3)]
 
-        @pl.when(hd == 0)
-        def _():
-            spread_back(m)
-            wait_third(1, ng, m)
-            branch_back(m)
-
         fetch_res(u).wait()
 
         @pl.when(u + 1 < U)
@@ -746,7 +761,8 @@
 
         dq, dk, dv, dh, db = bwd_unit(
             [qs[u, p, :] for p in parts], [ks[u, p, :] for p in parts], [vs[u, p, :] for p in parts],
-            [hs[u, p, :] for p in parts], [mgrad[u, p, :] for p in parts], [resb[slot, i] for i in range(NRES)],
+            [hs[u, p, :] for p in parts], [mgrad[u, p, :] for p in parts], [xs[u, a] for a in range(3)],
+            [resb[slot, i] for i in range(NRES)],
         )
         for a in range(3):
             rows = spans(m * BUF + a * BLK, BLK)
@@ -763,26 +779,23 @@
             lanes = lax.broadcasted_iota(jnp.int32, (BLK, BLK), 1)
             dbeta[rows, :] += jnp.where(lanes == hd, pull, 0.0)
 
-        @pl.when((u >= 1) & (u <= NF))
-        def _():
-            i = u - 1
-            slot = lax.rem(i, 4)
-
-            @pl.when(i >= 4)
-            def _():
-                rs_free(*rs_late(i - 4), slot)
-
-            rs_stage(*rs_late(i), slot)
-
         return carry
 
+    take()
+    for m in range(NB):
+        spread_back(m)
+        wait_third(1, ng, m)
+        branch_back(m)
+        if m == 0:
+            take()
     lax.fori_loop(0, U, attend_back, 0)
     dB[...] = dbeta[...].astype(BF)
-    statics = {5: (5, OC, HD), 0: (0, 0, HD), 1: (1, HD, HD), 2: (2, 2 * HD, HD), 3: (3, 3 * HD, HD), 4: (4, BC, BLK)}
     weight_term(5, ng, mix, 0, OC, HD)
-    for a in range(4):
-        weight_term(a, n1, dA, a * HD, a * HD, HD)
-    weight_term(4, n1, dB, 0, BC, BLK)
+    take()
+    for a in range(3):
+        weight_term(2 + a, n1, dA, a * HD, a * HD, HD)
+    weight_term(0, n1, dA, 3 * HD, 3 * HD, HD)
+    weight_term(1, n1, dB, 0, BC, BLK)
     flush()
 
     rt[...] = jnp.zeros_like(rt)
@@ -818,37 +831,7 @@
         t2[m] = (acc[m, other] + r1[0, m, other].astype(F32)).astype(BF)
         hop2_in(m).start()
 
-    done = min(max(U - 1, 0), NF)
-    order = [(6 + (i + ND) % NF, FB + (i + ND) % NF * FW, FW) for i in range(NF)]
-    order += [statics[k] for k in (5, 0, 1, 2, 3, 4)]
-
-    def target(ch, col):
-        if ch < 6:
-            return (o_q, o_k, o_v, o_h, o_b, o_o)[ch], 0
-        return (o_g, o_u, o_d)[(col - FB) // FL], (col - FB) % FL
-
-    writing = [None, None]
-    summed = [0]
-    freed = [max(done - 4, 0)]
-
-    def take(n):
-        if n >= 4 and freed[0] == n - 4:
-            rs_free(*order[n - 4], (n - 4) % 4)
-            freed[0] += 1
-        rs_stage(*order[n], n % 4)
-
-    def give():
-        n = summed[0]
-        side = n % 2
-        ch, col, width = order[n]
-        out, at = target(ch, col)
-        writing[side] = rs_sum(ch, col, width, out, at, side, writing[side])
-        summed[0] += 1
-
-    for n in range(done, NF + 1):
-        take(n)
-    give()
-    give()
+    take()
     for m in range(NB):
         hop2_in(m).wait()
     for copy in rt_copies:
@@ -875,24 +858,61 @@
         copy = send(gbuf.at[slot_here], gbuf.at[slot_here], gs_s.at[n], gs_r.at[n], peer)
         copy.start()
         gain_copies.append(copy)
-    for n in range(NF + 1, len(order)):
-        take(n)
-        give()
+    while taken[0] < len(order):
+        take()
     for copy in gain_copies:
         copy.wait()
     both = gbuf[0]
     for n in range(1, me.dp * me.wid):
         both = both + gbuf[n]
-    one[...] = both[0:1, :]
-    two[...] = both[8:9, :]
-    while summed[0] < len(order):
-        give()
-    for n in range(freed[0], len(order)):
+    gsum[...] = both
+    for ch, col, width in order:
+        for k in range(1, me.wid):
+            rs_z(ch, col, width, 0, k).wait_recv()
+    for n in range(len(order) - 4, len(order)):
         rs_free(*order[n], n % 4)
     for ch, col, width in order:
         for j in range(1, me.dp):
             rs_y(ch, col, width, j).wait_send()
-    for copy in writing:
+
+
+def final_kernel(
+    cfg, z_h, layer_in, tgrad_in, gsum,
+    layer_out, tgrad, one, two, o_q, o_k, o_v, o_h, o_b, o_o, o_g, o_u, o_d,
+    zbuf, total, gb, loads, stores, through,
+):
+    HD, FL, RS, wid = cfg["HD"], cfg["FL"], cfg["RS"], cfg["sizes"]["wid"]
+    FB = 5 * HD
+    targets = [(o_g, FB, FL), (o_u, FB + FL, FL), (o_d, FB + 2 * FL, FL), (o_q, 0, HD), (o_k, HD, HD), (o_v, 2 * HD, HD)]
+    targets += [(o_h, 3 * HD, HD), (o_o, 4 * HD, HD), (None, FB + 3 * FL, BLK)]
+    passed = [
+        pltpu.make_async_copy(layer_in, layer_out, through.at[0]),
+        pltpu.make_async_copy(tgrad_in, tgrad, through.at[1]),
+        pltpu.make_async_copy(gsum, gb, through.at[2]),
+    ]
+    copies = [
+        pltpu.make_async_copy(z_h.at[:, :, pl.ds(col, w)], zbuf.at[:, :, pl.ds(col, w)], loads.at[i])
+        for i, (_, col, w) in enumerate(targets)
+    ]
+    for copy in copies + passed:
+        copy.start()
+    written = []
+    for i, (out, col, w) in enumerate(targets):
+        copies[i].wait()
+        value = zbuf[0, :, col : col + w].astype(F32)
+        for k in range(1, wid):
+            value = value + zbuf[k, :, col : col + w].astype(F32)
+        if out is None:
+            o_b[...] = value[:, 0 : o_b.shape[1]]
+        else:
+            total[:, col : col + w] = value
+            copy = pltpu.make_async_copy(total.at[:, pl.ds(col, w)], out, stores.at[i])
+            copy.start()
+            written.append(copy)
+    passed[2].wait()
+    one[...] = gb[0:1, :]
+    two[...] = gb[8:9, :]
+    for copy in passed[:2] + written:
         copy.wait()
 
 
@@ -922,25 +942,24 @@
         outs = pl.pallas_call(
             functools.partial(layer_kernel, cfg),
             out_shape=(
-                sd((T, CB), BF), sd((T, CB), BF), sd((1, CB), F32), sd((1, CB), F32),
-                *[sd((RS, HD), F32)] * 4, sd((RS, BLK), F32), sd((RS, HD), F32), *[sd((RS, FL), F32)] * 3,
+                sd((T, CB), BF), sd((T, CB), BF), sd((16, CB), F32),
                 sd((D, CT), BF), sd((dp - 1, DR, CT), BF), sd((wid, RS, CT), BF), sd((U, NRES, BLK, BLK), BF),
             ),
             in_specs=[SM, VM] + [ANY] * 12,
-            out_specs=(VM,) * 4 + (ANY,) * 13,
+            out_specs=(VM,) * 3 + (ANY,) * 4,
             scratch_shapes=[
                 vm((D, CT), BF), *[vm((T, D), BF)] * 6, vm((T, HD), BF), *[vm((T, FL), BF)] * 3,
-                *[unit(BF)] * 4, unit(F32), unit(BF), vm((T, BLK), F32), vm((T, BLK), F32), vm((T, BLK), BF),
+                *[unit(BF)] * 4, unit(F32), unit(BF), vm((U, 3, BLK, BLK), BF), vm((T, BLK), F32), vm((T, BLK), F32), vm((T, BLK), BF),
                 vm((16, D), F32), vm((2, NRES, BLK, BLK), BF),
                 pair, vm((2, NB, 2, BUF, CB), BF), pair, vm((2, NB, 2, BUF, CB), BF), vm((NB, 2, BUF, CB), F32),
                 vm((NB, BUF, CB), BF), vm((NB, BUF, CB), BF), vm((T, CB), F32), vm((T, CB), F32),
-                vm((2, 4, CB, FW), BF), vm((2, RS, FW), F32),
+                vm((2, 4, CB, FW), BF),
                 vm((8, T), F32), vm((3, 8, T), F32), vm((T, BLK), F32), vm((dp * wid, 16, CB), F32),
                 DMA((3,)), DMA((9,)), DMA((3, 3)), DMA((3, 3)), DMA((nch, 2, wid)), DMA((nch, 2, wid)),
                 DMA((nch, wid, dp - 1)), DMA((nch, wid, dp - 1)),
                 *[DMA((4, NB, 2))] * 4, *[DMA((2, NB, 2))] * 2, DMA((2,)), DMA((2, 4)),
                 DMA((nch, dp - 1)), DMA((nch, dp - 1)), DMA((nch, wid - 1)), DMA((nch, wid - 1)), DMA((nch,)),
-                DMA((2 + wid,)), DMA((2,)), DMA((3,)), DMA((3,)), DMA((dp * wid - 1,)), DMA((dp * wid - 1,)),
+                DMA((2,)), DMA((3,)), DMA((3,)), DMA((dp * wid - 1,)), DMA((dp * wid - 1,)),
             ],
             compiler_params=pltpu.CompilerParams(
                 collective_id=0, has_side_effects=True, vmem_limit_bytes=cfg.get("limit", 63 << 20)
@@ -951,10 +970,24 @@
             cotangent.reshape(T, CB), gains, w_query, w_key, w_value, w_house,
             jnp.pad(w_beta, ((0, 0), (0, BLK - heads))), w_out.T, w_gate, w_up, w_down.T,
         )
-        layer_out, tgrad, one, two, gq, gk, gv, gh, gb, go, g_gate, g_up, g_down = outs[:13]
+        done = pl.pallas_call(
+            functools.partial(final_kernel, cfg),
+            out_shape=(
+                sd((T, CB), BF), sd((T, CB), BF), sd((1, CB), F32), sd((1, CB), F32),
+                *[sd((RS, HD), F32)] * 4, sd((RS, heads), F32), sd((RS, HD), F32), *[sd((RS, FL), F32)] * 3,
+            ),
+            in_specs=[ANY] * 4,
+            out_specs=(ANY, ANY, VM, VM) + (ANY,) * 4 + (VM,) + (ANY,) * 4,
+            scratch_shapes=[
+                vm((wid, RS, CT), BF), vm((RS, CT), F32), vm((16, CB), F32), DMA((9,)), DMA((9,)), DMA((3,)),
+            ],
+            compiler_params=pltpu.CompilerParams(vmem_limit_bytes=32 << 20),
+            name="final",
+        )(outs[5], outs[0], outs[1], outs[2])
+        layer_out, tgrad, one, two, gq, gk, gv, gh, gb, go, g_gate, g_up, g_down = done
         return (
-            layer_out.reshape(tokens.shape), tgrad.reshape(tokens.shape), one, gq, gk, gv, gh, gb[:, :heads],
-            go.T, two, g_gate, g_up, g_down.T,
+            layer_out.reshape(tokens.shape), tgrad.reshape(tokens.shape), one, gq, gk, gv, gh, gb, go.T, two,
+            g_gate, g_up, g_down.T,
         )
 
     rows = P(("dp", "wid"), "hid")

time: 448 us -> 414 us (0.924)
  Pallas kernels: 415 us -> 394 us
  local copies, waits for them, and re-layouts: 24.2 us -> 9.5 us
    pallas_call x1, Pallas kernels: 415 us -> 390 us  [shards(): pl.pallas_call(functools.partial(layer_kernel, cfg), out_shape=(sd((T, CB...]
    unnamed x16 -> x10, local copies, waits for them, and re-layouts: 22.3 us -> 7.58 us
where the time goes in v3:
time: 414 us; the launch traced here: 407 us
  Pallas kernels  394 us (95%)
  local copies, waits for them, and re-layouts  9.5 us (2%)
    pallas_call x1, Pallas kernels, shards(): pl.pallas_call(functools.partial(layer_kernel, cfg), out_shape=(sd((T, CB...  390 us

profile of v3, /device:TPU:0, one launch (start us, length us, event | category | flops | bytes accessed | tf_op | source)
XLA Modules:
  0.0 407.0 jit_solution(16358089555571680916)
XLA Ops:
  0.6 0.7 reduce
  1.3 0.7 reduce.1
  2.0 1.3 reshape.45.keep
  3.3 0.6 maximum_convert_fusion.gains
  3.9 0.8 copy.28
  4.8 0.6 pad.4.w_b
  5.4 390.2 %layer.1 = (bf16[768,384]{1,0:T(8,128)(2,1)}, bf16[768,384]{1,0:T(8,128)(2,1)}, f32[16,384]{1,0:T(8,128)}, bf16[1536,5120]{1,0:T(8,128)(2,1)}, bf16[1,768,5120]{...) custom-call(s32[2,3]{1,0:T(2,128)} %bitcast.13, s32[2,1,384]{2,1,0:T(1,128)} %reshape.45.keep, ...), custom_call_target="tpu_custom_call" | custom-call | tf_op jit(solution)/shard_map/layer/pallas_call | solution.py:942
  395.6 0.0 copy-start
  395.6 3.2 copy-done
  398.8 0.0 copy-start.1
  398.8 1.1 copy-done.1
  399.9 0.0 copy-start.2
  399.9 1.1 copy-done.2
  400.9 0.0 copy-start.3
  400.9 0.7 copy-done.3
  401.7 4.2 %final.1 = (bf16[768,384]{1,0:T(8,128)(2,1)}, bf16[768,384]{1,0:T(8,128)(2,1)}, f32[1,384]{1,0:T(1,128)}, f32[1,384]{1,0:T(1,128)}, f32[192,384]{1,0:T(8,128)}, ...) custom-call(bf16[4,192,5120]{2,1,0:T(8,128)(2,1)S(1)} %copy-done, ...), custom_call_target="tpu_custom_call" | custom-call | tf_op jit(solution)/shard_map/final/pallas_call | solution.py:973
  405.9 0.7 copy.29
  (2 shorter events, 0.0 us)
Async XLA Ops:
  395.6 3.2 copy-start
  398.8 1.1 copy-start.1
  399.9 1.1 copy-start.2
  400.9 0.7 copy-start.3

commit v4 on v3

--- a/solution.py
+++ b/solution.py
@@ -249,7 +249,7 @@
             for o in range(me.wid):
                 self.ycopy(lax.rem(me.d + me.dp - j, me.dp), o, j).wait_recv()
 
-    def drain(self):
+    def drain_z(self):
         me = self.me
         for way in (1, -1):
             for hop in range(me.wid):
@@ -258,9 +258,68 @@
                 def _():
                     self.zcopy(way, hop, hop).wait_send()
 
-        for j in range(1, me.dp):
-            for o in range(me.wid):
-                self.ycopy(me.d, o, j).wait_send()
+    def drain(self):
+        self.drain_z()
+        for j in range(1, self.me.dp):
+            for o in range(self.me.wid):
+                self.ycopy(self.me.d, o, j).wait_send()
+
+
+class Line(Gather):
+    def __init__(self, d, *args):
+        super().__init__(*args)
+        self.group = d
+
+    def zcopy(self, way, hop, sem):
+        me, side = self.me, (way + 1) // 2
+        part = self.piece(self.group, self.origin(way, hop))
+        return send(
+            part, part, self.sz.at[self.ch, side, sem], self.rz.at[self.ch, side, sem],
+            me.at(w=lax.clamp(0, me.w + way, me.wid - 1)),
+        )
+
+    def hop(self, hop):
+        for way in (1, -1):
+
+            @pl.when(self.has_piece(way, hop))
+            def _():
+                self.zcopy(way, hop, hop - 1).wait_recv()
+
+                @pl.when(self.has_next(way))
+                def _():
+                    self.zcopy(way, hop, hop).start()
+
+
+class Across(Gather):
+    def __init__(self, extra, *args):
+        super().__init__(*args)
+        me, rows, full, col, width, ch = args[:6]
+        self.lines = [
+            Line(lax.rem(me.d + me.dp - j, me.dp), me, rows, full, col, width, ch if j == 0 else extra + j - 1, *args[6:])
+            for j in range(me.dp)
+        ]
+
+    def start_z(self):
+        self.lines[0].start_z()
+
+    def hop(self, hop):
+        me = self.me
+        if hop == 0:
+            for j in range(1, me.dp):
+                self.ycopy(lax.rem(me.d + me.dp - j, me.dp), me.w, j).wait_recv()
+                self.lines[j].start_z()
+        else:
+            for line in self.lines:
+                line.hop(hop)
+
+    def finish(self):
+        pass
+
+    def drain(self):
+        for line in self.lines:
+            line.drain_z()
+        for j in range(1, self.me.dp):
+            self.ycopy(self.me.d, self.me.w, j).wait_send()
 
 
 def column(values, lane_index):
@@ -314,7 +373,10 @@
     ]
 
     def late(i):
-        return Gather(me, RS, W, pl.multiple_of(FB + i * FW, BLK), FW, 6 + i, *sems)
+        args = (me, RS, W, FB + i * FW, FW, 6 + i, *sems)
+        if i in cfg["across"]:
+            return Across(6 + NF + cfg["across"].index(i) * (me.dp - 1), *args)
+        return Gather(*args)
 
     NG = len(first) + NF
 
@@ -334,6 +396,8 @@
     events = [
         (k - hop + 1, hop) for k in range(NG + me.wid - 2) for hop in range(1, me.wid) if 0 <= k - hop + 1 < NG
     ]
+    for i in cfg["across"]:
+        events.insert(events.index((6 + i, 1)), (6 + i, 0))
 
     def advance(count):
         for _ in range(min(count, len(events))):
@@ -518,13 +582,10 @@
     for copy in hid[2]:
         copy.wait()
 
-    def finish_late(i, carry):
-        late(i).finish()
-        return carry
-
     NT = 256
     ND = 2 * FL // FW
-    lax.fori_loop(0, ND, finish_late, 0)
+    for i in range(ND):
+        late(i).finish()
 
     def ffn(m):
         def body(n, carry):
@@ -602,7 +663,8 @@
         ffn(m)
     ffn_terms(cotf, act, DC)
     flush()
-    lax.fori_loop(ND, NF, finish_late, 0)
+    for i in range(ND, NF):
+        late(i).finish()
 
     def normed_back(m):
         return lambda b: nt(gg[rows_of(m), :], W[block(b), GC : GC + FL]) + nt(
@@ -624,11 +686,8 @@
     for g in first:
         g.drain()
 
-    def drain_late(i, carry):
+    for i in range(NF):
         late(i).drain()
-        return carry
-
-    lax.fori_loop(0, NF, drain_late, 0)
     ffn_terms(n2, gg, GC)
     ffn_terms(n2, ug, UC)
     flush()
@@ -932,7 +991,7 @@
         U, NF, DR = NB * HL, 3 * FL // FW, D // dp
         CT = 5 * HD + 3 * FL + BLK
         heads = w_beta.shape[1]
-        cfg = dict(names=names, sizes=sizes, T=T, D=D, CB=CB, HL=HL, HD=HD, FL=FL, RS=RS, FW=FW)
+        cfg = dict(names=names, sizes=sizes, T=T, D=D, CB=CB, HL=HL, HD=HD, FL=FL, RS=RS, FW=FW, across=[4, 5])
         gains = jnp.concatenate([jnp.broadcast_to(g, (8, CB)) for g in (norm_one, norm_two)], axis=0).astype(F32)
         sd = jax.ShapeDtypeStruct
         nch = 6 + NF
@@ -955,7 +1014,7 @@
                 vm((NB, BUF, CB), BF), vm((NB, BUF, CB), BF), vm((T, CB), F32), vm((T, CB), F32),
                 vm((2, 4, CB, FW), BF),
                 vm((8, T), F32), vm((3, 8, T), F32), vm((T, BLK), F32), vm((dp * wid, 16, CB), F32),
-                DMA((3,)), DMA((9,)), DMA((3, 3)), DMA((3, 3)), DMA((nch, 2, wid)), DMA((nch, 2, wid)),
+                DMA((3,)), DMA((9,)), DMA((3, 3)), DMA((3, 3)), *[DMA((nch + len(cfg["across"]) * (dp - 1), 2, wid))] * 2,
                 DMA((nch, wid, dp - 1)), DMA((nch, wid, dp - 1)),
                 *[DMA((4, NB, 2))] * 4, *[DMA((2, NB, 2))] * 2, DMA((2,)), DMA((2, 4)),
                 DMA((nch, dp - 1)), DMA((nch, dp - 1)), DMA((nch, wid - 1)), DMA((nch, wid - 1)), DMA((nch,)),

time: 414 us -> 408 us (0.986)
  the two profiles are of different devices: /device:TPU:0 before, /device:TPU:24 now
where the time goes in v4:
time: 408 us; the launch traced here: 401 us
  Pallas kernels  388 us (95%)
  local copies, waits for them, and re-layouts  9.5 us (2%)
    pallas_call x1, Pallas kernels, shards(): pl.pallas_call(functools.partial(layer_kernel, cfg), out_shape=(sd((T, CB...  384 us

profile of v4, /device:TPU:24, one launch (start us, length us, event | category | flops | bytes accessed | tf_op | source)
XLA Modules:
  0.0 400.7 jit_solution(3908283931003568353)
XLA Ops:
  0.6 0.7 reduce
  1.3 0.7 reduce.1
  2.0 1.3 reshape.45.keep
  3.3 0.6 maximum_convert_fusion.gains
  3.9 0.8 copy.28
  4.8 0.6 pad.4.w_b
  5.4 383.9 %layer.1 = (bf16[768,384]{1,0:T(8,128)(2,1)}, bf16[768,384]{1,0:T(8,128)(2,1)}, f32[16,384]{1,0:T(8,128)}, bf16[1536,5120]{1,0:T(8,128)(2,1)}, bf16[1,768,5120]{...) custom-call(s32[2,3]{1,0:T(2,128)} %bitcast.13, s32[2,1,384]{2,1,0:T(1,128)} %reshape.45.keep, ...), custom_call_target="tpu_custom_call" | custom-call | tf_op jit(solution)/shard_map/layer/pallas_call | solution.py:1001
  389.3 0.0 copy-start
  389.3 3.2 copy-done
  392.5 0.0 copy-start.1
  392.5 1.1 copy-done.1
  393.6 0.0 copy-start.2
  393.6 1.1 copy-done.2
  394.7 0.0 copy-start.3
  394.7 0.7 copy-done.3
  395.4 4.2 %final.1 = (bf16[768,384]{1,0:T(8,128)(2,1)}, bf16[768,384]{1,0:T(8,128)(2,1)}, f32[1,384]{1,0:T(1,128)}, f32[1,384]{1,0:T(1,128)}, f32[192,384]{1,0:T(8,128)}, ...) custom-call(bf16[4,192,5120]{2,1,0:T(8,128)(2,1)S(1)} %copy-done, ...), custom_call_target="tpu_custom_call" | custom-call | tf_op jit(solution)/shard_map/final/pallas_call | solution.py:1032
  399.6 0.7 copy.29
  (2 shorter events, 0.0 us)
Async XLA Ops:
  389.3 3.2 copy-start
  392.5 1.1 copy-start.1
  393.6 1.1 copy-start.2
  394.7 0.7 copy-start.3

commit v5 on v4

--- a/solution.py
+++ b/solution.py
@@ -329,7 +329,7 @@
 
 def layer_kernel(
     cfg, lens, keep, tok, cot, gains, w_q, w_k, w_v, w_h, w_b, w_o, w_g, w_u, w_d,
-    layer_out, tgrad, gsum, g_h, ry_h, z_h, res_h,
+    layer_out, tgrad, gsum, g_h, ry_h, z_h, zt_h, res_h,
     W, tokf, cotf, n1, n2, hlow, ng, mix, act, gg, ug, qs, ks, vs, hs, hraw, mgrad, xs, beta, dbeta, dB, gf, resb,
     s1, r1, s2, r2, acc, t2, q2, hidown, hgrad, stage, rts, rtr, rt, gbuf,
     local, own, hx_s, hx_r, sz, rz, sy, ry, s1s, s1r, s2s, s2r, s3s, s3r, ress, stages,
@@ -578,7 +578,7 @@
         advance(2)
         wait_third(0, hlow, m)
         norm(hlow, n2, 8, m * BUF)
-    advance(len(events))
+    advance(max([i + 1 for i, (n, _) in enumerate(events) if n < 6 + 2 * FL // FW], default=0))
     for copy in hid[2]:
         copy.wait()
 
@@ -663,6 +663,7 @@
         ffn(m)
     ffn_terms(cotf, act, DC)
     flush()
+    advance(len(events))
     for i in range(ND, NF):
         late(i).finish()
 
@@ -706,32 +707,75 @@
 
     gm = W.at[0:DR, FB : FB + FW]
     peer_term = W.at[DR : 2 * DR, FB : FB + FW]
-    loaded = W.at[DR : 2 * DR, FB + FW : FB + 2 * FW]
+    inbox = W.at[DR : 2 * DR, FB + FW : FB + 2 * FW]
 
     def to_wid(slot):
-        return W.at[0:DR, pl.ds(pl.multiple_of(FB + FW + slot * FW, BLK), FW)]
-
-    def wid_rows(k):
-        return pl.ds(pl.multiple_of(lax.rem(me.w + k, me.wid) * RS, 16), RS)
-
-    def rs_z(ch, col, width, slot, k):
+        return W.at[0:DR, FB + FW + slot * FW : FB + 2 * FW + slot * FW]
+
+    near = me.w + 1 - 2 * lax.rem(me.w, 2)
+    far = 2 - 2 * lax.div(me.w, 2)
+    inner = (me.w == 1) | (me.w == 2)
+    outer = jnp.logical_not(inner)
+
+    def block_rows(o, count=1):
+        return pl.ds(pl.multiple_of(o * RS, 16), count * RS)
+
+    def to_near(ch, col, width, slot):
         return send(
-            to_wid(slot).at[wid_rows(k), pl.ds(0, width)], z_h.at[k, :, pl.ds(col, width)],
-            zs.at[ch, k - 1], zr.at[ch, k - 1], me.wid_peer(k),
-        )
-
-    def rs_own(ch, col, width, slot):
-        return pltpu.make_async_copy(
-            to_wid(slot).at[wid_rows(0), pl.ds(0, width)], z_h.at[0, :, pl.ds(col, width)], zo.at[ch]
+            to_wid(slot).at[block_rows(near), pl.ds(0, width)], z_h.at[1, :, pl.ds(col, width)],
+            zs.at[ch, 0], zr.at[ch, 0], me.at(w=near),
+        )
+
+    def to_inner(ch, col, width, slot):
+        return send(
+            to_wid(slot).at[block_rows(far, 2), pl.ds(0, width)], zt_h.at[:, pl.ds(col, width)],
+            zs.at[ch, 1], zr.at[ch, 1], me.at(w=near),
+        )
+
+    def to_far(ch, col, width, slot, i):
+        return send(
+            to_wid(slot).at[block_rows(far + i), pl.ds(0, width)], z_h.at[2, :, pl.ds(col, width)],
+            zs.at[ch, 2 + i], zr.at[ch, 2], me.at(w=far + i),
         )
 
     def rs_free(ch, col, width, slot):
-        for k in range(1, me.wid):
-            rs_z(ch, col, width, slot, k).wait_send()
+        to_near(ch, col, width, slot).wait_send()
+
+        @pl.when(outer)
+        def _():
+            to_inner(ch, col, width, slot).wait_send()
+
+        @pl.when(inner)
+        def _():
+            for i in range(2):
+                to_far(ch, col, width, slot, i).wait_send()
+
+    def rs_across(ch, col, width, slot):
+        @pl.when(inner)
+        def _():
+            to_inner(ch, col, width, slot).wait_recv()
+            load = pltpu.make_async_copy(
+                zt_h.at[:, pl.ds(col, width)], inbox.at[pl.ds(0, 2 * RS), pl.ds(0, width)], ld.at[2]
+            )
+            load.start()
+            load.wait()
+            for i in range(2):
+                rows = block_rows(far + i)
+                to_wid(slot)[rows, 0:width] = (
+                    to_wid(slot)[rows, 0:width].astype(F32) + inbox[i * RS : (i + 1) * RS, 0:width].astype(F32)
+                ).astype(BF)
+                to_far(ch, col, width, slot, i).start()
+
+    def rs_end(ch, col, width):
+        to_near(ch, col, width, 0).wait_recv()
+        to_far(ch, col, width, 0, 0).wait_recv()
 
     def rs_stage(ch, col, width, slot):
         here = pltpu.make_async_copy(g_h.at[dp_rows(0), pl.ds(col, width)], gm.at[:, pl.ds(0, width)], ld.at[0])
         here.start()
+        mine_out = pltpu.make_async_copy(
+            to_wid(slot).at[block_rows(me.w), pl.ds(0, width)], z_h.at[0, :, pl.ds(col, width)], zo.at[ch]
+        )
         for j in range(1, me.dp):
             rs_y(ch, col, width, j).wait_recv()
             there = pltpu.make_async_copy(
@@ -741,18 +785,24 @@
             if j == 1:
                 here.wait()
             there.wait()
-            for k in range(me.wid):
-                rows = wid_rows(k)
+            for i, o in enumerate((far, far + 1, near, me.w)):
+                rows = block_rows(o)
                 so_far = gm if j == 1 else to_wid(slot)
                 to_wid(slot)[rows, 0:width] = (
                     so_far[rows, 0:width].astype(F32) + peer_term[rows, 0:width].astype(F32)
                 ).astype(BF)
                 if j == me.dp - 1:
-                    if k > 0:
-                        rs_z(ch, col, width, slot, k).start()
-                    else:
-                        rs_own(ch, col, width, slot).start()
-        rs_own(ch, col, width, slot).wait()
+                    if i == 1:
+
+                        @pl.when(outer)
+                        def _():
+                            to_inner(ch, col, width, slot).start()
+
+                    if i == 2:
+                        to_near(ch, col, width, slot).start()
+                    if i == 3:
+                        mine_out.start()
+        mine_out.wait()
 
     places_of = [(3 * HD, HD), (BC, BLK), (0, HD), (HD, HD), (2 * HD, HD), (OC, HD)]
     order = [(6 + (i + ND) % NF, FB + (i + ND) % NF * FW, FW) for i in range(NF)]
@@ -765,6 +815,10 @@
         if n >= 4:
             rs_free(*order[n - 4], n % 4)
         rs_stage(*order[n], n % 4)
+        if n >= 1:
+            rs_across(*order[n - 1], (n - 1) % 4)
+        if n == len(order) - 1:
+            rs_across(*order[n], n % 4)
 
     def spread_back(m):
         for j in range(2):
@@ -926,8 +980,7 @@
         both = both + gbuf[n]
     gsum[...] = both
     for ch, col, width in order:
-        for k in range(1, me.wid):
-            rs_z(ch, col, width, 0, k).wait_recv()
+        rs_end(ch, col, width)
     for n in range(len(order) - 4, len(order)):
         rs_free(*order[n], n % 4)
     for ch, col, width in order:
@@ -940,7 +993,7 @@
     layer_out, tgrad, one, two, o_q, o_k, o_v, o_h, o_b, o_o, o_g, o_u, o_d,
     zbuf, total, gb, loads, stores, through,
 ):
-    HD, FL, RS, wid = cfg["HD"], cfg["FL"], cfg["RS"], cfg["sizes"]["wid"]
+    HD, FL, RS = cfg["HD"], cfg["FL"], cfg["RS"]
     FB = 5 * HD
     targets = [(o_g, FB, FL), (o_u, FB + FL, FL), (o_d, FB + 2 * FL, FL), (o_q, 0, HD), (o_k, HD, HD), (o_v, 2 * HD, HD)]
     targets += [(o_h, 3 * HD, HD), (o_o, 4 * HD, HD), (None, FB + 3 * FL, BLK)]
@@ -959,7 +1012,7 @@
     for i, (out, col, w) in enumerate(targets):
         copies[i].wait()
         value = zbuf[0, :, col : col + w].astype(F32)
-        for k in range(1, wid):
+        for k in range(1, 3):
             value = value + zbuf[k, :, col : col + w].astype(F32)
         if out is None:
             o_b[...] = value[:, 0 : o_b.shape[1]]
@@ -979,7 +1032,7 @@
     names = tuple(mesh.axis_names)
     sizes = {n: mesh.shape[n] for n in names}
     dp, wid = sizes["dp"], sizes["wid"]
-    assert sizes["hid"] == 4
+    assert sizes["hid"] == 4 and wid == 4
 
     def shards(
         tokens, cotangent, lengths, keep, norm_one, w_query, w_key, w_value, w_house, w_beta, w_out, norm_two,
@@ -1002,10 +1055,11 @@
             functools.partial(layer_kernel, cfg),
             out_shape=(
                 sd((T, CB), BF), sd((T, CB), BF), sd((16, CB), F32),
-                sd((D, CT), BF), sd((dp - 1, DR, CT), BF), sd((wid, RS, CT), BF), sd((U, NRES, BLK, BLK), BF),
+                sd((D, CT), BF), sd((dp - 1, DR, CT), BF), sd((3, RS, CT), BF), sd((2 * RS, CT), BF),
+                sd((U, NRES, BLK, BLK), BF),
             ),
             in_specs=[SM, VM] + [ANY] * 12,
-            out_specs=(VM,) * 3 + (ANY,) * 4,
+            out_specs=(VM,) * 3 + (ANY,) * 5,
             scratch_shapes=[
                 vm((D, CT), BF), *[vm((T, D), BF)] * 6, vm((T, HD), BF), *[vm((T, FL), BF)] * 3,
                 *[unit(BF)] * 4, unit(F32), unit(BF), vm((U, 3, BLK, BLK), BF), vm((T, BLK), F32), vm((T, BLK), F32), vm((T, BLK), BF),
@@ -1017,8 +1071,8 @@
                 DMA((3,)), DMA((9,)), DMA((3, 3)), DMA((3, 3)), *[DMA((nch + len(cfg["across"]) * (dp - 1), 2, wid))] * 2,
                 DMA((nch, wid, dp - 1)), DMA((nch, wid, dp - 1)),
                 *[DMA((4, NB, 2))] * 4, *[DMA((2, NB, 2))] * 2, DMA((2,)), DMA((2, 4)),
-                DMA((nch, dp - 1)), DMA((nch, dp - 1)), DMA((nch, wid - 1)), DMA((nch, wid - 1)), DMA((nch,)),
-                DMA((2,)), DMA((3,)), DMA((3,)), DMA((dp * wid - 1,)), DMA((dp * wid - 1,)),
+                DMA((nch, dp - 1)), DMA((nch, dp - 1)), DMA((nch, 4)), DMA((nch, 3)), DMA((nch,)),
+                DMA((3,)), DMA((3,)), DMA((3,)), DMA((dp * wid - 1,)), DMA((dp * wid - 1,)),
             ],
             compiler_params=pltpu.CompilerParams(
                 collective_id=0, has_side_effects=True, vmem_limit_bytes=cfg.get("limit", 63 << 20)
@@ -1038,7 +1092,7 @@
             in_specs=[ANY] * 4,
             out_specs=(ANY, ANY, VM, VM) + (ANY,) * 4 + (VM,) + (ANY,) * 4,
             scratch_shapes=[
-                vm((wid, RS, CT), BF), vm((RS, CT), F32), vm((16, CB), F32), DMA((9,)), DMA((9,)), DMA((3,)),
+                vm((3, RS, CT), BF), vm((RS, CT), F32), vm((16, CB), F32), DMA((9,)), DMA((9,)), DMA((3,)),
             ],
             compiler_params=pltpu.CompilerParams(vmem_limit_bytes=32 << 20),
             name="final",

time: 408 us -> 383 us (0.939)
  the two profiles are of different devices: /device:TPU:24 before, /device:TPU:0 now
where the time goes in v5:
time: 383 us; the launch traced here: 376 us
  Pallas kernels  364 us (95%)
  local copies, waits for them, and re-layouts  8.94 us (2%)
    pallas_call x1, Pallas kernels, shards(): pl.pallas_call(functools.partial(layer_kernel, cfg), out_shape=(sd((T, CB...  360 us

profile of v5, /device:TPU:0, one launch (start us, length us, event | category | flops | bytes accessed | tf_op | source)
XLA Modules:
  0.0 375.6 jit_solution(2456778370482266283)
XLA Ops:
  0.6 0.7 reduce
  1.3 0.7 reduce.1
  2.0 1.3 reshape.45.keep
  3.3 0.6 maximum_convert_fusion.gains
  3.9 0.8 copy.28
  4.8 0.6 pad.4.w_b
  5.4 359.8 %layer.1 = (bf16[768,384]{1,0:T(8,128)(2,1)}, bf16[768,384]{1,0:T(8,128)(2,1)}, f32[16,384]{1,0:T(8,128)}, bf16[1536,5120]{1,0:T(8,128)(2,1)}, bf16[1,768,5120]{...) custom-call(s32[2,3]{1,0:T(2,128)} %bitcast.13, ...), custom_call_target="tpu_custom_call" | custom-call | tf_op jit(solution)/shard_map/layer/pallas_call | solution.py:1054
  365.3 0.0 copy-start
  365.3 2.7 copy-done
  367.9 0.0 copy-start.1
  367.9 1.1 copy-done.1
  369.0 0.0 copy-start.2
  369.0 1.1 copy-done.2
  370.1 0.0 copy-start.3
  370.1 0.7 copy-done.3
  370.8 3.9 %final.1 = (bf16[768,384]{1,0:T(8,128)(2,1)}, bf16[768,384]{1,0:T(8,128)(2,1)}, f32[1,384]{1,0:T(1,128)}, f32[1,384]{1,0:T(1,128)}, f32[192,384]{1,0:T(8,128)}, ...) custom-call(bf16[3,192,5120]{2,1,0:T(8,128)(2,1)S(1)} %copy-done, ...), custom_call_target="tpu_custom_call" | custom-call | tf_op jit(solution)/shard_map/final/pallas_call | solution.py:1086
  374.7 0.7 copy.29
  (2 shorter events, 0.0 us)
Async XLA Ops:
  365.3 2.7 copy-start
  367.9 1.1 copy-start.1
  369.0 1.1 copy-start.2
  370.1 0.7 copy-start.3

commit v6 on v5

--- a/solution.py
+++ b/solution.py
@@ -484,7 +484,9 @@
         e0 = lens[m, 0]
         e1 = e0 + lens[m, 1]
         parts = [slice(a * BLK, (a + 1) * BLK) for a in range(3)]
-        keys = [keep[m, :, p] for p in parts]
+        keys = [keep[0:1, p] for p in parts]
+        for i in range(1, NB):
+            keys = [jnp.where(m == i, keep[i : i + 1, p], key) for p, key in zip(parts, keys)]
         out, res = fwd_unit(
             [qs[u, p, :] for p in parts], [ks[u, p, :] for p in parts], [vs[u, p, :] for p in parts],
             [hs[u, p, :] for p in parts], [xs[u, a] for a in range(3)], keys, e0, e1,
@@ -578,16 +580,15 @@
         advance(2)
         wait_third(0, hlow, m)
         norm(hlow, n2, 8, m * BUF)
-    advance(max([i + 1 for i, (n, _) in enumerate(events) if n < 6 + 2 * FL // FW], default=0))
     for copy in hid[2]:
         copy.wait()
 
     NT = 256
     ND = 2 * FL // FW
-    for i in range(ND):
-        late(i).finish()
-
-    def ffn(m):
+
+    PER = FL // FW
+
+    def ffn(m, part):
         def body(n, carry):
             at = pl.multiple_of(n * NT, NT)
             gate = nn(n2[rows_of(m), :], W[:, pl.ds(pl.multiple_of(GC + at, BLK), NT)])
@@ -600,7 +601,7 @@
             ug[rows_of(m), cols] = silu.astype(BF)
             return carry
 
-        lax.fori_loop(0, FL // NT, body, 0)
+        lax.fori_loop(part * (FW // NT), (part + 1) * (FW // NT), body, 0)
 
     def ffn_back(m):
         def body(n, carry):
@@ -659,10 +660,14 @@
         for n in range(FL // FW):
             weight_term(6 + (col - FB) // FW + n, left, right, n * FW, col + n * FW, FW)
 
-    for m in range(NB):
-        ffn(m)
-    ffn_terms(cotf, act, DC)
-    flush()
+    for part in range(PER):
+        advance(max([i + 1 for i, (n, _) in enumerate(events) if n <= 6 + PER + part], default=0))
+        late(part).finish()
+        late(PER + part).finish()
+        for m in range(NB):
+            ffn(m, part)
+        weight_term(6 + 2 * PER + part, cotf, act, part * FW, DC + part * FW, FW)
+        flush()
     advance(len(events))
     for i in range(ND, NF):
         late(i).finish()
@@ -806,7 +811,8 @@
 
     places_of = [(3 * HD, HD), (BC, BLK), (0, HD), (HD, HD), (2 * HD, HD), (OC, HD)]
     order = [(6 + (i + ND) % NF, FB + (i + ND) % NF * FW, FW) for i in range(NF)]
-    order += [(k, *places_of[k]) for k in (5, 2, 3, 4, 0, 1)]
+    order += [(k, *places_of[k]) for k in (5, 2, 3, 4)]
+    order += [(0, 3 * HD, HD - BLK), (6 + NF, 4 * HD - BLK, BLK), (1, BC, BLK)]
     taken = [0]
 
     def take():
@@ -907,7 +913,8 @@
     take()
     for a in range(3):
         weight_term(2 + a, n1, dA, a * HD, a * HD, HD)
-    weight_term(0, n1, dA, 3 * HD, 3 * HD, HD)
+    weight_term(0, n1, dA, 3 * HD, 3 * HD, HD - BLK)
+    weight_term(6 + NF, n1, dA, 4 * HD - BLK, 4 * HD - BLK, BLK)
     weight_term(1, n1, dB, 0, BC, BLK)
     flush()
 
@@ -1071,7 +1078,7 @@
                 DMA((3,)), DMA((9,)), DMA((3, 3)), DMA((3, 3)), *[DMA((nch + len(cfg["across"]) * (dp - 1), 2, wid))] * 2,
                 DMA((nch, wid, dp - 1)), DMA((nch, wid, dp - 1)),
                 *[DMA((4, NB, 2))] * 4, *[DMA((2, NB, 2))] * 2, DMA((2,)), DMA((2, 4)),
-                DMA((nch, dp - 1)), DMA((nch, dp - 1)), DMA((nch, 4)), DMA((nch, 3)), DMA((nch,)),
+                DMA((nch + 1, dp - 1)), DMA((nch + 1, dp - 1)), DMA((nch + 1, 4)), DMA((nch + 1, 3)), DMA((nch + 1,)),
                 DMA((3,)), DMA((3,)), DMA((3,)), DMA((dp * wid - 1,)), DMA((dp * wid - 1,)),
             ],
             compiler_params=pltpu.CompilerParams(
@@ -1079,7 +1086,7 @@
             ),
             name="layer",
         )(
-            lengths.reshape(NB, lengths.shape[2]), keep.reshape(NB, 1, BUF), tokens.reshape(T, CB),
+            lengths.reshape(NB, lengths.shape[2]), keep.reshape(NB, BUF), tokens.reshape(T, CB),
             cotangent.reshape(T, CB), gains, w_query, w_key, w_value, w_house,
             jnp.pad(w_beta, ((0, 0), (0, BLK - heads))), w_out.T, w_gate, w_up, w_down.T,
         )

time: 383 us -> 378 us (0.987)
  Pallas kernels: 364 us -> 360 us
    pallas_call x1, Pallas kernels: 360 us -> 356 us  [shards(): pl.pallas_call(functools.partial(layer_kernel, cfg), out_shape=(sd((T, CB...]
where the time goes in v6:
time: 378 us; the launch traced here: 370 us
  Pallas kernels  360 us (95%)
  local copies, waits for them, and re-layouts  7.68 us (2%)
    pallas_call x1, Pallas kernels, shards(): pl.pallas_call(functools.partial(layer_kernel, cfg), out_shape=(sd((T, CB...  356 us

profile of v6, /device:TPU:0, one launch (start us, length us, event | category | flops | bytes accessed | tf_op | source)
XLA Modules:
  0.0 370.4 jit_solution(15008246067471320892)
XLA Ops:
  0.6 0.7 reduce
  1.3 0.7 reduce.1
  2.1 0.6 maximum_convert_fusion.gains
  2.7 0.8 copy.28
  3.5 0.6 pad.4.w_b
  4.1 355.9 %layer.1 = (bf16[768,384]{1,0:T(8,128)(2,1)}, bf16[768,384]{1,0:T(8,128)(2,1)}, f32[16,384]{1,0:T(8,128)}, bf16[1536,5120]{1,0:T(8,128)(2,1)}, bf16[1,768,5120]{...) custom-call(s32[2,3]{1,0:T(2,128)} %bitcast.13, ...), custom_call_target="tpu_custom_call" | custom-call | tf_op jit(solution)/shard_map/layer/pallas_call | solution.py:1061
  360.1 0.0 copy-start
  360.1 2.7 copy-done
  362.8 0.0 copy-start.1
  362.8 1.1 copy-done.1
  363.8 0.0 copy-start.2
  363.8 1.1 copy-done.2
  364.9 0.0 copy-start.3
  364.9 0.7 copy-done.3
  365.6 3.9 %final.1 = (bf16[768,384]{1,0:T(8,128)(2,1)}, bf16[768,384]{1,0:T(8,128)(2,1)}, f32[1,384]{1,0:T(1,128)}, f32[1,384]{1,0:T(1,128)}, f32[192,384]{1,0:T(8,128)}, ...) custom-call(bf16[3,192,5120]{2,1,0:T(8,128)(2,1)S(1)} %copy-done, ...), custom_call_target="tpu_custom_call" | custom-call | tf_op jit(solution)/shard_map/final/pallas_call | solution.py:1093
  369.5 0.7 copy.29
  (2 shorter events, 0.0 us)
Async XLA Ops:
  360.1 2.7 copy-start
  362.8 1.1 copy-start.1
  363.8 1.1 copy-start.2
  364.9 0.7 copy-start.3
